TPU v7x, 32 devices: a whole 2x2x4 slice. The times are simulated.
32 devices in a mesh: cells: 8 (over z, x), genes: 4 (over y, core).
Axes of the slice: x: 2, y: 2, z: 4, core: 2. Of those that a mesh axis runs over, the one named last changes fastest.
Arguments:
- counts: bfloat16 [8192, 13500], P('cells', 'genes'), may hold values from 0.0099487305 to 200
- library: int32 [8192], P('cells'), may hold values from 1000 to 20000
- cell_mask: int32 [8192], P('cells'), may hold values 0 or 1
- slide_len: int32 [3], replicated, may hold values from 1 to 4096, 8192 in all
- kl_step: int32 [1], replicated, may hold values from 0 to 1999
- noise: bfloat16 [8192, 512], P('cells'), may hold values from -5 to 5
- emb_weight: bfloat16 [1024, 13500], P(None, 'genes'), may hold values from -0.0546875 to 0.0546875
- ln_gain: float32 [1024], replicated, may hold values from 0.5 to 1.5
- ln_bias: float32 [1024], replicated, may hold values from -1.5 to 1.5
- lat_weight: bfloat16 [1024, 1024], replicated, may hold values from -0.1875 to 0.1875
- lat_bias: float32 [1024], replicated, may hold values from -2 to 2
- up_weight: bfloat16 [1024, 512], replicated, may hold values from -0.25 to 0.25
- dec_weight: bfloat16 [1024, 13500], P(None, 'genes'), may hold values from -0.1875 to 0.1875
- prior_mean: float32 [512, 16], replicated, may hold values from -4 to 4
- prior_logvar: float32 [512, 16], replicated, may hold values from -1 to 1
- out_grad: bfloat16 [8192, 13500], P('cells', 'genes'), may hold values from -6 to 6
Outputs:
- decoded: bfloat16 [8192, 13500], P('cells', 'genes')
- counts_grad: bfloat16 [8192, 13500], P('cells', 'genes')
- emb_weight_grad: float32 [1024, 13500], P('cells', 'genes')
- ln_gain_grad: float32 [1024], P('cells')
- ln_bias_grad: float32 [1024], P('cells')
- lat_weight_grad: float32 [1024, 1024], P('cells')
- lat_bias_grad: float32 [1024], P('cells')
- up_weight_grad: float32 [1024, 512], P('cells')
- dec_weight_grad: float32 [1024, 13500], P('cells', 'genes')
- prior_mean_grad: float32 [512, 16], P('cells')
- prior_logvar_grad: float32 [512, 16], P('cells')
- kl_loss: float32 [1], replicated
Inputs may be any that keep to these rules, and one draw needn't show every extreme that they name: `slide_len`: slide lengths sum to 8192.
All inputs are finite; a program needn't handle non-finite values. No bound on the sum of `cell_mask` on one device may be relied on, other than what follows from the above.
Results may differ from a plain program's by a relative error of at most 0.009.
Values may be sent and summed in bfloat16 or wider, within the bound.
A program may use at most 192 MiB of HBM per device.

v0:
```python
import jax
import jax.numpy as jnp
from jax import lax
from jax.sharding import PartitionSpec as P

WARM = 1000


epsilon = 1e-05
free_bits = 1.0


def exact_dot(left, right):
    return jnp.dot(left, right, precision=lax.Precision.HIGHEST, preferred_element_type=jnp.float32)


def exact_tdot(left, right):
    return lax.dot_general(
        left,
        right,
        (((0,), (0,)), ((), ())),
        precision=lax.Precision.HIGHEST,
        preferred_element_type=jnp.float32,
    )


def half_dot(left, right):
    return jnp.dot(left, right, preferred_element_type=jnp.float32)


def half_tdot(left, right):
    return lax.dot_general(
        left, right, (((0,), (0,)), ((), ())), preferred_element_type=jnp.float32
    )


def half_ntdot(left, right):
    return lax.dot_general(
        left, right, (((1,), (1,)), ((), ())), preferred_element_type=jnp.float32
    )


def bottleneck_forward(
    embedded, noise_rows, ln_gain, ln_bias, lat_weight, lat_bias, up_weight, tables
):
    prec_tab, mean_prec, const_tab = tables
    latent_w = up_weight.shape[1]
    centred = embedded - jnp.mean(embedded, -1, keepdims=True)
    inv_dev = lax.rsqrt(jnp.mean(centred * centred, -1, keepdims=True) + epsilon)
    normal = centred * inv_dev
    hidden = normal * ln_gain + ln_bias
    hidden_low = hidden.astype(jnp.bfloat16)
    latent = half_dot(hidden_low, lat_weight) + lat_bias
    lat_mean = latent[:, :latent_w]
    log_var = latent[:, latent_w:]
    variance = jnp.exp(log_var)
    spread = jnp.exp(0.5 * log_var)
    sample_low = (lat_mean + spread * noise_rows.astype(jnp.float32)).astype(jnp.bfloat16)
    mixed_low = (hidden + half_ntdot(sample_low, up_weight)).astype(jnp.bfloat16)
    logits = -0.5 * (
        exact_dot(lat_mean * lat_mean, prec_tab)
        - 2.0 * exact_dot(lat_mean, mean_prec)
        + jnp.sum(const_tab, 0)
    )
    resp = jax.nn.softmax(logits * latent_w ** (-0.5), axis=-1)
    resp_prec = exact_dot(resp, prec_tab.T)
    resp_mean = exact_dot(resp, mean_prec.T)
    diverge = 0.5 * (
        exact_dot(resp, const_tab.T)
        - log_var
        + (variance + lat_mean * lat_mean) * resp_prec
        - 2.0 * lat_mean * resp_mean
        - 1.0
    )
    kept = (
        normal,
        inv_dev,
        hidden_low,
        lat_mean,
        log_var,
        variance,
        spread,
        sample_low,
        resp,
        resp_prec,
        resp_mean,
    )
    return (mixed_low, diverge, kept)


def bottleneck_backward(
    mixed_grad, weight, noise_rows, kept, ln_gain, lat_weight, up_weight, prior_mean, tables
):
    prec_tab, mean_prec, const_tab = tables
    (
        normal,
        inv_dev,
        hidden_low,
        lat_mean,
        log_var,
        variance,
        spread,
        sample_low,
        resp,
        resp_prec,
        resp_mean,
    ) = kept
    latent_w = up_weight.shape[1]
    up_grad = half_tdot(mixed_grad, sample_low)
    sample_grad = half_dot(mixed_grad, up_weight)
    mean_grad = sample_grad + weight * (lat_mean * resp_prec - resp_mean)
    var_grad = sample_grad * 0.5 * spread * noise_rows.astype(jnp.float32) + 0.5 * weight * (
        variance * resp_prec - 1.0
    )
    moment = variance + lat_mean * lat_mean
    resp_grad = 0.5 * (
        exact_dot(weight, const_tab)
        + exact_dot(weight * moment, prec_tab)
        - 2.0 * exact_dot(weight * lat_mean, mean_prec)
    )
    logit_grad = (
        resp * (resp_grad - jnp.sum(resp * resp_grad, -1, keepdims=True)) * latent_w ** (-0.5)
    )
    mean_grad = (
        mean_grad
        - lat_mean * exact_dot(logit_grad, prec_tab.T)
        + exact_dot(logit_grad, mean_prec.T)
    )
    const_grad = 0.5 * exact_tdot(weight, resp) - 0.5 * jnp.sum(logit_grad, 0)[None, :]
    mprec_grad = -exact_tdot(weight * lat_mean, resp) + exact_tdot(lat_mean, logit_grad)
    prec_grad = (
        0.5 * exact_tdot(weight * moment, resp)
        - 0.5 * exact_tdot(lat_mean * lat_mean, logit_grad)
        + prior_mean * prior_mean * const_grad
        + prior_mean * mprec_grad
    )
    pmean_grad = 2.0 * prior_mean * prec_tab * const_grad + prec_tab * mprec_grad
    plogv_grad = const_grad - prec_tab * prec_grad
    latent_grad = jnp.concatenate([mean_grad, var_grad], axis=1).astype(jnp.bfloat16)
    latb_grad = jnp.sum(latent_grad.astype(jnp.float32), 0)
    latw_grad = half_tdot(hidden_low, latent_grad)
    hidden_grad = mixed_grad.astype(jnp.float32) + half_ntdot(latent_grad, lat_weight)
    gain_grad = jnp.sum(hidden_grad * normal, 0)
    shift_grad = jnp.sum(hidden_grad, 0)
    normal_grad = hidden_grad * ln_gain
    embed_grad = inv_dev * (
        normal_grad
        - jnp.mean(normal_grad, -1, keepdims=True)
        - normal * jnp.mean(normal_grad * normal, -1, keepdims=True)
    )
    small = (latw_grad, up_grad, gain_grad, shift_grad, latb_grad, pmean_grad, plogv_grad)
    return (embed_grad.astype(jnp.bfloat16), small)


def on_device(
    counts,
    library,
    cell_mask,
    slide_len,
    kl_step,
    noise,
    emb_weight,
    ln_gain,
    ln_bias,
    lat_weight,
    lat_bias,
    up_weight,
    dec_weight,
    prior_mean,
    prior_logvar,
    out_grad,
):
    rows = counts.shape[0]
    first = lax.axis_index("cells") * rows
    place = first + jnp.arange(rows, dtype=jnp.int32)
    ends = jnp.cumsum(slide_len)
    slide_of = jnp.sum((ends[None, :] <= place[:, None]).astype(jnp.int32), 1)
    onehot = (slide_of[:, None] == jnp.arange(slide_len.shape[0], dtype=jnp.int32)[None, :]).astype(
        jnp.float32
    )
    live = cell_mask.astype(jnp.float32)
    libsize = library.astype(jnp.float32)
    lib_total, live_total = lax.psum(
        (jnp.sum(onehot * (libsize * live)[:, None], 0), jnp.sum(onehot * live[:, None], 0)),
        "cells",
    )
    slide_lib = lib_total / jnp.maximum(live_total, 1.0)
    scale = jnp.sum(onehot * slide_lib[None, :], 1) / libsize
    total = jnp.maximum(jnp.sum(live_total), 1.0)
    beta = jnp.minimum(1.0, kl_step[0].astype(jnp.float32) / WARM)
    prec_tab = jnp.exp(-prior_logvar)
    tables = (prec_tab, prior_mean * prec_tab, prior_mean * prior_mean * prec_tab + prior_logvar)
    counts_f = counts.astype(jnp.float32)
    normed_low = jnp.log1p(counts_f * scale[:, None]).astype(jnp.bfloat16)
    partial_embed = half_ntdot(normed_low, emb_weight)
    embedded = lax.psum(partial_embed, "genes")
    mixed_low, diverge, kept = bottleneck_forward(
        embedded, noise, ln_gain, ln_bias, lat_weight, lat_bias, up_weight, tables
    )
    kl_sum = lax.psum(jnp.sum(diverge * live[:, None], 0), "cells")
    decoded = half_dot(mixed_low, dec_weight).astype(jnp.bfloat16)
    average = kl_sum / total
    kl_loss = beta * jnp.sum(jnp.maximum(average, free_bits))
    active = (average > free_bits).astype(jnp.float32)
    partial_mixed = half_ntdot(out_grad, dec_weight)
    dec_grad = half_tdot(mixed_low, out_grad)
    weight_rows = beta * active[None, :] * live[:, None] / total
    mixed_grad = lax.psum(partial_mixed, "genes").astype(jnp.bfloat16)
    embed_grad, small = bottleneck_backward(
        mixed_grad, weight_rows, noise, kept, ln_gain, lat_weight, up_weight, prior_mean, tables
    )
    normed_grad = half_dot(embed_grad, emb_weight)
    counts_grad = (normed_grad * scale[:, None] / (1.0 + counts_f * scale[:, None])).astype(
        jnp.bfloat16
    )
    latw_grad, up_grad, gain_grad, shift_grad, latb_grad, pmean_grad, plogv_grad = small
    emb_grad = half_tdot(embed_grad, normed_low)
    summed = (
        lax.psum_scatter(emb_grad, "cells", scatter_dimension=0, tiled=True),
        lax.psum_scatter(dec_grad, "cells", scatter_dimension=0, tiled=True),
        lax.psum_scatter(latw_grad, "cells", scatter_dimension=0, tiled=True),
        lax.psum_scatter(up_grad, "cells", scatter_dimension=0, tiled=True),
        lax.psum_scatter(gain_grad, "cells", scatter_dimension=0, tiled=True),
        lax.psum_scatter(shift_grad, "cells", scatter_dimension=0, tiled=True),
        lax.psum_scatter(latb_grad, "cells", scatter_dimension=0, tiled=True),
        lax.psum_scatter(pmean_grad, "cells", scatter_dimension=0, tiled=True),
        lax.psum_scatter(plogv_grad, "cells", scatter_dimension=0, tiled=True),
    )
    emb_out, dec_out, latw_out, up_out, gain_out, shift_out, latb_out, pmean_out, plogv_out = summed
    return (
        decoded,
        counts_grad,
        emb_out,
        gain_out,
        shift_out,
        latw_out,
        latb_out,
        up_out,
        dec_out,
        pmean_out,
        plogv_out,
        kl_loss.reshape(1),
    )


def solution(mesh):
    placed = (
        P("cells", "genes"),
        P("cells"),
        P("cells"),
        P(),
        P(),
        P("cells", None),
        P(None, "genes"),
        P(),
        P(),
        P(),
        P(),
        P(),
        P(None, "genes"),
        P(),
        P(),
        P("cells", "genes"),
    )
    return jax.shard_map(
        on_device,
        mesh=mesh,
        in_specs=placed,
        out_specs=(
            P("cells", "genes"),
            P("cells", "genes"),
            P("cells", "genes"),
            P("cells"),
            P("cells"),
            P("cells", None),
            P("cells"),
            P("cells", None),
            P("cells", "genes"),
            P("cells", None),
            P("cells", None),
            P(),
        ),
        check_vma=False,
    )
```

profile of v0, /device:TPU:0, one launch (start us, length us, event | category | flops | bytes accessed | tf_op | source)
XLA Modules:
  0.0 957.3 jit_solution(9360086987290301371)
XLA Ops:
  9.8 23.1 %all-reduce.4 = (f32[3]{0:T(128)S(1)}, f32[3]{0:T(128)S(1)}) all-reduce(f32[3]{0:T(128)S(1)} %get-tuple-element.17, f32[3]{0:T(128)S(1)} %get-tuple-element.16), channel_id=1, replica_groups=mesh['cells'=8,'genes'=4] {'cells'}, use_global_device_ids=true, to_apply=%region_3.4 | all-reduce | flops 6 | bytes 48 | tf_op jit(solution)/shard_map/psum | solution.py:183
  34.4 14.0 %fusion.1 = f32[1024,1024]{1,0:T(8,128)} fusion(bf16[1024,3375]{0,1:T(8,128)(2,1)} %param.22, bf16[1024,3375]{0,1:T(8,128)(2,1)} %param.16, f32[1024]{0:T(1024)S(1)} %convert_divide_fusion), kind=kOutput, calls=%fused_computation.5 | convolution fusion | flops 7088256000 | bytes 18022400 | tf_op jit(solution)/shard_map/dot_general | solution.py:38
  49.1 14.3 %fusion.64 = f32[1024,1024]{1,0:T(8,128)} fusion(bf16[1024,3375]{0,1:T(8,128)(2,1)} %param.31, bf16[1024,3375]{0,1:T(8,128)(2,1)} %param.28), kind=kOutput, calls=%fused_computation.101 | convolution fusion | flops 7077888000 | bytes 18018304 | tf_op jit(solution)/shard_map/dot_general | solution.py:38
  64.3 67.0 %all-reduce.8.cloned.1.call-done = f32[1024,1024]{1,0:T(8,128)} async-done(((f32[1024,1024]{1,0:T(8,128)}), f32[1024,1024]{1,0:T(8,128)}) %all-reduce.8.cloned.1.call-update) | async-done | bytes 4194320 | tf_op jit(solution)/shard_map/psum | solution.py:196
  131.3 2.4 reduce_sum.166
  133.8 2.9 multiply_reduce_fusion.2
  137.2 2.5 broadcast_add_fusion
  139.7 1.9 convolution_multiply_fusion.1
  141.6 2.0 fusion.63
  143.6 1.8 fusion.55
  145.4 1.9 fusion.41
  148.6 2.7 multiply_reduce_fusion.4
  151.4 21.8 %psum.39 = f32[512]{0:T(512)S(1)} all-reduce(f32[512]{0:T(512)S(1)} %multiply_reduce_fusion.4), channel_id=1, replica_groups=mesh['cells'=8,'genes'=4] {'cells'}, use_global_device_ids=true, to_apply=%region_15.16 | all-reduce | flops 512 | bytes 4096 | tf_op jit(solution)/shard_map/psum | solution.py:200
  173.7 2.0 fusion.36
  177.3 2.3 convolution_add_fusion
  179.6 2.2 multiply_reduce_fusion.5
  188.5 76.6 %all-reduce.9 = bf16[1024,1024]{1,0:T(8,128)(2,1)} all-reduce(f32[1024,1024]{1,0:T(8,128)} %fusion.64), channel_id=1, replica_groups=mesh['cells'=8,'genes'=4] {'genes'}, use_global_device_ids=true, to_apply=%region_10.11 | all-reduce | flops 1048576 | bytes 6291456 | tf_op jit(solution)/shard_map/psum | solution.py:208
  266.0 7.7 fusion.6
  274.7 2.7 fusion.66
  277.5 1.8 fusion.40
  279.3 6.0 add_convert_fusion.1
  286.4 4.5 fusion.37
  291.2 8.4 multiply_reduce_fusion
  299.5 19.0 %fusion = f32[1024,3375]{0,1:T(8,128)} fusion(bf16[1024,3375]{0,1:T(8,128)(2,1)} %param.16, f32[1024]{0:T(1024)S(1)} %convert_divide_fusion, f32[1024,1024]{1,0:T(8,128)} %get-tuple-element.40, f32[1024,1024]{1,0:T(8,128)S(1)} %copy-done.4, f32[1024]{0:T(1024)S(1)} %get-tuple-element.43, f32[1024]{0:T(1024)S(1)} %get-tuple-element.44, ...), kind=kOutput, calls=%fused_computation.4 | convolution fusion | flops 7096644608 | bytes 29149184 | tf_op jit(solution)/shard_map/dot_general | solution.py:32
  320.1 3.6 add_convert_fusion
  325.0 13.4 %fusion.65 = f32[1024,3375]{0,1:T(8,128)} fusion(bf16[1024,1024]{1,0:T(8,128)(2,1)S(1)} %add_convert_fusion, bf16[1024,3375]{0,1:T(8,128)(2,1)} %param.31), kind=kOutput, calls=%fused_computation.102 | convolution fusion | flops 7077888000 | bytes 22833152 | tf_op jit(solution)/shard_map/dot_general | solution.py:32
  340.7 33.7 %all-reduce.3 = (f32[1024]{0:T(1024)S(1)}, f32[1024]{0:T(1024)S(1)}, f32[1024]{0:T(1024)S(1)}) all-reduce(f32[1024]{0:T(1024)S(1)} %get-tuple-element.12, f32[1024]{0:T(1024)S(1)} %get-tuple-element.15, f32[1024]{0:T(1024)S(1)} %convert_reduce_fusion), channel_id=3, replica_groups=mesh['cells'=8,'genes'=4] {'cells'}, use_global_device_ids=true, to_apply=%region_22.23.clone | all-reduce | flops 3072 | bytes 24576
  376.8 12.2 %convolution_convert_fusion = bf16[1024,3375]{0,1:T(8,128)(2,1)} fusion(bf16[1024,1024]{1,0:T(8,128)(2,1)} %copy-done.22, bf16[1024,3375]{0,1:T(8,128)(2,1)} %param.28), kind=kOutput, calls=%fused_computation.3 | convolution fusion | flops 7081344000 | bytes 15921152 | tf_op jit(solution)/shard_map/dot_general | solution.py:28
  389.0 16.2 %divide_convert_fusion = bf16[1024,3375]{0,1:T(8,128)(2,1)} fusion(bf16[1024,3375]{0,1:T(8,128)(2,1)} %param.16, bf16[1024,3375]{0,1:T(8,128)(2,1)} %param.22, f32[1024]{0:T(1024)S(1)} %convert_divide_fusion, f32[1024,1024]{1,0:T(8,128)S(1)} %copy-done.23, f32[1024,1024]{1,0:T(8,128)S(1)} %copy-done.5, f32[1024]{0:T(1024)S(1)} %get-tuple-element.43, ...), kind=kOutput, calls=%fused_computation | convolution fusion | flops 7107012608 | bytes 29149184 | tf_op jit(solution)/shard_map/dot_general | solution.py:28
  408.0 79.9 %reduce-scatter.13.cloned.1.call-done = f32[128,1024]{1,0:T(8,128)} async-done(((f32[1024,1024]{1,0:T(8,128)}), f32[128,1024]{1,0:T(8,128)}) %reduce-scatter.13.cloned.1.call-update) | async-done | bytes 524304 | tf_op jit(solution)/shard_map/reduce_scatter | solution.py:221
  487.9 230.7 %reduce-scatter.11.cloned.1.call-done = f32[128,3375]{0,1:T(8,128)} async-done(((f32[1024,3375]{0,1:T(8,128)}), f32[128,3375]{0,1:T(8,128)}) %reduce-scatter.11.cloned.1.call-update) | async-done | bytes 1728016 | tf_op jit(solution)/shard_map/reduce_scatter | solution.py:219
  718.6 230.2 %reduce-scatter.17.cloned.1.call-done = f32[128,3375]{0,1:T(8,128)} async-done(((f32[1024,3375]{0,1:T(8,128)}), f32[128,3375]{0,1:T(8,128)}) %reduce-scatter.17.cloned.1.call-update) | async-done | bytes 1728016 | tf_op jit(solution)/shard_map/reduce_scatter | solution.py:220
  (96 shorter events, 27.0 us)
Async XLA Ops:
  7.2 129.5 %copy-start = (bf16[1024,1024]{1,0:T(8,128)(2,1)S(1)}, bf16[1024,1024]{1,0:T(8,128)(2,1)}, u32[]{:S(2)}) copy-start(bf16[1024,1024]{1,0:T(8,128)(2,1)} %param.25) | copy-start | bytes 6291460
  7.2 124.1 %all-reduce.8.cloned.1.call-start = ((), (), s32[]{:S(2)}) async-start(), calls=%async_computation.6 | async-start | bytes 8388608 | tf_op jit(solution)/shard_map/psum | solution.py:196
  48.4 356.8 %reduce-scatter.21.cloned.1.call-start = ((), (), s32[]{:S(2)}) async-start(), calls=%async_computation.12 | async-start | bytes 294912
  49.1 15.0 %copy-start.13 = (f32[512,16]{0,1:T(8,128)S(1)}, f32[512,16]{0,1:T(8,128)}, u32[]{:S(2)}) copy-start(f32[512,16]{0,1:T(8,128)} %param.30) | copy-start | bytes 98308
  49.1 15.0 %copy-start.14 = (f32[512,16]{0,1:T(8,128)S(1)}, f32[512,16]{0,1:T(8,128)}, u32[]{:S(2)}) copy-start(f32[512,16]{0,1:T(8,128)} %param.29) | copy-start | bytes 98308
  64.3 72.5 %copy-start.16 = (f32[1024]{0:T(1024)S(1)}, f32[1024]{0:T(1024)}, u32[]{:S(2)}) copy-start(f32[1024]{0:T(1024)} %param.26) | copy-start | bytes 12292
  64.3 72.5 %copy-start.17 = (f32[1024]{0:T(1024)S(1)}, f32[1024]{0:T(1024)}, u32[]{:S(2)}) copy-start(f32[1024]{0:T(1024)} %param.24) | copy-start | bytes 12292
  64.3 72.5 %copy-start.18 = (f32[1024]{0:T(1024)S(1)}, f32[1024]{0:T(1024)}, u32[]{:S(2)}) copy-start(f32[1024]{0:T(1024)} %param.23) | copy-start | bytes 12292
  133.8 3.5 copy-start.2
  139.7 7.6 copy-start.6
  145.4 1.9 copy-start.9
  147.3 1.3 copy-start.10
  173.1 2.7 copy-start.7
  188.4 218.2 %reduce-scatter.19.cloned.1.call-start = ((), (), s32[]{:S(2)}) async-start(), calls=%async_computation.11 | async-start | bytes 294912
  265.9 142.1 %reduce-scatter.15.cloned.1.call-start = ((), (), s32[]{:S(2)}) async-start(), calls=%async_computation.9 | async-start | bytes 2359296 | tf_op jit(solution)/shard_map/reduce_scatter | solution.py:222
  266.0 8.7 copy-start.8
  273.7 1.0 copy-start.20
  277.4 210.5 %reduce-scatter.13.cloned.1.call-start = ((), (), s32[]{:S(2)}) async-start(), calls=%async_computation.8 | async-start | bytes 4718592 | tf_op jit(solution)/shard_map/reduce_scatter | solution.py:221
  279.3 7.0 copy-start.3
  285.4 1.0 copy-start.11
  290.9 427.7 %reduce-scatter.11.cloned.1.call-start = ((), (), s32[]{:S(2)}) async-start(), calls=%async_computation.7 | async-start | bytes 15556608 | tf_op jit(solution)/shard_map/reduce_scatter | solution.py:219
  291.2 8.4 copy-start.4
  318.5 1.2 copy-start.15
  318.5 1.5 copy-start.21
  318.6 630.3 %reduce-scatter.17.cloned.1.call-start = ((), (), s32[]{:S(2)}) async-start(), calls=%async_computation.10 | async-start | bytes 15556608 | tf_op jit(solution)/shard_map/reduce_scatter | solution.py:220
  323.7 1.3 copy-start.22
  338.4 0.7 copy-start.19
  338.4 1.9 copy-start.12
  376.8 12.2 %copy-start.5 = (f32[1024,1024]{1,0:T(8,128)S(1)}, f32[1024,1024]{1,0:T(8,128)}, u32[]{:S(2)}) copy-start(f32[1024,1024]{1,0:T(8,128)} %all-reduce.8.cloned.1.call-done) | copy-start | bytes 12582916
  376.8 12.2 %copy-start.23 = (f32[1024,1024]{1,0:T(8,128)S(1)}, f32[1024,1024]{1,0:T(8,128)}, u32[]{:S(2)}) copy-start(f32[1024,1024]{1,0:T(8,128)} %get-tuple-element.40) | copy-start | bytes 12582916
  389.0 559.8 %copy-start.1 = (bf16[1024,1024]{1,0:T(8,128)(2,1)S(1)}, bf16[1024,1024]{1,0:T(8,128)(2,1)}, u32[]{:S(2)}) copy-start(bf16[1024,1024]{1,0:T(8,128)(2,1)} %param.25) | copy-start | bytes 6291460
Sparse Core Ops, SparseCore 0:
  48.5 82.7 all-reduce.7
  188.5 58.4 reduce-scatter.20
  266.1 58.3 reduce-scatter.18
  328.4 68.1 reduce-scatter.14
  400.6 87.2 reduce-scatter.12
  491.9 226.6 reduce-scatter.10
  722.7 226.0 reduce-scatter.16
where the time goes:
time: 963 us; the launch traced here: 957 us
  waiting for transfers between devices  608 us (63%)
  blocking collectives  155 us (16%)
  matrix products  150 us (16%)
  between operations  18.7 us (2%)
  local copies, waits for them, and re-layouts  13.8 us (1%)
  other arithmetic  10.6 us (1%)
    reduce_scatter x1, waiting for transfers between devices, on_device(): lax.psum_scatter(emb_grad, 'cells', scatter_dimension=0, tiled=True)  231 us
    reduce_scatter x1, waiting for transfers between devices, on_device(): lax.psum_scatter(dec_grad, 'cells', scatter_dimension=0, tiled=True)  230 us
    reduce_scatter x1, waiting for transfers between devices, on_device(): lax.psum_scatter(latw_grad, 'cells', scatter_dimension=0, tiled=True)  79.9 us
    psum x1, blocking collectives, on_device(): mixed_grad = lax.psum(partial_mixed, 'genes').astype(jnp.bfloat16)  76.6 us
    psum x1, waiting for transfers between devices, on_device(): embedded = lax.psum(partial_embed, 'genes')  67 us
    dot_general x4, matrix products, half_ntdot(): lax.dot_general(left, right, (((1,), (1,)), ((), ())), preferred_element_...  40.3 us
    dot_general x4, matrix products, half_tdot(): lax.dot_general(left, right, (((0,), (0,)), ((), ())), preferred_element_...  39.6 us
    dot_general x4, matrix products, half_dot(): return jnp.dot(left, right, preferred_element_type=jnp.float32)  38.5 us
  transfers between devices with their start and end apart: 7, of which 4 were waited for; matrix products, arithmetic and copies ran while one was open for 12% of the time, Pallas kernels for 0%

commit v1 on v0

v1 whole, which is shorter than its diff:
```python
import jax
import jax.numpy as jnp
from jax import lax
from jax.sharding import PartitionSpec as P

WARM = 1000
EPS = 1e-05
FREE = 1.0
BF = jnp.bfloat16
F32 = jnp.float32


def edot(left, right, dims=((1,), (0,))):
    return lax.dot_general(
        left, right, (dims, ((), ())), precision=lax.Precision.HIGHEST, preferred_element_type=F32
    )


def hdot(left, right, dims=((1,), (0,))):
    return lax.dot_general(left, right, (dims, ((), ())), preferred_element_type=F32)


def bits_of(n):
    return n.bit_length() - 1


def flip(x, axis, size, mask):
    return lax.ppermute(x, axis, [(i, i ^ mask) for i in range(size)])


def butterfly(x, axis, size):
    for k in range(bits_of(size)):
        x = x + flip(x, axis, size, 1 << k)
    return x


def scatter_rows(x, axis, size, at):
    for k in range(bits_of(size)):
        bit = (at >> k) & 1
        halves = x.reshape((2, x.shape[0] // 2) + x.shape[1:])
        keep = lax.dynamic_index_in_dim(halves, bit, 0, keepdims=False)
        send = lax.dynamic_index_in_dim(halves, 1 - bit, 0, keepdims=False)
        x = keep.astype(F32) + flip(send.astype(BF), axis, size, 1 << k).astype(F32)
    return x


def gather_rows(x, axis, size, at):
    for k in reversed(range(bits_of(size))):
        bit = (at >> k) & 1
        other = flip(x, axis, size, 1 << k)
        first = jnp.where(bit == 0, x, other)
        second = jnp.where(bit == 0, other, x)
        x = jnp.concatenate([first, second], 0)
    return x


def place_of(at, size):
    block = 0
    for k in range(bits_of(size)):
        block = block * 2 + ((at >> k) & 1)
    return block


def halving(blocks, right, axis, size, order):
    live = list(range(size))
    arrived = {r: [] for r in live}
    for k in order:
        sent = [r for r in live if (r >> k) & 1]
        live = [r for r in live if not (r >> k) & 1]
        part = hdot(jnp.concatenate([blocks[r] for r in sent], 1), right, ((0,), (0,)))
        for got in range(len(arrived[sent[0]])):
            part = part + jnp.concatenate([arrived[r][got] for r in sent], 0).astype(F32)
        came = flip(part.astype(BF), axis, size, 1 << k)
        width = blocks[0].shape[1]
        for i, r in enumerate(sent):
            arrived[r ^ (1 << k)].append(came[i * width : (i + 1) * width])
    total = hdot(blocks[0], right, ((0,), (0,)))
    for part in arrived[0]:
        total = total + part.astype(F32)
    return total


def cut(width, parts):
    step = -(-width // (parts * 128)) * 128
    edges = list(range(0, width, step)) + [width]
    return list(zip(edges[:-1], edges[1:]))


def on_device(
    counts,
    library,
    cell_mask,
    slide_len,
    kl_step,
    noise,
    emb_weight,
    ln_gain,
    ln_bias,
    lat_weight,
    lat_bias,
    up_weight,
    dec_weight,
    prior_mean,
    prior_logvar,
    out_grad,
    ncell,
    ngene,
):
    rows, width = counts.shape
    model = emb_weight.shape[0]
    latent_w = up_weight.shape[1]
    cell_at = lax.axis_index("cells")
    gene_at = lax.axis_index("genes")
    nslide = slide_len.shape[0]
    place = cell_at * rows + jnp.arange(rows, dtype=jnp.int32)
    ends = jnp.cumsum(slide_len)
    slide_of = jnp.sum((ends[None, :] <= place[:, None]).astype(jnp.int32), 1)
    onehot = (slide_of[:, None] == jnp.arange(nslide, dtype=jnp.int32)[None, :]).astype(F32)
    live = cell_mask.astype(F32)
    libsize = library.astype(F32)
    stats = jnp.concatenate(
        [jnp.sum(onehot * (libsize * live)[:, None], 0), jnp.sum(onehot * live[:, None], 0)]
    )
    stats = butterfly(stats, "cells", ncell)
    lib_total, live_total = stats[:nslide], stats[nslide:]
    slide_lib = lib_total / jnp.maximum(live_total, 1.0)
    scale = jnp.sum(onehot * slide_lib[None, :], 1) / libsize
    total = jnp.maximum(jnp.sum(live_total), 1.0)
    beta = jnp.minimum(1.0, kl_step[0].astype(F32) / WARM)

    partial_mixed = hdot(out_grad, dec_weight, ((1,), (1,))).astype(BF)
    mixed_grad = scatter_rows(partial_mixed, "genes", ngene, gene_at).astype(BF)

    counts_f = counts.astype(F32)
    normed = jnp.log(1.0 + counts_f * scale[:, None]).astype(BF)
    partial_embed = hdot(normed, emb_weight, ((1,), (1,))).astype(BF)
    embedded = scatter_rows(partial_embed, "genes", ngene, gene_at)

    mine = rows // ngene
    first = place_of(gene_at, ngene) * mine
    my_noise = lax.dynamic_slice_in_dim(noise, first, mine, 0).astype(F32)
    my_live = lax.dynamic_slice_in_dim(live, first, mine, 0)
    prec = jnp.exp(-prior_logvar)
    mprec = prior_mean * prec
    ctab = prior_mean * mprec + prior_logvar

    centred = embedded - jnp.mean(embedded, -1, keepdims=True)
    inv_dev = lax.rsqrt(jnp.mean(centred * centred, -1, keepdims=True) + EPS)
    normal = centred * inv_dev
    hidden = normal * ln_gain + ln_bias
    hidden_low = hidden.astype(BF)
    latent = hdot(hidden_low, lat_weight) + lat_bias
    lat_mean = latent[:, :latent_w]
    log_var = latent[:, latent_w:]
    variance = jnp.exp(log_var)
    spread = jnp.exp(0.5 * log_var)
    sample_low = (lat_mean + spread * my_noise).astype(BF)
    mixed_mine = (hidden + hdot(sample_low, up_weight, ((1,), (1,)))).astype(BF)
    mixed = gather_rows(mixed_mine, "genes", ngene, gene_at)

    step = model // ncell

    def blocks_of(x):
        return [
            lax.dynamic_slice_in_dim(x, (cell_at ^ r) * step, step, 1) for r in range(ncell)
        ]

    nbits = bits_of(ncell)
    straight = list(range(nbits))
    turned = [1, 0] + straight[2:] if nbits > 1 else straight
    pieces = cut(width, 4)

    def weight_sum(x, right):
        blocks = blocks_of(x)
        outs = []
        for i, (lo, hi) in enumerate(pieces):
            order = turned if i == 0 else straight
            outs.append(halving(blocks, right[:, lo:hi], "cells", ncell, order))
        return jnp.concatenate(outs, 1)

    dec_out = weight_sum(mixed, out_grad)
    decoded = hdot(mixed, dec_weight).astype(BF)

    moment = variance + lat_mean * lat_mean
    square = lat_mean * lat_mean
    logits = -0.5 * (
        edot(
            jnp.concatenate([square, lat_mean], 1), jnp.concatenate([prec, -2.0 * mprec], 0)
        )
        + jnp.sum(ctab, 0)
    )
    resp = jax.nn.softmax(logits * latent_w ** (-0.5), axis=-1)
    spreads = edot(resp, jnp.concatenate([ctab, prec, mprec], 0), ((1,), (1,)))
    resp_ctab = spreads[:, :latent_w]
    resp_prec = spreads[:, latent_w : 2 * latent_w]
    resp_mean = spreads[:, 2 * latent_w :]
    diverge = 0.5 * (
        resp_ctab - log_var + moment * resp_prec - 2.0 * lat_mean * resp_mean - 1.0
    )
    kl_sum = jnp.sum(diverge * my_live[:, None], 0)
    kl_sum = butterfly(butterfly(kl_sum, "genes", ngene), "cells", ncell)
    average = kl_sum / total
    kl_loss = beta * jnp.sum(jnp.maximum(average, FREE))
    active = (average > FREE).astype(F32)
    weight = beta * active[None, :] * my_live[:, None] / total

    up_part = hdot(mixed_grad, sample_low, ((0,), (0,)))
    sample_grad = hdot(mixed_grad, up_weight)
    mean_grad = sample_grad + weight * (lat_mean * resp_prec - resp_mean)
    var_grad = sample_grad * 0.5 * spread * my_noise + 0.5 * weight * (variance * resp_prec - 1.0)
    w_moment = weight * moment
    w_mean = weight * lat_mean
    left3 = jnp.concatenate([weight, w_moment, w_mean], 1)
    resp_grad = 0.5 * edot(left3, jnp.concatenate([ctab, prec, -2.0 * mprec], 0))
    logit_grad = (
        resp * (resp_grad - jnp.sum(resp * resp_grad, -1, keepdims=True)) * latent_w ** (-0.5)
    )
    back = edot(logit_grad, jnp.concatenate([prec, mprec], 0), ((1,), (1,)))
    mean_grad = mean_grad - lat_mean * back[:, :latent_w] + back[:, latent_w:]
    by_resp = edot(left3, resp, ((0,), (0,)))
    by_logit = edot(jnp.concatenate([square, lat_mean], 1), logit_grad, ((0,), (0,)))
    const_grad = 0.5 * by_resp[:latent_w] - 0.5 * jnp.sum(logit_grad, 0)[None, :]
    mprec_grad = by_logit[latent_w:] - by_resp[2 * latent_w :]
    prec_grad = (
        0.5 * by_resp[latent_w : 2 * latent_w]
        - 0.5 * by_logit[:latent_w]
        + prior_mean * prior_mean * const_grad
        + prior_mean * mprec_grad
    )
    pmean_part = 2.0 * prior_mean * prec * const_grad + prec * mprec_grad
    plogv_part = const_grad - prec * prec_grad
    latent_grad = jnp.concatenate([mean_grad, var_grad], 1).astype(BF)
    latb_part = jnp.sum(latent_grad.astype(F32), 0)
    hidden_grad = mixed_grad.astype(F32) + hdot(latent_grad, lat_weight, ((1,), (1,)))
    gain_part = jnp.sum(hidden_grad * normal, 0)
    shift_part = jnp.sum(hidden_grad, 0)
    normal_grad = hidden_grad * ln_gain
    embed_mine = (
        inv_dev
        * (
            normal_grad
            - jnp.mean(normal_grad, -1, keepdims=True)
            - normal * jnp.mean(normal_grad * normal, -1, keepdims=True)
        )
    ).astype(BF)
    embed_grad = gather_rows(embed_mine, "genes", ngene, gene_at)

    emb_out = weight_sum(embed_grad, normed)
    normed_grad = hdot(embed_grad, emb_weight)
    counts_grad = (normed_grad * scale[:, None] / (1.0 + counts_f * scale[:, None])).astype(BF)

    latw_part = hdot(hidden_low, latent_grad, ((0,), (0,)))
    small = jnp.concatenate([latw_part, up_part], 1).astype(BF)
    cols = small.shape[1]
    small = small.reshape(model, ngene, cols // ngene).transpose(1, 0, 2)
    small = scatter_rows(small, "genes", ngene, gene_at)
    small = small.reshape(ncell, step, cols // ngene)
    keepers = [lax.dynamic_index_in_dim(small, cell_at ^ r, 0, keepdims=False) for r in range(ncell)]
    for k in straight:
        sent = [r for r in range(ncell) if keepers[r] is not None and (r >> k) & 1]
        came = flip(jnp.stack([keepers[r] for r in sent]).astype(BF), "cells", ncell, 1 << k)
        for i, r in enumerate(sent):
            keepers[r] = None
            keepers[r ^ (1 << k)] = keepers[r ^ (1 << k)] + came[i].astype(F32)
    share = keepers[0].astype(BF)[None]
    small = gather_rows(share, "genes", ngene, gene_at).astype(F32)
    small = small.transpose(1, 0, 2).reshape(step, cols)
    latw_out = small[:, : 2 * latent_w]
    up_out = small[:, 2 * latent_w :]

    parts = jnp.concatenate(
        [
            gain_part.reshape(-1, 128),
            shift_part.reshape(-1, 128),
            latb_part.reshape(-1, 128),
            pmean_part.reshape(-1, 128),
            plogv_part.reshape(-1, 128),
        ],
        0,
    )
    parts = butterfly(butterfly(parts, "genes", ngene), "cells", ncell)
    vec = model // 128
    tab = pmean_part.size // 128

    def own(flat, full_shape):
        whole = flat.reshape(full_shape)
        each = full_shape[0] // ncell
        return lax.dynamic_slice_in_dim(whole, cell_at * each, each, 0)

    gain_out = own(parts[:vec], (model,))
    shift_out = own(parts[vec : 2 * vec], (model,))
    latb_out = own(parts[2 * vec : 3 * vec], (2 * latent_w,))
    pmean_out = own(parts[3 * vec : 3 * vec + tab], pmean_part.shape)
    plogv_out = own(parts[3 * vec + tab :], plogv_part.shape)
    return (
        decoded,
        counts_grad,
        emb_out,
        gain_out,
        shift_out,
        latw_out,
        latb_out,
        up_out,
        dec_out,
        pmean_out,
        plogv_out,
        kl_loss.reshape(1),
    )


def solution(mesh):
    ncell, ngene = mesh.shape["cells"], mesh.shape["genes"]

    def body(*args):
        return on_device(*args, ncell=ncell, ngene=ngene)

    return jax.shard_map(
        body,
        mesh=mesh,
        in_specs=(
            P("cells", "genes"),
            P("cells"),
            P("cells"),
            P(),
            P(),
            P("cells", None),
            P(None, "genes"),
            P(),
            P(),
            P(),
            P(),
            P(),
            P(None, "genes"),
            P(),
            P(),
            P("cells", "genes"),
        ),
        out_specs=(
            P("cells", "genes"),
            P("cells", "genes"),
            P("cells", "genes"),
            P("cells"),
            P("cells"),
            P("cells", None),
            P("cells"),
            P("cells", None),
            P("cells", "genes"),
            P("cells", None),
            P("cells", None),
            P(),
        ),
        check_vma=False,
    )
```

time: 963 us -> 449 us (0.47)
  waiting for transfers between devices: 608 us -> 176 us
  blocking collectives: 155 us -> 0 us
  starting transfers between devices: 0.75 us -> 61.6 us
  local copies, waits for them, and re-layouts: 13.8 us -> 51.6 us
  matrix products: 150 us -> 113 us
  other arithmetic: 10.6 us -> 32.6 us
  between operations: 18.7 us -> 5.67 us
    reduce_scatter x4 -> x0, waiting for transfers between devices: 541 us -> none  [the longest x1 231 us: on_device(): lax.psum_scatter(emb_grad, 'cells', scatter_dimension=0, tiled=True)]
    ppermute x0 -> x52, waiting for transfers between devices: none -> 176 us  [flip(): return lax.ppermute(x, axis, [(i, i ^ mask) for i in range(size)])]
    psum x3 -> x0, blocking collectives: 122 us -> none  [the longest x1 76.6 us: on_device(): mixed_grad = lax.psum(partial_mixed, 'genes').astype(jnp.bfloat16)]
    psum x1 -> x0, waiting for transfers between devices: 67 us -> none  [on_device(): embedded = lax.psum(partial_embed, 'genes')]
    ppermute x0 -> x52, starting transfers between devices: none -> 61.6 us  [flip(): return lax.ppermute(x, axis, [(i, i ^ mask) for i in range(size)])]
    dot_general x27 -> x48, matrix products: 150 us -> 113 us  [the longest x42 107 us: hdot(): lax.dot_general(left, right, (dims, ((), ())), preferred_element_type=F32)]
    unnamed x1 -> x0, blocking collectives: 33.7 us -> none
    unnamed x56 -> x152, local copies, waits for them, and re-layouts: 13.8 us -> 26.8 us
  transfers between devices with their start and end apart: 7 -> 52, of which waited for: 4 -> 25; matrix products, arithmetic and copies ran while one was open for 12% -> 34% of each run, Pallas kernels for 0% -> 0%
where the time goes in v1:
time: 449 us; the launch traced here: 441 us
  waiting for transfers between devices  176 us (39%)
  matrix products  113 us (25%)
  starting transfers between devices  61.6 us (14%)
  local copies, waits for them, and re-layouts  51.6 us (11%)
  other arithmetic  32.6 us (7%)
  between operations  5.67 us (1%)
    ppermute x52, waiting for transfers between devices, flip(): return lax.ppermute(x, axis, [(i, i ^ mask) for i in range(size)])  176 us
    dot_general x42, matrix products, hdot(): lax.dot_general(left, right, (dims, ((), ())), preferred_element_type=F32)  107 us
    ppermute x52, starting transfers between devices, flip(): return lax.ppermute(x, axis, [(i, i ^ mask) for i in range(size)])  61.6 us
    unnamed x152, local copies, waits for them, and re-layouts  26.8 us
  transfers between devices with their start and end apart: 52, of which 25 were waited for; matrix products, arithmetic and copies ran while one was open for 34% of the time, Pallas kernels for 0%

profile of v1, /device:TPU:0, one launch (start us, length us, event | category | flops | bytes accessed | tf_op | source)
XLA Modules:
  0.0 440.8 jit_solution(2289403794828319434)
XLA Ops:
  3.4 3.0 collective-permute-start
  11.6 3.0 collective-permute-start.2
  17.7 5.6 %log_convert_fusion = bf16[1024,3375]{0,1:T(8,128)(2,1)S(1)} fusion(bf16[1024,3375]{0,1:T(8,128)(2,1)} %param.16, f32[1024]{0:T(1024)S(1)} %convert_divide_fusion), kind=kLoop, calls=%fused_computation.1 | loop fusion | flops 13824000 | bytes 13828096 | tf_op jit(solution)/shard_map/convert_element_type | solution.py:135
  23.3 12.5 %convolution_convert_fusion.3 = bf16[1024,1024]{1,0:T(8,128)(2,1)S(1)} fusion(bf16[1024,3375]{0,1:T(8,128)(2,1)S(1)} %log_convert_fusion, bf16[1024,3375]{0,1:T(8,128)(2,1)} %param.22), kind=kOutput, calls=%fused_computation.44 | convolution fusion | flops 7078936576 | bytes 15921152 | tf_op jit(solution)/shard_map/dot_general | solution.py:20
  37.5 8.2 %convolution_convert_fusion.2 = bf16[1024,1024]{1,0:T(8,128)(2,1)S(1)} fusion(bf16[1024,3375]{0,1:T(8,128)(2,1)S(1)} %copy-done.5, bf16[1024,3375]{0,1:T(8,128)(2,1)S(1)} %copy-done.54), kind=kOutput, calls=%fused_computation.43 | convolution fusion | flops 7078936576 | bytes 15921152 | tf_op jit(solution)/shard_map/dot_general | solution.py:20
  54.5 11.3 %collective-permute-done.4 = bf16[256,1024]{1,0:T(8,128)(2,1)S(1)} collective-permute-done((bf16[256,1024]{1,0:T(8,128)(2,1)S(1)}, bf16[256,1024]{1,0:T(8,128)(2,1)S(1)}, u32[]{:S(2)}, u32[]{:S(2)}) %collective-permute-start.4) | collective-permute-done | bytes 524320 | tf_op jit(solution)/shard_map/ppermute | solution.py:28
  83.5 2.8 collective-permute-start.13
  92.9 2.8 fusion.92
  106.0 21.6 %collective-permute-done.29 = f32[152,128]{1,0:T(8,128)S(1)} collective-permute-done((f32[152,128]{1,0:T(8,128)S(1)}, f32[152,128]{1,0:T(8,128)S(1)}, u32[]{:S(2)}, u32[]{:S(2)}) %collective-permute-start.29) | collective-permute-done | bytes 77856 | tf_op jit(solution)/shard_map/ppermute | solution.py:28
  137.2 4.7 %copy.104 = bf16[4,1024,384]{2,1,0:T(8,128)(2,1)} copy(bf16[4,1024,384]{1,2,0:T(8,128)(2,1)} %bitcast.78) | data formatting | bytes 6291456 | tf_op jit(solution)/shard_map/transpose | solution.py:255
  144.6 2.7 dynamic-slice_bitcast_fusion
  152.9 3.5 broadcast_select_fusion.1
  156.9 4.8 %convolution_convert_fusion.6 = bf16[512,896]{1,0:T(8,128)(2,1)} fusion(bf16[1024,3375]{0,1:T(8,128)(2,1)} %param.31, bf16[1024,128]{1,0:T(8,128)(2,1)S(1)} %get-tuple-element.94, bf16[1024,128]{1,0:T(8,128)(2,1)S(1)} %get-tuple-element.92, bf16[1024,128]{1,0:T(8,128)(2,1)S(1)} %get-tuple-element.96, bf16[1024,128]{1,0:T(8,128)(2,1)S(1)} %get-tuple-element.95), kind=kOutput, calls=%fused_computation.53 | convolution fusion | flops 944177152 | bytes 3801088 | tf_op jit(solution)/shard_map/dot_general | solution.py:20
  170.1 16.1 %divide_convert_fusion = bf16[1024,3375]{0,1:T(8,128)(2,1)} fusion(bf16[1024,3375]{0,1:T(8,128)(2,1)} %param.16, bf16[1024,3375]{0,1:T(8,128)(2,1)} %param.22, f32[1024]{0:T(1024)S(1)} %convert_divide_fusion, bf16[512,1024]{1,0:T(8,128)(2,1)S(1)} %get-tuple-element.104, bf16[512,1024]{1,0:T(8,128)(2,1)S(1)} %get-tuple-element.103), kind=kOutput, calls=%fused_computation | convolution fusion | flops 7102818304 | bytes 22837248 | tf_op jit(solution)/shard_map/dot_general | solution.py:20
  193.3 13.4 %convolution_convert_fusion = bf16[1024,3375]{0,1:T(8,128)(2,1)} fusion(bf16[1024,3375]{0,1:T(8,128)(2,1)} %param.28, bf16[512,1024]{1,0:T(8,128)(2,1)S(1)} %get-tuple-element.163, bf16[512,1024]{1,0:T(8,128)(2,1)S(1)} %get-tuple-element.164), kind=kOutput, calls=%fused_computation.3 | convolution fusion | flops 7085538304 | bytes 15921152 | tf_op jit(solution)/shard_map/dot_general | solution.py:20
  214.4 32.3 %collective-permute-done.49 = bf16[512,687]{0,1:T(8,128)(2,1)S(1)} collective-permute-done((bf16[512,687]{0,1:T(8,128)(2,1)S(1)}, bf16[512,687]{0,1:T(8,128)(2,1)S(1)}, u32[]{:S(2)}, u32[]{:S(2)}) %collective-permute-start.49) | collective-permute-done | bytes 703520 | tf_op jit(solution)/shard_map/ppermute | solution.py:28
  252.6 2.9 add_convert_fusion.6
  255.5 5.5 %collective-permute-done.25 = bf16[512,687]{0,1:T(8,128)(2,1)} collective-permute-done((bf16[512,687]{0,1:T(8,128)(2,1)}, bf16[512,687]{0,1:T(8,128)(2,1)}, u32[]{:S(2)}, u32[]{:S(2)}) %collective-permute-start.25) | collective-permute-done | bytes 703520 | tf_op jit(solution)/shard_map/ppermute | solution.py:28
  288.0 9.8 %collective-permute-done.19 = bf16[512,896]{1,0:T(8,128)(2,1)S(1)} collective-permute-done((bf16[512,896]{1,0:T(8,128)(2,1)}, bf16[512,896]{1,0:T(8,128)(2,1)S(1)}, u32[]{:S(2)}, u32[]{:S(2)}) %collective-permute-start.19) | collective-permute-done | bytes 917536 | tf_op jit(solution)/shard_map/ppermute | solution.py:28
  301.2 16.3 %collective-permute-done.22 = bf16[512,896]{1,0:T(8,128)(2,1)S(1)} collective-permute-done((bf16[512,896]{1,0:T(8,128)(2,1)S(1)}, bf16[512,896]{1,0:T(8,128)(2,1)S(1)}, u32[]{:S(2)}, u32[]{:S(2)}) %collective-permute-start.22) | collective-permute-done | bytes 917536 | tf_op jit(solution)/shard_map/ppermute | solution.py:28
  322.2 3.7 collective-permute-done.35
  326.3 13.2 %collective-permute-done.51 = bf16[128,687]{1,0:T(8,128)(2,1)S(1)} collective-permute-done((bf16[128,687]{1,0:T(8,128)(2,1)S(1)}, bf16[128,687]{1,0:T(8,128)(2,1)S(1)}, u32[]{:S(2)}, u32[]{:S(2)}) %collective-permute-start.51) | collective-permute-done | bytes 175904 | tf_op jit(solution)/shard_map/ppermute | solution.py:28
  339.6 3.4 collective-permute-start.27
  343.6 4.7 %collective-permute-done.27 = bf16[128,687]{1,0:T(8,128)(2,1)S(1)} collective-permute-done((bf16[128,687]{1,0:T(8,128)(2,1)S(1)}, bf16[128,687]{1,0:T(8,128)(2,1)S(1)}, u32[]{:S(2)}, u32[]{:S(2)}) %collective-permute-start.27) | collective-permute-done | bytes 175904 | tf_op jit(solution)/shard_map/ppermute | solution.py:28
  354.7 3.5 collective-permute-start.42
  361.6 17.9 %collective-permute-done.36 = bf16[2,128,384]{2,1,0:T(8,128)(2,1)S(1)} collective-permute-done((bf16[2,128,384]{2,1,0:T(8,128)(2,1)S(1)}, bf16[2,128,384]{2,1,0:T(8,128)(2,1)S(1)}, u32[]{:S(2)}, u32[]{:S(2)}) %collective-permute-start.36) | collective-permute-done | bytes 196640 | tf_op jit(solution)/shard_map/ppermute | solution.py:28
  379.6 3.0 collective-permute-start.37
  383.3 10.1 %collective-permute-done.37 = bf16[1,128,384]{2,1,0:T(8,128)(2,1)S(1)} collective-permute-done((bf16[1,128,384]{2,1,0:T(8,128)(2,1)S(1)}, bf16[1,128,384]{2,1,0:T(8,128)(2,1)S(1)}, u32[]{:S(2)}, u32[]{:S(2)}) %collective-permute-start.37) | collective-permute-done | bytes 98336 | tf_op jit(solution)/shard_map/ppermute | solution.py:28
  398.2 2.8 collective-permute-start.21
  407.8 8.4 %collective-permute-done.18 = bf16[128,896]{1,0:T(8,128)(2,1)S(1)} collective-permute-done((bf16[128,896]{1,0:T(8,128)(2,1)S(1)}, bf16[128,896]{1,0:T(8,128)(2,1)S(1)}, u32[]{:S(2)}, u32[]{:S(2)}) %collective-permute-start.18) | collective-permute-done | bytes 229408 | tf_op jit(solution)/shard_map/ppermute | solution.py:28
  417.9 3.2 collective-permute-done.21
  421.8 4.1 collective-permute-done.24
  (374 shorter events, 174.3 us)
Async XLA Ops:
  54.3 32.0 %collective-permute-start.8 = (bf16[256,1024]{1,0:T(8,128)(2,1)}, bf16[256,1024]{1,0:T(8,128)(2,1)}, u32[]{:S(2)}, u32[]{:S(2)}) collective-permute-start(bf16[256,1024]{1,0:T(8,128)(2,1)} %fusion.91), channel_id=1, source_target_pairs={{0,2},{1,3},{2,0},{3,1},{4,6},{5,7},{6,4},{7,5},{8,10},{9,11},{10,... | collective-permute-start | bytes 1572872 | tf_op jit(solution)/shard_map/ppermute | solution.py:28
  100.3 29.0 %collective-permute-start.5 = (bf16[256,1024]{1,0:T(8,128)(2,1)S(1)}, bf16[256,1024]{1,0:T(8,128)(2,1)S(1)}, u32[]{:S(2)}, u32[]{:S(2)}) collective-permute-start(bf16[256,1024]{1,0:T(8,128)(2,1)S(1)} %fusion), channel_id=1, source_target_pairs={{0,2},{1,3},{2,0},{3,1},{4,6},{5,7},{6,4},{7,5},{8,10},{9,11},{10,... | collective-permute-start | bytes 1572872 | tf_op jit(solution)/shard_map/ppermute | solution.py:28
  102.5 28.1 %collective-permute-start.14 = (bf16[256,1024]{1,0:T(8,128)(2,1)S(1)}, bf16[256,1024]{1,0:T(8,128)(2,1)S(1)}, u32[]{:S(2)}, u32[]{:S(2)}) collective-permute-start(bf16[256,1024]{1,0:T(8,128)(2,1)S(1)} %multiply_convert_fusion), channel_id=1, source_target_pairs={{0,2},{1,3},{2,0},{3,1},{4,6},{5,7},{6,4},{7,5},{8,10},{9,11},{10,... | collective-permute-start | bytes 1572872 | tf_op jit(solution)/shard_map/ppermute | solution.py:28
  102.9 24.7 %collective-permute-start.29 = (f32[152,128]{1,0:T(8,128)S(1)}, f32[152,128]{1,0:T(8,128)S(1)}, u32[]{:S(2)}, u32[]{:S(2)}) collective-permute-start(f32[152,128]{1,0:T(8,128)S(1)} %add.486), channel_id=1, source_target_pairs={{0,2},{1,3},{2,0},{3,1},{4,6},{5,7},{6,4},{7,5},{8,10},{9,11},{10,... | collective-permute-start | bytes 233480 | tf_op jit(solution)/shard_map/ppermute | solution.py:28
  130.6 21.3 %collective-permute-start.6 = (bf16[512,1024]{1,0:T(8,128)(2,1)}, bf16[512,1024]{1,0:T(8,128)(2,1)S(1)}, u32[]{:S(2)}, u32[]{:S(2)}) collective-permute-start(bf16[512,1024]{1,0:T(8,128)(2,1)} %pad_maximum_fusion.20), channel_id=1, source_target_pairs={{0,1},{1,0},{2,3},{3,2},{4,5},{5,4},{6,7},{7,6},{8,9},{9,8},{10,11... | collective-permute-start | bytes 3145736 | tf_op jit(solution)/shard_map/ppermute | solution.py:28
  147.3 61.2 %collective-permute-start.33 = (bf16[2,1024,384]{2,1,0:T(8,128)(2,1)}, bf16[2,1024,384]{2,1,0:T(8,128)(2,1)}, u32[]{:S(2)}, u32[]{:S(2)}) collective-permute-start(bf16[2,1024,384]{2,1,0:T(8,128)(2,1)} %dynamic-slice_bitcast_fusion), channel_id=1, source_target_pairs={{0,1},{1,0},{2,3},{3,2},{4,5},{5,4},{6,7},{7,6},{8,9},{9,8},{10,11... | collective-permute-start | bytes 4718600 | tf_op jit(solution)/shard_map/ppermute | solution.py:28
  188.5 88.5 %collective-permute-start.40 = (bf16[512,896]{1,0:T(8,128)(2,1)}, bf16[512,896]{1,0:T(8,128)(2,1)}, u32[]{:S(2)}, u32[]{:S(2)}) collective-permute-start(bf16[512,896]{1,0:T(8,128)(2,1)} %convolution_convert_fusion.7), channel_id=1, source_target_pairs={{0,8},{4,12},{8,0},{12,4},{16,24},{20,28},{24,16},{28,20},{1,9},{5... | collective-permute-start | bytes 2752520 | tf_op jit(solution)/shard_map/ppermute | solution.py:28
  188.5 91.0 %collective-permute-start.43 = (bf16[512,896]{1,0:T(8,128)(2,1)}, bf16[512,896]{1,0:T(8,128)(2,1)}, u32[]{:S(2)}, u32[]{:S(2)}) collective-permute-start(bf16[512,896]{1,0:T(8,128)(2,1)} %convolution_convert_fusion.6), channel_id=1, source_target_pairs={{0,4},{4,0},{8,12},{12,8},{16,20},{20,16},{24,28},{28,24},{1,5},{5... | collective-permute-start | bytes 2752520 | tf_op jit(solution)/shard_map/ppermute | solution.py:28
  189.0 92.2 %collective-permute-start.46 = (bf16[512,896]{1,0:T(8,128)(2,1)}, bf16[512,896]{1,0:T(8,128)(2,1)}, u32[]{:S(2)}, u32[]{:S(2)}) collective-permute-start(bf16[512,896]{1,0:T(8,128)(2,1)} %convolution_convert_fusion.5), channel_id=1, source_target_pairs={{0,4},{4,0},{8,12},{12,8},{16,20},{20,16},{24,28},{28,24},{1,5},{5... | collective-permute-start | bytes 2752520 | tf_op jit(solution)/shard_map/ppermute | solution.py:28
  190.5 56.2 %collective-permute-start.49 = (bf16[512,687]{0,1:T(8,128)(2,1)S(1)}, bf16[512,687]{0,1:T(8,128)(2,1)S(1)}, u32[]{:S(2)}, u32[]{:S(2)}) collective-permute-start(bf16[512,687]{0,1:T(8,128)(2,1)S(1)} %convolution_convert_fusion.11), channel_id=1, source_target_pairs={{0,4},{4,0},{8,12},{12,8},{16,20},{20,16},{24,28},{28,24},{1,5},{5... | collective-permute-start | bytes 2110472 | tf_op jit(solution)/shard_map/ppermute | solution.py:28
  208.5 52.5 %collective-permute-start.25 = (bf16[512,687]{0,1:T(8,128)(2,1)}, bf16[512,687]{0,1:T(8,128)(2,1)}, u32[]{:S(2)}, u32[]{:S(2)}) collective-permute-start(bf16[512,687]{0,1:T(8,128)(2,1)} %convolution_convert_fusion.12), channel_id=1, source_target_pairs={{0,4},{4,0},{8,12},{12,8},{16,20},{20,16},{24,28},{28,24},{1,5},{5... | collective-permute-start | bytes 2110472 | tf_op jit(solution)/shard_map/ppermute | solution.py:28
  246.7 27.6 %collective-permute-start.34 = (bf16[1,1024,384]{2,1,0:T(8,128)(2,1)}, bf16[1,1024,384]{2,1,0:T(8,128)(2,1)}, u32[]{:S(2)}, u32[]{:S(2)}) collective-permute-start(bf16[1,1024,384]{2,1,0:T(8,128)(2,1)} %dynamic-slice_convert_fusion), channel_id=1, source_target_pairs={{0,2},{1,3},{2,0},{3,1},{4,6},{5,7},{6,4},{7,5},{8,10},{9,11},{10,... | collective-permute-start | bytes 2359304 | tf_op jit(solution)/shard_map/ppermute | solution.py:28
  261.0 23.5 %collective-permute-start.16 = (bf16[512,896]{1,0:T(8,128)(2,1)}, bf16[512,896]{1,0:T(8,128)(2,1)}, u32[]{:S(2)}, u32[]{:S(2)}) collective-permute-start(bf16[512,896]{1,0:T(8,128)(2,1)} %convolution_convert_fusion.10), channel_id=1, source_target_pairs={{0,8},{4,12},{8,0},{12,4},{16,24},{20,28},{24,16},{28,20},{1,9},{5... | collective-permute-start | bytes 2752520 | tf_op jit(solution)/shard_map/ppermute | solution.py:28
  274.3 23.5 %collective-permute-start.19 = (bf16[512,896]{1,0:T(8,128)(2,1)}, bf16[512,896]{1,0:T(8,128)(2,1)S(1)}, u32[]{:S(2)}, u32[]{:S(2)}) collective-permute-start(bf16[512,896]{1,0:T(8,128)(2,1)} %convolution_convert_fusion.9), channel_id=1, source_target_pairs={{0,4},{4,0},{8,12},{12,8},{16,20},{20,16},{24,28},{28,24},{1,5},{5... | collective-permute-start | bytes 2752520 | tf_op jit(solution)/shard_map/ppermute | solution.py:28
  277.0 40.5 %collective-permute-start.22 = (bf16[512,896]{1,0:T(8,128)(2,1)S(1)}, bf16[512,896]{1,0:T(8,128)(2,1)S(1)}, u32[]{:S(2)}, u32[]{:S(2)}) collective-permute-start(bf16[512,896]{1,0:T(8,128)(2,1)S(1)} %copy-done.56), channel_id=1, source_target_pairs={{0,4},{4,0},{8,12},{12,8},{16,20},{20,16},{24,28},{28,24},{1,5},{5... | collective-permute-start | bytes 2752520 | tf_op jit(solution)/shard_map/ppermute | solution.py:28
  279.6 39.2 %collective-permute-start.50 = (bf16[256,687]{1,0:T(8,128)(2,1)S(1)}, bf16[256,687]{1,0:T(8,128)(2,1)S(1)}, u32[]{:S(2)}, u32[]{:S(2)}) collective-permute-start(bf16[256,687]{1,0:T(8,128)(2,1)S(1)} %copy-done.57), channel_id=1, source_target_pairs={{0,8},{4,12},{8,0},{12,4},{16,24},{20,28},{24,16},{28,20},{1,9},{5... | collective-permute-start | bytes 1055240 | tf_op jit(solution)/shard_map/ppermute | solution.py:28
  281.2 39.8 %collective-permute-start.26 = (bf16[256,687]{1,0:T(8,128)(2,1)S(1)}, bf16[256,687]{1,0:T(8,128)(2,1)S(1)}, u32[]{:S(2)}, u32[]{:S(2)}) collective-permute-start(bf16[256,687]{1,0:T(8,128)(2,1)S(1)} %add_convert_fusion.7), channel_id=1, source_target_pairs={{0,8},{4,12},{8,0},{12,4},{16,24},{20,28},{24,16},{28,20},{1,9},{5... | collective-permute-start | bytes 1055240 | tf_op jit(solution)/shard_map/ppermute | solution.py:28
  284.6 41.3 %collective-permute-start.35 = (bf16[4,128,384]{2,1,0:T(8,128)(2,1)S(1)}, bf16[4,128,384]{2,1,0:T(8,128)(2,1)S(1)}, u32[]{:S(2)}, u32[]{:S(2)}) collective-permute-start(bf16[4,128,384]{2,1,0:T(8,128)(2,1)S(1)} %pad_maximum_fusion.28), channel_id=1, source_target_pairs={{0,4},{4,0},{8,12},{12,8},{16,20},{20,16},{24,28},{28,24},{1,5},{5... | collective-permute-start | bytes 1179656 | tf_op jit(solution)/shard_map/ppermute | solution.py:28
  297.8 51.1 %collective-permute-start.41 = (bf16[256,896]{1,0:T(8,128)(2,1)S(1)}, bf16[256,896]{1,0:T(8,128)(2,1)S(1)}, u32[]{:S(2)}, u32[]{:S(2)}) collective-permute-start(bf16[256,896]{1,0:T(8,128)(2,1)S(1)} %add_convert_fusion.2), channel_id=1, source_target_pairs={{0,4},{4,0},{8,12},{12,8},{16,20},{20,16},{24,28},{28,24},{1,5},{5... | collective-permute-start | bytes 1376264 | tf_op jit(solution)/shard_map/ppermute | solution.py:28
  317.5 35.4 %collective-permute-start.44 = (bf16[256,896]{1,0:T(8,128)(2,1)S(1)}, bf16[256,896]{1,0:T(8,128)(2,1)S(1)}, u32[]{:S(2)}, u32[]{:S(2)}) collective-permute-start(bf16[256,896]{1,0:T(8,128)(2,1)S(1)} %add_convert_fusion.1), channel_id=1, source_target_pairs={{0,8},{4,12},{8,0},{12,4},{16,24},{20,28},{24,16},{28,20},{1,9},{5... | collective-permute-start | bytes 1376264 | tf_op jit(solution)/shard_map/ppermute | solution.py:28
  318.8 35.9 %collective-permute-start.47 = (bf16[256,896]{1,0:T(8,128)(2,1)S(1)}, bf16[256,896]{1,0:T(8,128)(2,1)S(1)}, u32[]{:S(2)}, u32[]{:S(2)}) collective-permute-start(bf16[256,896]{1,0:T(8,128)(2,1)S(1)} %add_convert_fusion), channel_id=1, source_target_pairs={{0,8},{4,12},{8,0},{12,4},{16,24},{20,28},{24,16},{28,20},{1,9},{5... | collective-permute-start | bytes 1376264 | tf_op jit(solution)/shard_map/ppermute | solution.py:28
  321.0 38.8 %collective-permute-start.17 = (bf16[256,896]{1,0:T(8,128)(2,1)S(1)}, bf16[256,896]{1,0:T(8,128)(2,1)S(1)}, u32[]{:S(2)}, u32[]{:S(2)}) collective-permute-start(bf16[256,896]{1,0:T(8,128)(2,1)S(1)} %add_convert_fusion.5), channel_id=1, source_target_pairs={{0,4},{4,0},{8,12},{12,8},{16,20},{20,16},{24,28},{28,24},{1,5},{5... | collective-permute-start | bytes 1376264 | tf_op jit(solution)/shard_map/ppermute | solution.py:28
  348.3 31.3 %collective-permute-start.20 = (bf16[256,896]{1,0:T(8,128)(2,1)S(1)}, bf16[256,896]{1,0:T(8,128)(2,1)S(1)}, u32[]{:S(2)}, u32[]{:S(2)}) collective-permute-start(bf16[256,896]{1,0:T(8,128)(2,1)S(1)} %add_convert_fusion.4), channel_id=1, source_target_pairs={{0,8},{4,12},{8,0},{12,4},{16,24},{20,28},{24,16},{28,20},{1,9},{5... | collective-permute-start | bytes 1376264 | tf_op jit(solution)/shard_map/ppermute | solution.py:28
  348.9 44.6 %collective-permute-start.23 = (bf16[256,896]{1,0:T(8,128)(2,1)S(1)}, bf16[256,896]{1,0:T(8,128)(2,1)S(1)}, u32[]{:S(2)}, u32[]{:S(2)}) collective-permute-start(bf16[256,896]{1,0:T(8,128)(2,1)S(1)} %add_convert_fusion.3), channel_id=1, source_target_pairs={{0,8},{4,12},{8,0},{12,4},{16,24},{20,28},{24,16},{28,20},{1,9},{5... | collective-permute-start | bytes 1376264 | tf_op jit(solution)/shard_map/ppermute | solution.py:28
  352.9 26.6 %collective-permute-start.36 = (bf16[2,128,384]{2,1,0:T(8,128)(2,1)S(1)}, bf16[2,128,384]{2,1,0:T(8,128)(2,1)S(1)}, u32[]{:S(2)}, u32[]{:S(2)}) collective-permute-start(bf16[2,128,384]{2,1,0:T(8,128)(2,1)S(1)} %pad_maximum_fusion.29), channel_id=1, source_target_pairs={{0,8},{4,12},{8,0},{12,4},{16,24},{20,28},{24,16},{28,20},{1,9},{5... | collective-permute-start | bytes 589832 | tf_op jit(solution)/shard_map/ppermute | solution.py:28
  354.7 46.5 %collective-permute-start.42 = (bf16[128,896]{1,0:T(8,128)(2,1)S(1)}, bf16[128,896]{1,0:T(8,128)(2,1)S(1)}, u32[]{:S(2)}, u32[]{:S(2)}) collective-permute-start(bf16[128,896]{1,0:T(8,128)(2,1)S(1)} %fusion.27), channel_id=1, source_target_pairs={{0,16},{4,20},{8,24},{12,28},{16,0},{20,4},{24,8},{28,12},{1,17},{... | collective-permute-start | bytes 688136 | tf_op jit(solution)/shard_map/ppermute | solution.py:28
  359.8 43.2 %collective-permute-start.45 = (bf16[128,896]{1,0:T(8,128)(2,1)S(1)}, bf16[128,896]{1,0:T(8,128)(2,1)S(1)}, u32[]{:S(2)}, u32[]{:S(2)}) collective-permute-start(bf16[128,896]{1,0:T(8,128)(2,1)S(1)} %fusion.26), channel_id=1, source_target_pairs={{0,16},{4,20},{8,24},{12,28},{16,0},{20,4},{24,8},{28,12},{1,17},{... | collective-permute-start | bytes 688136 | tf_op jit(solution)/shard_map/ppermute | solution.py:28
  379.5 25.2 %collective-permute-start.48 = (bf16[128,896]{1,0:T(8,128)(2,1)S(1)}, bf16[128,896]{1,0:T(8,128)(2,1)S(1)}, u32[]{:S(2)}, u32[]{:S(2)}) collective-permute-start(bf16[128,896]{1,0:T(8,128)(2,1)S(1)} %fusion.25), channel_id=1, source_target_pairs={{0,16},{4,20},{8,24},{12,28},{16,0},{20,4},{24,8},{28,12},{1,17},{... | collective-permute-start | bytes 688136 | tf_op jit(solution)/shard_map/ppermute | solution.py:28
  393.4 22.8 %collective-permute-start.18 = (bf16[128,896]{1,0:T(8,128)(2,1)S(1)}, bf16[128,896]{1,0:T(8,128)(2,1)S(1)}, u32[]{:S(2)}, u32[]{:S(2)}) collective-permute-start(bf16[128,896]{1,0:T(8,128)(2,1)S(1)} %fusion.30), channel_id=1, source_target_pairs={{0,16},{4,20},{8,24},{12,28},{16,0},{20,4},{24,8},{28,12},{1,17},{... | collective-permute-start | bytes 688136 | tf_op jit(solution)/shard_map/ppermute | solution.py:28
  398.2 22.9 %collective-permute-start.21 = (bf16[128,896]{1,0:T(8,128)(2,1)S(1)}, bf16[128,896]{1,0:T(8,128)(2,1)S(1)}, u32[]{:S(2)}, u32[]{:S(2)}) collective-permute-start(bf16[128,896]{1,0:T(8,128)(2,1)S(1)} %fusion.29), channel_id=1, source_target_pairs={{0,16},{4,20},{8,24},{12,28},{16,0},{20,4},{24,8},{28,12},{1,17},{... | collective-permute-start | bytes 688136 | tf_op jit(solution)/shard_map/ppermute | solution.py:28
  401.2 24.8 %collective-permute-start.24 = (bf16[128,896]{1,0:T(8,128)(2,1)S(1)}, bf16[128,896]{1,0:T(8,128)(2,1)S(1)}, u32[]{:S(2)}, u32[]{:S(2)}) collective-permute-start(bf16[128,896]{1,0:T(8,128)(2,1)S(1)} %fusion.28), channel_id=1, source_target_pairs={{0,16},{4,20},{8,24},{12,28},{16,0},{20,4},{24,8},{28,12},{1,17},{... | collective-permute-start | bytes 688136 | tf_op jit(solution)/shard_map/ppermute | solution.py:28
  403.0 30.1 %collective-permute-start.39 = (bf16[2,128,384]{2,1,0:T(8,128)(2,1)S(1)}, bf16[2,128,384]{2,1,0:T(8,128)(2,1)}, u32[]{:S(2)}, u32[]{:S(2)}) collective-permute-start(bf16[2,128,384]{2,1,0:T(8,128)(2,1)S(1)} %pad_maximum_fusion.30), channel_id=1, source_target_pairs={{0,1},{1,0},{2,3},{3,2},{4,5},{5,4},{6,7},{7,6},{8,9},{9,8},{10,11... | collective-permute-start | bytes 589832 | tf_op jit(solution)/shard_map/ppermute | solution.py:28
  (87 other events, 730.1 us)

commit v2 on v1

--- a/solution.py
+++ b/solution.py
@@ -1,6 +1,10 @@
+import functools
+
 import jax
 import jax.numpy as jnp
 from jax import lax
+from jax.experimental import pallas as pl
+from jax.experimental.pallas import tpu as pltpu
 from jax.sharding import PartitionSpec as P
 
 WARM = 1000
@@ -8,6 +12,134 @@
 FREE = 1.0
 BF = jnp.bfloat16
 F32 = jnp.float32
+
+
+MESH = pl.DeviceIdType.MESH
+
+
+def chunks_of(width, step):
+    edges = list(range(0, width, step)) + [width]
+    return list(zip(edges[:-1], edges[1:]))
+
+
+def xor_const(at, k_bits, value):
+    out=0
+    for k in range(k_bits):
+        bit=lax.rem(lax.div(at, 1<<k), 2)
+        if (value>>k)&1: bit=1-bit
+        out=out+bit*(1<<k)
+    return out
+
+def rev(i, n):
+    return int(format(i, f"0{n}b")[::-1], 2) if n else 0
+
+TILE=256
+def sum_kernel(ncell, chunks, *refs):
+    nb=bits_of(ncell)
+    nch=len(chunks)
+    xts=refs[0:2]; rights=refs[2:4]; outs=refs[4:6]
+    pos=6
+    lefts=refs[pos:pos+2]; pos+=2
+    sends=[refs[pos+t*nch:pos+(t+1)*nch] for t in range(2)]; pos+=2*nch
+    recvs=[[refs[pos+(t*nch+i)*nb:pos+(t*nch+i+1)*nb] for i in range(nch)] for t in range(2)]; pos+=2*nch*nb
+    lsem, ssem, rsem = refs[pos:pos+3]
+    at=lax.axis_index("cells")
+    model=xts[0].shape[0]
+    step=model//ncell
+    peers=[xor_const(at,nb,1<<k) for k in range(nb)]
+    barrier=pltpu.get_barrier_semaphore()
+    for p in peers:
+        pl.semaphore_signal(barrier, inc=1, device_id={"cells":p}, device_id_type=MESH)
+    loads=[]
+    for t in range(2):
+        for i in range(ncell):
+            src=xor_const(at,nb,rev(i,nb))
+            cp=pltpu.make_async_copy(xts[t].at[pl.ds(pl.multiple_of(src*step,step),step)], lefts[t].at[pl.ds(i*step,step)], lsem.at[t])
+            cp.start(); loads.append(cp)
+    pl.semaphore_wait(barrier, nb)
+
+    def mm(t, c, lo, hi, emit):
+        a,b=chunks[c]
+        full=(b-a)//TILE
+        def one(off, w):
+            left=lefts[t][lo:hi,:]
+            right=rights[t][:, pl.ds(a+off, w)]
+            emit(off, w, jnp.dot(left,right,preferred_element_type=F32))
+        if full:
+            def body(j,_):
+                one(pl.multiple_of(j*TILE,TILE),TILE); return 0
+            lax.fori_loop(0,full,body,0)
+        if (b-a)%TILE: one(full*TILE,(b-a)%TILE)
+
+    copies={}
+    def send(t,c,k,src):
+        cp=pltpu.make_async_remote_copy(src_ref=src,dst_ref=recvs[t][c][k],send_sem=ssem.at[t,c,k],recv_sem=rsem.at[t,c,k],
+            device_id={"cells":peers[k]},device_id_type=MESH)
+        cp.start(); copies[t,c,k]=cp
+
+    def stage(t,c,k):
+        h=model>>(k+1)
+        for j in range(k):
+            if j==k-1: copies[t,c,j].wait_recv()
+        if k==0:
+            dst=sends[t][c];
+            def emit(off,w,v): dst[:,pl.ds(off,w)]=v.astype(BF)
+            mm(t,c,h,2*h,emit)
+            send(t,c,0,dst)
+            return
+        dst=recvs[t][c][k-1]
+        def emit(off,w,v):
+            for j in range(k):
+                v=v+recvs[t][c][j][h:2*h,pl.ds(off,w)].astype(F32)
+            dst[h:2*h,pl.ds(off,w)]=v.astype(BF)
+        mm(t,c,h,2*h,emit)
+        send(t,c,k,dst.at[pl.ds(h,h)])
+
+    def final(t,c):
+        copies[t,c,nb-1].wait_recv()
+        a,b=chunks[c]
+        def emit(off,w,v):
+            for j in range(nb):
+                v=v+recvs[t][c][j][0:step,pl.ds(off,w)].astype(F32)
+            outs[t][:,pl.ds(a+off,w)]=v
+        mm(t,c,0,step,emit)
+
+    for cp in loads[:ncell]: cp.wait()
+    order=[(0,c) for c in range(nch)]+[(1,c) for c in range(nch)]
+    n=len(order)
+    ahead=3
+    for i in range(min(ahead,n)):
+        if i==0: pass
+        if order[i][0]==1 and i>0 and order[i-1][0]==0:
+            for cp in loads[ncell:]: cp.wait()
+        stage(*order[i],0)
+    for s in range(n+nb):
+        if s+ahead<n:
+            if order[s+ahead]==(1,0):
+                for cp in loads[ncell:]: cp.wait()
+            stage(*order[s+ahead],0)
+        for k in range(1,nb+1):
+            i=s-(k-1)
+            if 0<=i<n:
+                if k<nb: stage(*order[i],k)
+                else: final(*order[i])
+    for cp in copies.values(): cp.wait_send()
+
+def pair_sums(xt_a, xt_b, right_a, right_b, ncell, chunk=512):
+    model,rows=xt_a.shape; width=right_a.shape[1]
+    nb=bits_of(ncell); step=model//ncell
+    chunks=chunks_of(width,chunk); nch=len(chunks)
+    sends=[pltpu.VMEM((model//2,b-a),BF) for _ in range(2) for a,b in chunks]
+    recvs=[pltpu.VMEM((model>>(k+1),b-a),BF) for _ in range(2) for a,b in chunks for k in range(nb)]
+    vm=pl.BlockSpec(memory_space=pltpu.VMEM); anyv=pl.BlockSpec(memory_space=pl.ANY)
+    return pl.pallas_call(
+        functools.partial(sum_kernel,ncell,chunks),
+        out_shape=[jax.ShapeDtypeStruct((step,width),F32)]*2,
+        in_specs=[anyv,anyv,vm,vm], out_specs=[vm,vm],
+        scratch_shapes=[pltpu.VMEM((model,rows),BF)]*2+sends+recvs+[pltpu.SemaphoreType.DMA((2,)),pltpu.SemaphoreType.DMA((2,nch,nb)),pltpu.SemaphoreType.DMA((2,nch,nb))],
+        compiler_params=pltpu.CompilerParams(collective_id=0,has_side_effects=True,vmem_limit_bytes=67043328),
+        name="pair_sums",
+    )(xt_a,xt_b,right_a,right_b)
 
 
 def edot(left, right, dims=((1,), (0,))):
@@ -59,31 +191,6 @@
     for k in range(bits_of(size)):
         block = block * 2 + ((at >> k) & 1)
     return block
-
-
-def halving(blocks, right, axis, size, order):
-    live = list(range(size))
-    arrived = {r: [] for r in live}
-    for k in order:
-        sent = [r for r in live if (r >> k) & 1]
-        live = [r for r in live if not (r >> k) & 1]
-        part = hdot(jnp.concatenate([blocks[r] for r in sent], 1), right, ((0,), (0,)))
-        for got in range(len(arrived[sent[0]])):
-            part = part + jnp.concatenate([arrived[r][got] for r in sent], 0).astype(F32)
-        came = flip(part.astype(BF), axis, size, 1 << k)
-        width = blocks[0].shape[1]
-        for i, r in enumerate(sent):
-            arrived[r ^ (1 << k)].append(came[i * width : (i + 1) * width])
-    total = hdot(blocks[0], right, ((0,), (0,)))
-    for part in arrived[0]:
-        total = total + part.astype(F32)
-    return total
-
-
-def cut(width, parts):
-    step = -(-width // (parts * 128)) * 128
-    edges = list(range(0, width, step)) + [width]
-    return list(zip(edges[:-1], edges[1:]))
 
 
 def on_device(
@@ -159,26 +266,7 @@
     mixed = gather_rows(mixed_mine, "genes", ngene, gene_at)
 
     step = model // ncell
-
-    def blocks_of(x):
-        return [
-            lax.dynamic_slice_in_dim(x, (cell_at ^ r) * step, step, 1) for r in range(ncell)
-        ]
-
-    nbits = bits_of(ncell)
-    straight = list(range(nbits))
-    turned = [1, 0] + straight[2:] if nbits > 1 else straight
-    pieces = cut(width, 4)
-
-    def weight_sum(x, right):
-        blocks = blocks_of(x)
-        outs = []
-        for i, (lo, hi) in enumerate(pieces):
-            order = turned if i == 0 else straight
-            outs.append(halving(blocks, right[:, lo:hi], "cells", ncell, order))
-        return jnp.concatenate(outs, 1)
-
-    dec_out = weight_sum(mixed, out_grad)
+    straight = list(range(bits_of(ncell)))
     decoded = hdot(mixed, dec_weight).astype(BF)
 
     moment = variance + lat_mean * lat_mean
@@ -245,7 +333,7 @@
     ).astype(BF)
     embed_grad = gather_rows(embed_mine, "genes", ngene, gene_at)
 
-    emb_out = weight_sum(embed_grad, normed)
+    dec_out, emb_out = pair_sums(mixed.T, embed_grad.T, out_grad, normed, ncell)
     normed_grad = hdot(embed_grad, emb_weight)
     counts_grad = (normed_grad * scale[:, None] / (1.0 + counts_f * scale[:, None])).astype(BF)
 

time: 449 us -> 452 us (level)
  Pallas kernels: 0 us -> 180 us
  waiting for transfers between devices: 176 us -> 58 us
  matrix products: 113 us -> 68.6 us
  starting transfers between devices: 61.6 us -> 29.3 us
  local copies, waits for them, and re-layouts: 51.6 us -> 63.6 us
  other arithmetic: 32.6 us -> 39.5 us
    pallas_call x0 -> x1, Pallas kernels: none -> 180 us  [pair_sums(): pl.pallas_call(functools.partial(sum_kernel, ncell, chunks), out_shape=[j...]
    ppermute x52 -> x28, waiting for transfers between devices: 176 us -> 58 us  [flip(): return lax.ppermute(x, axis, [(i, i ^ mask) for i in range(size)])]
    dot_general x42 -> x10, matrix products: 107 us -> 62.3 us  [hdot(): lax.dot_general(left, right, (dims, ((), ())), preferred_element_type=F32)]
    ppermute x52 -> x28, starting transfers between devices: 61.6 us -> 29.3 us  [flip(): return lax.ppermute(x, axis, [(i, i ^ mask) for i in range(size)])]
    unnamed x152 -> x81, local copies, waits for them, and re-layouts: 26.8 us -> 44.8 us
    slice x8 -> x0, local copies, waits for them, and re-layouts: 7.37 us -> none  [halving(): arrived[r ^ 1 << k].append(came[i * width:(i + 1) * width])]
    dynamic_slice x0 -> x5, local copies, waits for them, and re-layouts: none -> 6.25 us  [the longest x4 5.27 us: scatter_rows(): keep = lax.dynamic_index_in_dim(halves, bit, 0, keepdims=False)]
  transfers between devices with their start and end apart: 52 -> 28, of which waited for: 25 -> 15; matrix products, arithmetic and copies ran while one was open for 34% -> 31% of each run, Pallas kernels for 0% -> 40%
where the time goes in v2:
time: 452 us; the launch traced here: 444 us
  Pallas kernels  180 us (40%)
  matrix products  68.6 us (15%)
  local copies, waits for them, and re-layouts  63.6 us (14%)
  waiting for transfers between devices  58 us (13%)
  other arithmetic  39.5 us (9%)
  starting transfers between devices  29.3 us (6%)
  between operations  4.77 us (1%)
    pallas_call x1, Pallas kernels, pair_sums(): pl.pallas_call(functools.partial(sum_kernel, ncell, chunks), out_shape=[j...  180 us
    dot_general x10, matrix products, hdot(): lax.dot_general(left, right, (dims, ((), ())), preferred_element_type=F32)  62.3 us
    ppermute x28, waiting for transfers between devices, flip(): return lax.ppermute(x, axis, [(i, i ^ mask) for i in range(size)])  58 us
    unnamed x81, local copies, waits for them, and re-layouts  44.8 us
    ppermute x28, starting transfers between devices, flip(): return lax.ppermute(x, axis, [(i, i ^ mask) for i in range(size)])  29.3 us
  transfers between devices with their start and end apart: 28, of which 15 were waited for; matrix products, arithmetic and copies ran while one was open for 31% of the time, Pallas kernels for 40%

profile of v2, /device:TPU:0, one launch (start us, length us, event | category | flops | bytes accessed | tf_op | source)
XLA Modules:
  0.0 443.6 jit_solution(17837720010506209594)
XLA Ops:
  3.2 3.0 collective-permute-start
  6.2 12.0 %convolution_convert_fusion.2 = bf16[1024,1024]{1,0:T(8,128)(2,1)S(1)} fusion(bf16[1024,3375]{0,1:T(8,128)(2,1)} %param.31, bf16[1024,3375]{0,1:T(8,128)(2,1)} %param.28), kind=kOutput, calls=%fused_computation.11 | convolution fusion | flops 7078936576 | bytes 15921152 | tf_op jit(solution)/shard_map/dot_general | solution.py:152
  19.2 10.2 %copy.73 = bf16[1024,3375]{1,0:T(8,128)(2,1)} copy(bf16[1024,3375]{0,1:T(8,128)(2,1)} %param.16) | data formatting | bytes 13824000 | tf_op args[0]
  31.1 2.0 collective-permute-done.1
  33.1 2.6 collective-permute-start.2
  38.4 6.7 %log_convert_fusion.refs_3_ = bf16[1024,3375]{1,0:T(8,128)(2,1)S(1)} fusion(bf16[1024,3375]{1,0:T(8,128)(2,1)} %copy.73, f32[1024]{0:T(1024)S(1)} %convert_divide_fusion), kind=kLoop, calls=%fused_computation.1 | loop fusion | flops 13824000 | bytes 13828096 | tf_op jit(solution)/shard_map/convert_element_type | solution.py:242
  45.1 12.7 %convolution_convert_fusion.3 = bf16[1024,1024]{1,0:T(8,128)(2,1)S(1)} fusion(bf16[1024,3375]{1,0:T(8,128)(2,1)S(1)} %log_convert_fusion.refs_3_, bf16[1024,3375]{0,1:T(8,128)(2,1)} %param.22), kind=kOutput, calls=%fused_computation.12 | convolution fusion | flops 7078936576 | bytes 15921152 | tf_op jit(solution)/shard_map/dot_general | solution.py:152
  60.6 2.6 collective-permute-done.3
  71.3 10.6 %collective-permute-done.4 = bf16[256,1024]{0,1:T(8,128)(2,1)} collective-permute-done((bf16[256,1024]{0,1:T(8,128)(2,1)}, bf16[256,1024]{0,1:T(8,128)(2,1)}, u32[]{:S(2)}, u32[]{:S(2)}) %collective-permute-start.4) | collective-permute-done | bytes 524320 | tf_op jit(solution)/shard_map/ppermute | solution.py:160
  91.1 2.1 collective-permute-done.10
  93.4 9.9 %copy.81.refs_2_ = bf16[1024,3375]{1,0:T(8,128)(2,1)} copy(bf16[1024,3375]{0,1:T(8,128)(2,1)} %param.31) | data formatting | bytes 13824000 | tf_op args[15]
  106.7 2.3 constant_dynamic-slice_fusion.3
  109.0 2.5 copy.77
  111.5 2.6 collective-permute-start.13
  120.9 2.1 fusion.12
  129.1 5.1 %copy.84 = bf16[4,1024,384]{2,1,0:T(8,128)(2,1)} copy(bf16[4,1024,384]{1,2,0:T(8,128)(2,1)} %bitcast.78) | data formatting | bytes 6291456 | tf_op jit(solution)/shard_map/transpose | solution.py:343
  138.7 2.5 fusion.2
  143.1 2.9 collective-permute-done.18
  146.3 4.3 collective-permute-done.19
  150.5 2.8 collective-permute-start.20
  158.2 2.2 convert_add_fusion
  162.7 6.9 %collective-permute-done.14 = bf16[256,1024]{0,1:T(8,128)(2,1)} collective-permute-done((bf16[256,1024]{0,1:T(8,128)(2,1)}, bf16[256,1024]{0,1:T(8,128)(2,1)}, u32[]{:S(2)}, u32[]{:S(2)}) %collective-permute-start.14) | collective-permute-done | bytes 524320 | tf_op jit(solution)/shard_map/ppermute | solution.py:160
  175.2 5.6 %collective-permute-done.5 = bf16[256,1024]{0,1:T(8,128)(2,1)} collective-permute-done((bf16[256,1024]{0,1:T(8,128)(2,1)}, bf16[256,1024]{0,1:T(8,128)(2,1)}, u32[]{:S(2)}, u32[]{:S(2)}) %collective-permute-start.5) | collective-permute-done | bytes 524320 | tf_op jit(solution)/shard_map/ppermute | solution.py:160
  182.3 11.1 %collective-permute-done.22 = bf16[1,1024,384]{2,1,0:T(8,128)(2,1)} collective-permute-done((bf16[1,1024,384]{2,1,0:T(8,128)(2,1)}, bf16[1,1024,384]{2,1,0:T(8,128)(2,1)}, u32[]{:S(2)}, u32[]{:S(2)}) %collective-permute-start.22) | collective-permute-done | bytes 786464 | tf_op jit(solution)/shard_map/ppermute | solution.py:160
  197.4 2.6 broadcast_select_fusion.1
  200.0 2.6 collective-permute-done.23
  203.2 15.9 %divide_convert_fusion = bf16[1024,3375]{1,0:T(8,128)(2,1)} fusion(bf16[1024,3375]{1,0:T(8,128)(2,1)S(1)} %bitcast.77, bf16[1024,3375]{0,1:T(8,128)(2,1)} %param.22, f32[1024]{0:T(1024)S(1)} %convert_divide_fusion, bf16[512,1024]{0,1:T(8,128)(2,1)} %get-tuple-element.84, bf16[512,1024]{0,1:T(8,128)(2,1)S(1)} %get-tuple-element.83), kind=kOutput, calls=%fused_computation | convolution fusion | flops 7102818304 | bytes 22837248 | tf_op jit(solution)/shard_map/dot_general | solution.py:152
  222.2 3.5 collective-permute-done.25
  227.9 12.7 %convolution_convert_fusion = bf16[1024,3375]{0,1:T(8,128)(2,1)} fusion(bf16[1024,3375]{0,1:T(8,128)(2,1)} %param.28, bf16[512,1024]{0,1:T(8,128)(2,1)S(1)} %get-tuple-element.86, bf16[512,1024]{0,1:T(8,128)(2,1)S(1)} %get-tuple-element.85), kind=kOutput, calls=%fused_computation.3 | convolution fusion | flops 7085538304 | bytes 15921152 | tf_op jit(solution)/shard_map/dot_general | solution.py:152
  244.6 179.6 %pair_sums.1 = (f32[128,3375]{1,0:T(8,128)}, f32[128,3375]{1,0:T(8,128)}) custom-call(bf16[1024,1024]{1,0:T(8,128)(2,1)} %fusion.1.refs_0_, bf16[1024,1024]{1,0:T(8,128)(2,1)} %fusion.refs_1_, bf16[1024,3375]{1,0:T(8,128)(2,1)} %copy.81.refs_2_, bf16[1024,3375]{1,0:T(8,128)(2,1)} %copy-done), custom_call_target="tpu_custom_call" | custom-call | tf_op jit(solution)/shard_map/pair_sums/pallas_call | solution.py:135
  424.2 2.8 copy.87
  428.7 10.2 %copy.86 = bf16[1024,3375]{0,1:T(8,128)(2,1)} copy(bf16[1024,3375]{1,0:T(8,128)(2,1)} %divide_convert_fusion) | data formatting | bytes 13824000
  (216 shorter events, 81.5 us)
Async XLA Ops:
  3.2 26.3 %collective-permute-start = (f32[6]{0:T(128)S(1)}, f32[6]{0:T(128)S(1)}, u32[]{:S(2)}, u32[]{:S(2)}) collective-permute-start(f32[6]{0:T(128)S(1)} %pad_maximum_fusion.28), channel_id=1, source_target_pairs={{0,4},{4,0},{8,12},{12,8},{16,20},{20,16},{24,28},{28,24},{1,5},{5... | collective-permute-start | bytes 80 | tf_op jit(solution)/shard_map/ppermute | solution.py:160
  19.2 19.1 %copy-start.29 = (s32[1024]{0:T(1024)S(1)}, s32[1024]{0:T(1024)}, u32[]{:S(2)}) copy-start(s32[1024]{0:T(1024)} %param.17) | copy-start | bytes 12292
  19.2 40.9 %collective-permute-start.7 = (bf16[512,1024]{1,0:T(8,128)(2,1)}, bf16[512,1024]{1,0:T(8,128)(2,1)S(1)}, u32[]{:S(2)}, u32[]{:S(2)}) collective-permute-start(bf16[512,1024]{1,0:T(8,128)(2,1)} %dynamic-slice_bitcast_fusion.1), channel_id=1, source_target_pairs={{0,1},{1,0},{2,3},{3,2},{4,5},{5,4},{6,7},{7,6},{8,9},{9,8},{10,11... | collective-permute-start | bytes 3145736 | tf_op jit(solution)/shard_map/ppermute | solution.py:160
  29.6 3.6 collective-permute-start.1
  33.1 4.5 %collective-permute-start.2 = (f32[6]{0:T(128)S(1)}, f32[6]{0:T(128)S(1)}, u32[]{:S(2)}, u32[]{:S(2)}) collective-permute-start(f32[6]{0:T(128)S(1)} %add.242), channel_id=1, source_target_pairs={{0,16},{4,20},{8,24},{12,28},{16,0},{20,4},{24,8},{28,12},{1,17},{... | collective-permute-start | bytes 80 | tf_op jit(solution)/shard_map/ppermute | solution.py:160
  60.2 3.0 collective-permute-start.3
  66.8 15.1 %collective-permute-start.4 = (bf16[256,1024]{0,1:T(8,128)(2,1)}, bf16[256,1024]{0,1:T(8,128)(2,1)}, u32[]{:S(2)}, u32[]{:S(2)}) collective-permute-start(bf16[256,1024]{0,1:T(8,128)(2,1)} %bitcast.58), channel_id=1, source_target_pairs={{0,2},{1,3},{2,0},{3,1},{4,6},{5,7},{6,4},{7,5},{8,10},{9,11},{10,... | collective-permute-start | bytes 1572872 | tf_op jit(solution)/shard_map/ppermute | solution.py:160
  70.7 43.4 %collective-permute-start.8 = (bf16[256,1024]{0,1:T(8,128)(2,1)}, bf16[256,1024]{0,1:T(8,128)(2,1)}, u32[]{:S(2)}, u32[]{:S(2)}) collective-permute-start(bf16[256,1024]{0,1:T(8,128)(2,1)} %bitcast.57), channel_id=1, source_target_pairs={{0,2},{1,3},{2,0},{3,1},{4,6},{5,7},{6,4},{7,5},{8,10},{9,11},{10,... | collective-permute-start | bytes 1572872 | tf_op jit(solution)/shard_map/ppermute | solution.py:160
  88.4 1.2 collective-permute-start.9
  89.6 3.6 collective-permute-start.10
  93.2 11.5 %collective-permute-start.11 = (f32[512]{0:T(512)S(1)}, f32[512]{0:T(512)S(1)}, u32[]{:S(2)}, u32[]{:S(2)}) collective-permute-start(f32[512]{0:T(512)S(1)} %add.269), channel_id=1, source_target_pairs={{0,4},{4,0},{8,12},{12,8},{16,20},{20,16},{24,28},{28,24},{1,5},{5... | collective-permute-start | bytes 6152 | tf_op jit(solution)/shard_map/ppermute | solution.py:160
  104.7 6.8 %collective-permute-start.12 = (f32[512]{0:T(512)S(1)}, f32[512]{0:T(512)S(1)}, u32[]{:S(2)}, u32[]{:S(2)}) collective-permute-start(f32[512]{0:T(512)S(1)} %add.270), channel_id=1, source_target_pairs={{0,8},{4,12},{8,0},{12,4},{16,24},{20,28},{24,16},{28,20},{1,9},{5... | collective-permute-start | bytes 6152 | tf_op jit(solution)/shard_map/ppermute | solution.py:160
  111.5 4.5 %collective-permute-start.13 = (f32[512]{0:T(512)S(1)}, f32[512]{0:T(512)S(1)}, u32[]{:S(2)}, u32[]{:S(2)}) collective-permute-start(f32[512]{0:T(512)S(1)} %add.271), channel_id=1, source_target_pairs={{0,16},{4,20},{8,24},{12,28},{16,0},{20,4},{24,8},{28,12},{1,17},{... | collective-permute-start | bytes 6152 | tf_op jit(solution)/shard_map/ppermute | solution.py:160
  134.9 2.2 collective-permute-start.16
  136.5 21.6 %collective-permute-start.21 = (bf16[2,1024,384]{2,1,0:T(8,128)(2,1)S(1)}, bf16[2,1024,384]{2,1,0:T(8,128)(2,1)}, u32[]{:S(2)}, u32[]{:S(2)}) collective-permute-start(bf16[2,1024,384]{2,1,0:T(8,128)(2,1)S(1)} %dynamic-slice_bitcast_fusion), channel_id=1, source_target_pairs={{0,1},{1,0},{2,3},{3,2},{4,5},{5,4},{6,7},{7,6},{8,9},{9,8},{10,11... | collective-permute-start | bytes 4718600 | tf_op jit(solution)/shard_map/ppermute | solution.py:160
  137.1 4.5 %collective-permute-start.17 = (f32[152,128]{1,0:T(8,128)S(1)}, f32[152,128]{1,0:T(8,128)S(1)}, u32[]{:S(2)}, u32[]{:S(2)}) collective-permute-start(f32[152,128]{1,0:T(8,128)S(1)} %add.280), channel_id=1, source_target_pairs={{0,2},{1,3},{2,0},{3,1},{4,6},{5,7},{6,4},{7,5},{8,10},{9,11},{10,... | collective-permute-start | bytes 233480 | tf_op jit(solution)/shard_map/ppermute | solution.py:160
  141.6 4.5 %collective-permute-start.18 = (f32[152,128]{1,0:T(8,128)S(1)}, f32[152,128]{1,0:T(8,128)S(1)}, u32[]{:S(2)}, u32[]{:S(2)}) collective-permute-start(f32[152,128]{1,0:T(8,128)S(1)} %add.281), channel_id=1, source_target_pairs={{0,4},{4,0},{8,12},{12,8},{16,20},{20,16},{24,28},{28,24},{1,5},{5... | collective-permute-start | bytes 233480 | tf_op jit(solution)/shard_map/ppermute | solution.py:160
  146.1 4.5 %collective-permute-start.19 = (f32[152,128]{1,0:T(8,128)S(1)}, f32[152,128]{1,0:T(8,128)S(1)}, u32[]{:S(2)}, u32[]{:S(2)}) collective-permute-start(f32[152,128]{1,0:T(8,128)S(1)} %add.282), channel_id=1, source_target_pairs={{0,8},{4,12},{8,0},{12,4},{16,24},{20,28},{24,16},{28,20},{1,9},{5... | collective-permute-start | bytes 233480 | tf_op jit(solution)/shard_map/ppermute | solution.py:160
  150.5 6.6 %collective-permute-start.20 = (f32[152,128]{1,0:T(8,128)S(1)}, f32[152,128]{1,0:T(8,128)S(1)}, u32[]{:S(2)}, u32[]{:S(2)}) collective-permute-start(f32[152,128]{1,0:T(8,128)S(1)} %add.283), channel_id=1, source_target_pairs={{0,16},{4,20},{8,24},{12,28},{16,0},{20,4},{24,8},{28,12},{1,17},{... | collective-permute-start | bytes 233480 | tf_op jit(solution)/shard_map/ppermute | solution.py:160
  154.5 15.1 %collective-permute-start.14 = (bf16[256,1024]{0,1:T(8,128)(2,1)}, bf16[256,1024]{0,1:T(8,128)(2,1)}, u32[]{:S(2)}, u32[]{:S(2)}) collective-permute-start(bf16[256,1024]{0,1:T(8,128)(2,1)} %multiply_convert_fusion), channel_id=1, source_target_pairs={{0,2},{1,3},{2,0},{3,1},{4,6},{5,7},{6,4},{7,5},{8,10},{9,11},{10,... | collective-permute-start | bytes 1572872 | tf_op jit(solution)/shard_map/ppermute | solution.py:160
  155.8 25.0 %collective-permute-start.5 = (bf16[256,1024]{0,1:T(8,128)(2,1)}, bf16[256,1024]{0,1:T(8,128)(2,1)}, u32[]{:S(2)}, u32[]{:S(2)}) collective-permute-start(bf16[256,1024]{0,1:T(8,128)(2,1)} %fusion.2), channel_id=1, source_target_pairs={{0,2},{1,3},{2,0},{3,1},{4,6},{5,7},{6,4},{7,5},{8,10},{9,11},{10,... | collective-permute-start | bytes 1572872 | tf_op jit(solution)/shard_map/ppermute | solution.py:160
  161.3 32.0 %collective-permute-start.22 = (bf16[1,1024,384]{2,1,0:T(8,128)(2,1)}, bf16[1,1024,384]{2,1,0:T(8,128)(2,1)}, u32[]{:S(2)}, u32[]{:S(2)}) collective-permute-start(bf16[1,1024,384]{2,1,0:T(8,128)(2,1)} %dynamic-slice_convert_fusion), channel_id=1, source_target_pairs={{0,2},{1,3},{2,0},{3,1},{4,6},{5,7},{6,4},{7,5},{8,10},{9,11},{10,... | collective-permute-start | bytes 2359304 | tf_op jit(solution)/shard_map/ppermute | solution.py:160
  172.7 24.6 %collective-permute-start.15 = (bf16[512,1024]{0,1:T(8,128)(2,1)}, bf16[512,1024]{0,1:T(8,128)(2,1)}, u32[]{:S(2)}, u32[]{:S(2)}) collective-permute-start(bf16[512,1024]{0,1:T(8,128)(2,1)} %pad_maximum_fusion.10), channel_id=1, source_target_pairs={{0,1},{1,0},{2,3},{3,2},{4,5},{5,4},{6,7},{7,6},{8,9},{9,8},{10,11... | collective-permute-start | bytes 3145736 | tf_op jit(solution)/shard_map/ppermute | solution.py:160
  180.8 22.4 %slice-start = ((s8[7077888]{0:T(1024)(128)(4,1)}), s8[4194304]{0:T(1024)(128)(4,1)S(1)}, s32[]{:S(2)}) async-start(s8[7077888]{0:T(1024)(128)(4,1)} %bitcast.76), calls=%async_computation | async-start | bytes 8388608
  194.8 7.8 %collective-permute-start.23 = (bf16[4,128,384]{2,1,0:T(8,128)(2,1)S(1)}, bf16[4,128,384]{2,1,0:T(8,128)(2,1)S(1)}, u32[]{:S(2)}, u32[]{:S(2)}) collective-permute-start(bf16[4,128,384]{2,1,0:T(8,128)(2,1)S(1)} %pad_maximum_fusion.14), channel_id=1, source_target_pairs={{0,4},{4,0},{8,12},{12,8},{16,20},{20,16},{24,28},{28,24},{1,5},{5... | collective-permute-start | bytes 1179656 | tf_op jit(solution)/shard_map/ppermute | solution.py:160
  197.4 23.2 %collective-permute-start.6 = (bf16[512,1024]{0,1:T(8,128)(2,1)}, bf16[512,1024]{0,1:T(8,128)(2,1)}, u32[]{:S(2)}, u32[]{:S(2)}) collective-permute-start(bf16[512,1024]{0,1:T(8,128)(2,1)} %pad_maximum_fusion.8), channel_id=1, source_target_pairs={{0,1},{1,0},{2,3},{3,2},{4,5},{5,4},{6,7},{7,6},{8,9},{9,8},{10,11... | collective-permute-start | bytes 3145736 | tf_op jit(solution)/shard_map/ppermute | solution.py:160
  202.7 16.4 %collective-permute-start.24 = (bf16[2,128,384]{2,1,0:T(8,128)(2,1)S(1)}, bf16[2,128,384]{2,1,0:T(8,128)(2,1)}, u32[]{:S(2)}, u32[]{:S(2)}) collective-permute-start(bf16[2,128,384]{2,1,0:T(8,128)(2,1)S(1)} %pad_maximum_fusion.15), channel_id=1, source_target_pairs={{0,8},{4,12},{8,0},{12,4},{16,24},{20,28},{24,16},{28,20},{1,9},{5... | collective-permute-start | bytes 589832 | tf_op jit(solution)/shard_map/ppermute | solution.py:160
  203.2 17.3 %copy-start.5 = (bf16[256,1024]{0,1:T(8,128)(2,1)S(1)}, bf16[256,1024]{0,1:T(8,128)(2,1)}, u32[]{:S(2)}) copy-start(bf16[256,1024]{0,1:T(8,128)(2,1)} %copy-done.4) | copy-start | bytes 1572868
  203.2 17.3 %copy-start.7 = (bf16[256,1024]{0,1:T(8,128)(2,1)S(1)}, bf16[256,1024]{0,1:T(8,128)(2,1)}, u32[]{:S(2)}) copy-start(bf16[256,1024]{0,1:T(8,128)(2,1)} %copy-done.6) | copy-start | bytes 1572868
  220.2 5.6 %collective-permute-start.25 = (bf16[1,128,384]{2,1,0:T(8,128)(2,1)S(1)}, bf16[1,128,384]{2,1,0:T(8,128)(2,1)S(1)}, u32[]{:S(2)}, u32[]{:S(2)}) collective-permute-start(bf16[1,128,384]{2,1,0:T(8,128)(2,1)S(1)} %add_convert_fusion.1), channel_id=1, source_target_pairs={{0,16},{4,20},{8,24},{12,28},{16,0},{20,4},{24,8},{28,12},{1,17},{... | collective-permute-start | bytes 294920 | tf_op jit(solution)/shard_map/ppermute | solution.py:160
  226.8 13.8 %collective-permute-start.26 = (bf16[1,128,384]{2,1,0:T(8,128)(2,1)S(1)}, bf16[1,128,384]{2,1,0:T(8,128)(2,1)S(1)}, u32[]{:S(2)}, u32[]{:S(2)}) collective-permute-start(bf16[1,128,384]{2,1,0:T(8,128)(2,1)S(1)} %add_convert_fusion), channel_id=1, source_target_pairs={{0,2},{1,3},{2,0},{3,1},{4,6},{5,7},{6,4},{7,5},{8,10},{9,11},{10,... | collective-permute-start | bytes 294920 | tf_op jit(solution)/shard_map/ppermute | solution.py:160
  241.3 197.6 %collective-permute-start.27 = (bf16[2,128,384]{2,1,0:T(8,128)(2,1)}, bf16[2,128,384]{2,1,0:T(8,128)(2,1)}, u32[]{:S(2)}, u32[]{:S(2)}) collective-permute-start(bf16[2,128,384]{2,1,0:T(8,128)(2,1)} %pad_maximum_fusion.16), channel_id=1, source_target_pairs={{0,1},{1,0},{2,3},{3,2},{4,5},{5,4},{6,7},{7,6},{8,9},{9,8},{10,11... | collective-permute-start | bytes 589832 | tf_op jit(solution)/shard_map/ppermute | solution.py:160
  (29 other events, 197.0 us)

commit v3 on v1

--- a/solution.py
+++ b/solution.py
@@ -1,6 +1,10 @@
+import functools
+
 import jax
 import jax.numpy as jnp
 from jax import lax
+from jax.experimental import pallas as pl
+from jax.experimental.pallas import tpu as pltpu
 from jax.sharding import PartitionSpec as P
 
 WARM = 1000
@@ -10,6 +14,227 @@
 F32 = jnp.float32
 
 
+MESH = pl.DeviceIdType.MESH
+
+
+def bits_of(n):
+    return n.bit_length() - 1
+
+
+def bit_of(at, k):
+    return lax.rem(lax.div(at, 1 << k), 2)
+
+
+def xor_of(at, nbits, value):
+    out = 0
+    for k in range(nbits):
+        bit = bit_of(at, k)
+        out = out + (1 - bit if (value >> k) & 1 else bit) * (1 << k)
+    return out
+
+
+def reversed_bits(i, n):
+    out = 0
+    for k in range(n):
+        out = out * 2 + ((i >> k) & 1)
+    return out
+
+
+def weight_kernel(cfg, *refs):
+    ncell, nch, ch, ahead, inplace = cfg
+    nb = bits_of(ncell)
+    take = iter(refs)
+    og_ref, ct_ref, dw_ref, ew_ref, scale_ref, xm_hbm, xe_hbm, pm_hbm, pe_hbm = [next(take) for _ in range(9)]
+    decoded_ref, cgrad_ref, dsum_ref, esum_ref = [next(take) for _ in range(4)]
+    xm, xe, pm, pe, keep = [next(take) for _ in range(5)]
+    recvs = [next(take) for _ in range(nb)]
+    sends = {k: next(take) for k in range(nb) if k not in inplace}
+    lsem, ssem, rsem = [next(take) for _ in range(3)]
+    model = xm.shape[1]
+    step = model // ncell
+    half = model // 2
+    at = lax.axis_index("cells")
+    peers = [xor_of(at, nb, 1 << k) for k in range(nb)]
+    s = pl.program_id(0)
+    slots = keep.shape[0]
+
+    def loads():
+        out = [pltpu.make_async_copy(xm_hbm, xm, lsem.at[0]), pltpu.make_async_copy(xe_hbm, xe, lsem.at[1])]
+        for t, (src, dst) in enumerate(((pm_hbm, pm), (pe_hbm, pe))):
+            if step % 128:
+                out.append(pltpu.make_async_copy(src, dst, lsem.at[2 + t]))
+            else:
+                for i in range(ncell):
+                    block = xor_of(at, nb, reversed_bits(i, nb))
+                    out.append(
+                        pltpu.make_async_copy(
+                            src.at[:, pl.ds(pl.multiple_of(block * step, step), step)],
+                            dst.at[:, pl.ds(i * step, step)],
+                            lsem.at[2 + t + 2 * i],
+                        )
+                    )
+        return out
+
+    def source(i, k):
+        h = model >> (k + 1)
+        if k in inplace:
+            return recvs[k - 1].at[i, :, pl.ds(h, h)]
+        return sends[k].at[i]
+
+    def copy(i, k):
+        return pltpu.make_async_remote_copy(
+            src_ref=source(i, k),
+            dst_ref=recvs[k].at[i],
+            send_sem=ssem.at[k, i],
+            recv_sem=rsem.at[k, i],
+            device_id={"cells": peers[k]},
+            device_id_type=MESH,
+        )
+
+    @pl.when(s == 0)
+    def _():
+        for cp in loads():
+            cp.start()
+        barrier = pltpu.get_barrier_semaphore()
+        for p in peers:
+            pl.semaphore_signal(barrier, inc=1, device_id={"cells": p}, device_id_type=MESH)
+        for cp in loads():
+            cp.wait()
+        pl.semaphore_wait(barrier, nb)
+
+    def out_parts(i, g, p_ref):
+        sends[0][i] = jnp.dot(g, p_ref[:, half:], preferred_element_type=F32).astype(BF)
+        copy(i, 0).start()
+        keep[lax.rem(i, slots)] = jnp.dot(g, p_ref[:, :half], preferred_element_type=F32)
+
+    @pl.when(s < nch)
+    def _():
+        out_parts(s, og_ref[...], pm)
+        decoded_ref[...] = lax.dot_general(
+            dw_ref[...], xm[...], (((1,), (1,)), ((), ())), preferred_element_type=F32
+        ).astype(BF)
+
+    @pl.when((s >= nch) & (s < 2 * nch))
+    def _():
+        scale = scale_ref[...]
+        z = 1.0 + ct_ref[...].astype(F32) * scale
+        out_parts(s, jnp.log(z).astype(BF), pe)
+        grad = lax.dot_general(
+            ew_ref[...], xe[...], (((1,), (1,)), ((), ())), preferred_element_type=F32
+        )
+        z = 1.0 + ct_ref[...].astype(F32) * scale
+        cgrad_ref[...] = (grad * scale / z).astype(BF)
+
+    for k in range(1, nb + 1):
+        i = s - ahead - (k - 1)
+
+        @pl.when((i >= 0) & (i < 2 * nch))
+        def _(i=i, k=k):
+            copy(i, k - 1).wait_recv()
+            slot = lax.rem(i, slots)
+            if k < nb:
+                h = model >> (k + 1)
+                lo, hi = h, 2 * h
+            else:
+                lo, hi = 0, step
+            v = keep[slot, :, lo:hi]
+            for j in range(k):
+                v = v + recvs[j][i, :, lo:hi].astype(F32)
+            if k < nb:
+                if k in inplace:
+                    recvs[k - 1][i, :, lo:hi] = v.astype(BF)
+                else:
+                    sends[k][i] = v.astype(BF)
+                copy(i, k).start()
+            else:
+
+                @pl.when(i < nch)
+                def _():
+                    dsum_ref[...] = v
+
+                @pl.when(i >= nch)
+                def _():
+                    esum_ref[...] = v
+
+    @pl.when(s == pl.num_programs(0) - 1)
+    def _():
+        def body(i, _):
+            for k in range(nb):
+                copy(i, k).wait_send()
+            return 0
+
+        lax.fori_loop(0, 2 * nch, body, 0)
+
+
+def weight_step(mixed, embed, og_t, counts_t, dec_t, emb_t, scale, ncell):
+    width, rows = og_t.shape
+    model = mixed.shape[1]
+    nb = bits_of(ncell)
+    step = model // ncell
+    ch = 384
+    nch = -(-width // ch)
+    ahead = 3
+    inplace = tuple(k for k in range(1, nb) if (model >> (k + 1)) % 128 == 0)
+    n = 2 * nch
+    if step % 128:
+        order = jnp.array([reversed_bits(i, nb) for i in range(ncell)], jnp.int32)
+        blocks = lax.axis_index("cells") ^ order
+        mixed_p, embed_p = [
+            jnp.take(x.reshape(rows, ncell, step), blocks, axis=1).reshape(rows, model)
+            for x in (mixed, embed)
+        ]
+    else:
+        mixed_p, embed_p = mixed, embed
+    last = nch - 1
+    first = lambda s: (jnp.minimum(s, last), 0)
+    second = lambda s: (jnp.clip(s - nch, 0, last), 0)
+    lag = ahead + nb - 1
+    big = lambda f: pl.BlockSpec((ch, rows), f)
+    anyv = pl.BlockSpec(memory_space=pl.ANY)
+    cfg = (ncell, nch, ch, ahead, inplace)
+    outs = pl.pallas_call(
+        functools.partial(weight_kernel, cfg),
+        grid=(n + lag,),
+        out_shape=[
+            jax.ShapeDtypeStruct((width, rows), BF),
+            jax.ShapeDtypeStruct((width, rows), BF),
+            jax.ShapeDtypeStruct((width, step), F32),
+            jax.ShapeDtypeStruct((width, step), F32),
+        ],
+        in_specs=[
+            big(first),
+            big(second),
+            pl.BlockSpec((ch, model), first),
+            pl.BlockSpec((ch, model), second),
+            pl.BlockSpec((1, rows), lambda s: (0, 0)),
+            anyv,
+            anyv,
+            anyv,
+            anyv,
+        ],
+        out_specs=[
+            big(first),
+            big(second),
+            pl.BlockSpec((ch, step), lambda s: (jnp.clip(s - lag, 0, last), 0)),
+            pl.BlockSpec((ch, step), lambda s: (jnp.clip(s - lag - nch, 0, last), 0)),
+        ],
+        scratch_shapes=[pltpu.VMEM((rows, model), BF)] * 4
+        + [pltpu.VMEM((lag + 2, ch, model // 2), F32)]
+        + [pltpu.VMEM((n, ch, model >> (k + 1)), BF) for k in range(nb)]
+        + [pltpu.VMEM((n, ch, model >> (k + 1)), BF) for k in range(nb) if k not in inplace]
+        + [
+            pltpu.SemaphoreType.DMA((2 + 2 * ncell,)),
+            pltpu.SemaphoreType.DMA((nb, n)),
+            pltpu.SemaphoreType.DMA((nb, n)),
+        ],
+        compiler_params=pltpu.CompilerParams(
+            collective_id=0, has_side_effects=True, vmem_limit_bytes=67043328
+        ),
+        name="weight_step",
+    )(og_t, counts_t, dec_t, emb_t, scale, mixed, embed, mixed_p, embed_p)
+    return outs
+
+
 def edot(left, right, dims=((1,), (0,))):
     return lax.dot_general(
         left, right, (dims, ((), ())), precision=lax.Precision.HIGHEST, preferred_element_type=F32
@@ -18,10 +243,6 @@
 
 def hdot(left, right, dims=((1,), (0,))):
     return lax.dot_general(left, right, (dims, ((), ())), preferred_element_type=F32)
-
-
-def bits_of(n):
-    return n.bit_length() - 1
 
 
 def flip(x, axis, size, mask):
@@ -59,31 +280,6 @@
     for k in range(bits_of(size)):
         block = block * 2 + ((at >> k) & 1)
     return block
-
-
-def halving(blocks, right, axis, size, order):
-    live = list(range(size))
-    arrived = {r: [] for r in live}
-    for k in order:
-        sent = [r for r in live if (r >> k) & 1]
-        live = [r for r in live if not (r >> k) & 1]
-        part = hdot(jnp.concatenate([blocks[r] for r in sent], 1), right, ((0,), (0,)))
-        for got in range(len(arrived[sent[0]])):
-            part = part + jnp.concatenate([arrived[r][got] for r in sent], 0).astype(F32)
-        came = flip(part.astype(BF), axis, size, 1 << k)
-        width = blocks[0].shape[1]
-        for i, r in enumerate(sent):
-            arrived[r ^ (1 << k)].append(came[i * width : (i + 1) * width])
-    total = hdot(blocks[0], right, ((0,), (0,)))
-    for part in arrived[0]:
-        total = total + part.astype(F32)
-    return total
-
-
-def cut(width, parts):
-    step = -(-width // (parts * 128)) * 128
-    edges = list(range(0, width, step)) + [width]
-    return list(zip(edges[:-1], edges[1:]))
 
 
 def on_device(
@@ -159,27 +355,7 @@
     mixed = gather_rows(mixed_mine, "genes", ngene, gene_at)
 
     step = model // ncell
-
-    def blocks_of(x):
-        return [
-            lax.dynamic_slice_in_dim(x, (cell_at ^ r) * step, step, 1) for r in range(ncell)
-        ]
-
-    nbits = bits_of(ncell)
-    straight = list(range(nbits))
-    turned = [1, 0] + straight[2:] if nbits > 1 else straight
-    pieces = cut(width, 4)
-
-    def weight_sum(x, right):
-        blocks = blocks_of(x)
-        outs = []
-        for i, (lo, hi) in enumerate(pieces):
-            order = turned if i == 0 else straight
-            outs.append(halving(blocks, right[:, lo:hi], "cells", ncell, order))
-        return jnp.concatenate(outs, 1)
-
-    dec_out = weight_sum(mixed, out_grad)
-    decoded = hdot(mixed, dec_weight).astype(BF)
+    straight = list(range(bits_of(ncell)))
 
     moment = variance + lat_mean * lat_mean
     square = lat_mean * lat_mean
@@ -245,9 +421,19 @@
     ).astype(BF)
     embed_grad = gather_rows(embed_mine, "genes", ngene, gene_at)
 
-    emb_out = weight_sum(embed_grad, normed)
-    normed_grad = hdot(embed_grad, emb_weight)
-    counts_grad = (normed_grad * scale[:, None] / (1.0 + counts_f * scale[:, None])).astype(BF)
+    decoded, counts_grad, dec_out, emb_out = [
+        x.T
+        for x in weight_step(
+            mixed,
+            embed_grad,
+            out_grad.T,
+            counts.T,
+            dec_weight.T,
+            emb_weight.T,
+            scale[None, :],
+            ncell,
+        )
+    ]
 
     latw_part = hdot(hidden_low, latent_grad, ((0,), (0,)))
     small = jnp.concatenate([latw_part, up_part], 1).astype(BF)

time: 449 us -> 377 us (0.84); the launches traced: 441 us -> 376 us
  Pallas kernels: 0 us -> 178 us
  waiting for transfers between devices: 176 us -> 49.4 us
  matrix products: 113 us -> 37 us
  starting transfers between devices: 61.6 us -> 38.3 us
  local copies, waits for them, and re-layouts: 51.6 us -> 40.5 us
    pallas_call x0 -> x1, Pallas kernels: none -> 178 us  [weight_step(): pl.pallas_call(functools.partial(weight_kernel, cfg), grid=(n + lag,), ou...]
    ppermute x52 -> x28, waiting for transfers between devices: 176 us -> 49.4 us  [flip(): return lax.ppermute(x, axis, [(i, i ^ mask) for i in range(size)])]
    dot_general x42 -> x8, matrix products: 107 us -> 30 us  [hdot(): lax.dot_general(left, right, (dims, ((), ())), preferred_element_type=F32)]
    ppermute x52 -> x28, starting transfers between devices: 61.6 us -> 38.3 us  [flip(): return lax.ppermute(x, axis, [(i, i ^ mask) for i in range(size)])]
    slice x8 -> x0, local copies, waits for them, and re-layouts: 7.37 us -> none  [halving(): arrived[r ^ 1 << k].append(came[i * width:(i + 1) * width])]
    unnamed x152 -> x80, local copies, waits for them, and re-layouts: 26.8 us -> 21.1 us
    convert_element_type x1 -> x0, other arithmetic: 5.57 us -> none  [on_device(): normed = jnp.log(1.0 + counts_f * scale[:, None]).astype(BF)]
  transfers between devices with their start and end apart: 52 -> 28, of which waited for: 25 -> 16; matrix products, arithmetic and copies ran while one was open for 34% -> 13% of each run, Pallas kernels for 0% -> 47%
where the time goes in v3:
time: 377 us; the launch traced here: 376 us
  Pallas kernels  178 us (47%)
  waiting for transfers between devices  49.4 us (13%)
  local copies, waits for them, and re-layouts  40.5 us (11%)
  starting transfers between devices  38.3 us (10%)
  matrix products  37 us (10%)
  other arithmetic  28.7 us (8%)
  between operations  4.38 us (1%)
    pallas_call x1, Pallas kernels, weight_step(): pl.pallas_call(functools.partial(weight_kernel, cfg), grid=(n + lag,), ou...  178 us
    ppermute x28, waiting for transfers between devices, flip(): return lax.ppermute(x, axis, [(i, i ^ mask) for i in range(size)])  49.4 us
    ppermute x28, starting transfers between devices, flip(): return lax.ppermute(x, axis, [(i, i ^ mask) for i in range(size)])  38.3 us
    dot_general x8, matrix products, hdot(): lax.dot_general(left, right, (dims, ((), ())), preferred_element_type=F32)  30 us
    unnamed x80, local copies, waits for them, and re-layouts  21.1 us
  transfers between devices with their start and end apart: 28, of which 16 were waited for; matrix products, arithmetic and copies ran while one was open for 13% of the time, Pallas kernels for 47%

profile of v3, /device:TPU:0, one launch (start us, length us, event | category | flops | bytes accessed | tf_op | source)
XLA Modules:
  0.0 376.2 jit_solution(9858622112462540437)
XLA Ops:
  3.2 3.0 collective-permute-start
  7.8 2.1 collective-permute-start.1
  11.5 3.0 collective-permute-start.2
  17.5 12.2 %fusion.3 = bf16[1024,1024]{1,0:T(8,128)(2,1)S(1)} fusion(bf16[1024,3375]{0,1:T(8,128)(2,1)} %param.22, bf16[1024,3375]{0,1:T(8,128)(2,1)} %param.16, f32[1024]{0:T(1024)S(1)} %convert_divide_fusion), kind=kOutput, calls=%fused_computation.10 | convolution fusion | flops 7092760576 | bytes 15925248 | tf_op jit(solution)/shard_map/dot_general | solution.py:245
  30.9 8.2 %convolution_convert_fusion.1 = bf16[1024,1024]{1,0:T(8,128)(2,1)S(1)} fusion(bf16[1024,3375]{0,1:T(8,128)(2,1)S(1)} %copy-done.3, bf16[1024,3375]{0,1:T(8,128)(2,1)S(1)} %copy-done.4), kind=kOutput, calls=%fused_computation.12 | convolution fusion | flops 7078936576 | bytes 15921152 | tf_op jit(solution)/shard_map/dot_general | solution.py:245
  40.8 1.9 convert_add_fusion.2
  42.8 1.9 collective-permute-start.4
  46.4 11.3 %collective-permute-done.4 = bf16[256,1024]{1,0:T(8,128)(2,1)S(1)} collective-permute-done((bf16[256,1024]{1,0:T(8,128)(2,1)S(1)}, bf16[256,1024]{1,0:T(8,128)(2,1)S(1)}, u32[]{:S(2)}, u32[]{:S(2)}) %collective-permute-start.4) | collective-permute-done | bytes 524320 | tf_op jit(solution)/shard_map/ppermute | solution.py:249
  64.2 1.8 collective-permute-start.10
  66.0 2.2 collective-permute-done.10
  69.9 1.9 collective-permute-done.11
  75.4 2.8 collective-permute-start.13
  85.4 2.2 fusion.16
  87.7 2.6 multiply_reduce_fusion
  91.7 2.0 pad_maximum_fusion
  93.7 4.6 %copy.43 = bf16[4,1024,384]{2,1,0:T(8,128)(2,1)} copy(bf16[4,1024,384]{1,2,0:T(8,128)(2,1)} %bitcast.76) | data formatting | bytes 6291456 | tf_op jit(solution)/shard_map/transpose | solution.py:441
  98.3 2.7 dynamic-slice_bitcast_fusion
  104.8 1.8 collective-permute-start.17
  106.6 2.6 fusion.4
  109.5 1.8 collective-permute-start.18
  111.3 2.7 collective-permute-done.18
  114.0 1.9 collective-permute-start.19
  115.9 2.6 collective-permute-done.19
  118.5 2.9 collective-permute-start.20
  130.6 12.9 %collective-permute-done.22 = bf16[1,1024,384]{2,1,0:T(8,128)(2,1)} collective-permute-done((bf16[1,1024,384]{2,1,0:T(8,128)(2,1)}, bf16[1,1024,384]{2,1,0:T(8,128)(2,1)}, u32[]{:S(2)}, u32[]{:S(2)}) %collective-permute-start.22) | collective-permute-done | bytes 786464 | tf_op jit(solution)/shard_map/ppermute | solution.py:249
  146.4 4.8 %collective-permute-done.14 = bf16[256,1024]{1,0:T(8,128)(2,1)S(1)} collective-permute-done((bf16[256,1024]{1,0:T(8,128)(2,1)S(1)}, bf16[256,1024]{1,0:T(8,128)(2,1)S(1)}, u32[]{:S(2)}, u32[]{:S(2)}) %collective-permute-start.14) | collective-permute-done | bytes 524320 | tf_op jit(solution)/shard_map/ppermute | solution.py:249
  159.2 2.3 collective-permute-done.24
  163.0 2.6 collective-permute-start.25
  173.5 2.9 broadcast_select_fusion.1
  180.7 177.9 %weight_step.1 = (bf16[3375,1024]{1,0:T(8,128)(2,1)}, bf16[3375,1024]{1,0:T(8,128)(2,1)}, f32[3375,128]{1,0:T(8,128)}, f32[3375,128]{1,0:T(8,128)}) custom-call(bf16[3375,1024]{1,0:T(8,128)(2,1)} %bitcast.79, bf16[3375,1024]{1,0:T(8,128)(2,1)} %bitcast.80, bf16[3375,1024]{1,0:T(8,128)(2,1)} %bitcast.81, bf16[3375,1024]{1,0:T(8,128)(2,1)} %bitcast.82, ...), custom_call_target="tpu_custom_call" | custom-call | tf_op jit(solution)/shard_map/weight_step/pallas_call | solution.py:195
  362.0 6.8 %copy.58 = bf16[1024,3375]{0,1:T(8,128)(2,1)} copy(bf16[1024,3375]{0,1:T(8,128)(2,1)} %bitcast.86) | data formatting | bytes 13824000
  368.8 2.9 copy.59
  (207 shorter events, 76.1 us)
Async XLA Ops:
  3.2 4.5 %collective-permute-start = (f32[6]{0:T(128)S(1)}, f32[6]{0:T(128)S(1)}, u32[]{:S(2)}, u32[]{:S(2)}) collective-permute-start(f32[6]{0:T(128)S(1)} %pad_maximum_fusion.26), channel_id=1, source_target_pairs={{0,4},{4,0},{8,12},{12,8},{16,20},{20,16},{24,28},{28,24},{1,5},{5... | collective-permute-start | bytes 80 | tf_op jit(solution)/shard_map/ppermute | solution.py:249
  7.8 3.7 collective-permute-start.1
  11.5 4.6 %collective-permute-start.2 = (f32[6]{0:T(128)S(1)}, f32[6]{0:T(128)S(1)}, u32[]{:S(2)}, u32[]{:S(2)}) collective-permute-start(f32[6]{0:T(128)S(1)} %add.244), channel_id=1, source_target_pairs={{0,16},{4,20},{8,24},{12,28},{16,0},{20,4},{24,8},{28,12},{1,17},{... | collective-permute-start | bytes 80 | tf_op jit(solution)/shard_map/ppermute | solution.py:249
  30.9 9.9 %collective-permute-start.3 = (bf16[512,1024]{1,0:T(8,128)(2,1)}, bf16[512,1024]{1,0:T(8,128)(2,1)}, u32[]{:S(2)}, u32[]{:S(2)}) collective-permute-start(bf16[512,1024]{1,0:T(8,128)(2,1)} %dynamic-slice_bitcast_fusion.2), channel_id=1, source_target_pairs={{0,1},{1,0},{2,3},{3,2},{4,5},{5,4},{6,7},{7,6},{8,9},{9,8},{10,11... | collective-permute-start | bytes 3145736 | tf_op jit(solution)/shard_map/ppermute | solution.py:249
  40.2 4.6 %collective-permute-start.7 = (bf16[512,1024]{1,0:T(8,128)(2,1)}, bf16[512,1024]{1,0:T(8,128)(2,1)S(1)}, u32[]{:S(2)}, u32[]{:S(2)}) collective-permute-start(bf16[512,1024]{1,0:T(8,128)(2,1)} %dynamic-slice_bitcast_fusion.1), channel_id=1, source_target_pairs={{0,1},{1,0},{2,3},{3,2},{4,5},{5,4},{6,7},{7,6},{8,9},{9,8},{10,11... | collective-permute-start | bytes 3145736 | tf_op jit(solution)/shard_map/ppermute | solution.py:249
  42.8 14.9 %collective-permute-start.4 = (bf16[256,1024]{1,0:T(8,128)(2,1)S(1)}, bf16[256,1024]{1,0:T(8,128)(2,1)S(1)}, u32[]{:S(2)}, u32[]{:S(2)}) collective-permute-start(bf16[256,1024]{1,0:T(8,128)(2,1)S(1)} %fusion.14), channel_id=1, source_target_pairs={{0,2},{1,3},{2,0},{3,1},{4,6},{5,7},{6,4},{7,5},{8,10},{9,11},{10,... | collective-permute-start | bytes 1572872 | tf_op jit(solution)/shard_map/ppermute | solution.py:249
  46.2 32.0 %collective-permute-start.8 = (bf16[256,1024]{1,0:T(8,128)(2,1)}, bf16[256,1024]{1,0:T(8,128)(2,1)}, u32[]{:S(2)}, u32[]{:S(2)}) collective-permute-start(bf16[256,1024]{1,0:T(8,128)(2,1)} %fusion.15), channel_id=1, source_target_pairs={{0,2},{1,3},{2,0},{3,1},{4,6},{5,7},{6,4},{7,5},{8,10},{9,11},{10,... | collective-permute-start | bytes 1572872 | tf_op jit(solution)/shard_map/ppermute | solution.py:249
  58.2 32.1 %copy-start.23 = (f32[256]{0:T(256)}, f32[256]{0:T(256)S(1)}, u32[]{:S(2)}) copy-start(f32[256]{0:T(256)S(1)} %add_rsqrt_fusion) | copy-start | bytes 3076
  62.9 1.2 collective-permute-start.9
  64.2 4.0 %collective-permute-start.10 = (f32[512]{0:T(512)S(1)}, f32[512]{0:T(512)S(1)}, u32[]{:S(2)}, u32[]{:S(2)}) collective-permute-start(f32[512]{0:T(512)S(1)} %add.271), channel_id=1, source_target_pairs={{0,2},{1,3},{2,0},{3,1},{4,6},{5,7},{6,4},{7,5},{8,10},{9,11},{10,... | collective-permute-start | bytes 6152 | tf_op jit(solution)/shard_map/ppermute | solution.py:249
  68.2 3.6 collective-permute-start.11
  71.8 3.6 collective-permute-start.12
  75.4 4.5 %collective-permute-start.13 = (f32[512]{0:T(512)S(1)}, f32[512]{0:T(512)S(1)}, u32[]{:S(2)}, u32[]{:S(2)}) collective-permute-start(f32[512]{0:T(512)S(1)} %add.274), channel_id=1, source_target_pairs={{0,16},{4,20},{8,24},{12,28},{16,0},{20,4},{24,8},{28,12},{1,17},{... | collective-permute-start | bytes 6152 | tf_op jit(solution)/shard_map/ppermute | solution.py:249
  101.0 20.3 %collective-permute-start.21 = (bf16[2,1024,384]{2,1,0:T(8,128)(2,1)}, bf16[2,1024,384]{2,1,0:T(8,128)(2,1)S(1)}, u32[]{:S(2)}, u32[]{:S(2)}) collective-permute-start(bf16[2,1024,384]{2,1,0:T(8,128)(2,1)} %dynamic-slice_bitcast_fusion), channel_id=1, source_target_pairs={{0,1},{1,0},{2,3},{3,2},{4,5},{5,4},{6,7},{7,6},{8,9},{9,8},{10,11... | collective-permute-start | bytes 4718600 | tf_op jit(solution)/shard_map/ppermute | solution.py:249
  102.5 2.3 collective-permute-start.16
  103.1 18.3 %copy-start = (bf16[4,1024,384]{2,1,0:T(8,128)(2,1)S(1)}, bf16[4,1024,384]{2,1,0:T(8,128)(2,1)}, u32[]{:S(2)}) copy-start(bf16[4,1024,384]{2,1,0:T(8,128)(2,1)} %copy.43) | copy-start | bytes 9437188
  104.8 4.7 %collective-permute-start.17 = (f32[152,128]{1,0:T(8,128)S(1)}, f32[152,128]{1,0:T(8,128)S(1)}, u32[]{:S(2)}, u32[]{:S(2)}) collective-permute-start(f32[152,128]{1,0:T(8,128)S(1)} %add.283), channel_id=1, source_target_pairs={{0,2},{1,3},{2,0},{3,1},{4,6},{5,7},{6,4},{7,5},{8,10},{9,11},{10,... | collective-permute-start | bytes 233480 | tf_op jit(solution)/shard_map/ppermute | solution.py:249
  109.2 18.9 %collective-permute-start.5 = (bf16[256,1024]{1,0:T(8,128)(2,1)}, bf16[256,1024]{1,0:T(8,128)(2,1)}, u32[]{:S(2)}, u32[]{:S(2)}) collective-permute-start(bf16[256,1024]{1,0:T(8,128)(2,1)} %fusion.4), channel_id=1, source_target_pairs={{0,2},{1,3},{2,0},{3,1},{4,6},{5,7},{6,4},{7,5},{8,10},{9,11},{10,... | collective-permute-start | bytes 1572872 | tf_op jit(solution)/shard_map/ppermute | solution.py:249
  109.5 4.5 %collective-permute-start.18 = (f32[152,128]{1,0:T(8,128)S(1)}, f32[152,128]{1,0:T(8,128)S(1)}, u32[]{:S(2)}, u32[]{:S(2)}) collective-permute-start(f32[152,128]{1,0:T(8,128)S(1)} %add.284), channel_id=1, source_target_pairs={{0,4},{4,0},{8,12},{12,8},{16,20},{20,16},{24,28},{28,24},{1,5},{5... | collective-permute-start | bytes 233480 | tf_op jit(solution)/shard_map/ppermute | solution.py:249
  114.0 4.5 %collective-permute-start.19 = (f32[152,128]{1,0:T(8,128)S(1)}, f32[152,128]{1,0:T(8,128)S(1)}, u32[]{:S(2)}, u32[]{:S(2)}) collective-permute-start(f32[152,128]{1,0:T(8,128)S(1)} %add.285), channel_id=1, source_target_pairs={{0,8},{4,12},{8,0},{12,4},{16,24},{20,28},{24,16},{28,20},{1,9},{5... | collective-permute-start | bytes 233480 | tf_op jit(solution)/shard_map/ppermute | solution.py:249
  118.5 7.8 %collective-permute-start.20 = (f32[152,128]{1,0:T(8,128)S(1)}, f32[152,128]{1,0:T(8,128)S(1)}, u32[]{:S(2)}, u32[]{:S(2)}) collective-permute-start(f32[152,128]{1,0:T(8,128)S(1)} %add.286), channel_id=1, source_target_pairs={{0,16},{4,20},{8,24},{12,28},{16,0},{20,4},{24,8},{28,12},{1,17},{... | collective-permute-start | bytes 233480 | tf_op jit(solution)/shard_map/ppermute | solution.py:249
  122.7 20.7 %collective-permute-start.22 = (bf16[1,1024,384]{2,1,0:T(8,128)(2,1)}, bf16[1,1024,384]{2,1,0:T(8,128)(2,1)}, u32[]{:S(2)}, u32[]{:S(2)}) collective-permute-start(bf16[1,1024,384]{2,1,0:T(8,128)(2,1)} %dynamic-slice_convert_fusion), channel_id=1, source_target_pairs={{0,2},{1,3},{2,0},{3,1},{4,6},{5,7},{6,4},{7,5},{8,10},{9,11},{10,... | collective-permute-start | bytes 2359304 | tf_op jit(solution)/shard_map/ppermute | solution.py:249
  125.2 26.0 %collective-permute-start.14 = (bf16[256,1024]{1,0:T(8,128)(2,1)S(1)}, bf16[256,1024]{1,0:T(8,128)(2,1)S(1)}, u32[]{:S(2)}, u32[]{:S(2)}) collective-permute-start(bf16[256,1024]{1,0:T(8,128)(2,1)S(1)} %multiply_convert_fusion), channel_id=1, source_target_pairs={{0,2},{1,3},{2,0},{3,1},{4,6},{5,7},{6,4},{7,5},{8,10},{9,11},{10,... | collective-permute-start | bytes 1572872 | tf_op jit(solution)/shard_map/ppermute | solution.py:249
  128.1 15.3 %copy-start.2 = (f32[2,1024,384]{2,1,0:T(8,128)S(1)}, f32[2,1024,384]{2,1,0:T(8,128)}, u32[]{:S(2)}) copy-start(f32[2,1024,384]{2,1,0:T(8,128)} %copy-done.1) | copy-start | bytes 9437188
  130.5 42.9 %collective-permute-start.6 = (bf16[512,1024]{1,0:T(8,128)(2,1)}, bf16[512,1024]{1,0:T(8,128)(2,1)}, u32[]{:S(2)}, u32[]{:S(2)}) collective-permute-start(bf16[512,1024]{1,0:T(8,128)(2,1)} %pad_maximum_fusion.6), channel_id=1, source_target_pairs={{0,1},{1,0},{2,3},{3,2},{4,5},{5,4},{6,7},{7,6},{8,9},{9,8},{10,11... | collective-permute-start | bytes 3145736 | tf_op jit(solution)/shard_map/ppermute | solution.py:249
  130.6 20.6 %copy-start.10 = (bf16[256,1024]{1,0:T(8,128)(2,1)S(1)}, bf16[256,1024]{1,0:T(8,128)(2,1)}, u32[]{:S(2)}) copy-start(bf16[256,1024]{1,0:T(8,128)(2,1)} %copy-done.9) | copy-start | bytes 1572868
  144.8 8.3 %collective-permute-start.23 = (bf16[4,128,384]{2,1,0:T(8,128)(2,1)S(1)}, bf16[4,128,384]{2,1,0:T(8,128)(2,1)S(1)}, u32[]{:S(2)}, u32[]{:S(2)}) collective-permute-start(bf16[4,128,384]{2,1,0:T(8,128)(2,1)S(1)} %pad_maximum_fusion.12), channel_id=1, source_target_pairs={{0,4},{4,0},{8,12},{12,8},{16,20},{20,16},{24,28},{28,24},{1,5},{5... | collective-permute-start | bytes 1179656 | tf_op jit(solution)/shard_map/ppermute | solution.py:249
  153.1 20.4 %collective-permute-start.15 = (bf16[512,1024]{1,0:T(8,128)(2,1)}, bf16[512,1024]{1,0:T(8,128)(2,1)}, u32[]{:S(2)}, u32[]{:S(2)}) collective-permute-start(bf16[512,1024]{1,0:T(8,128)(2,1)} %pad_maximum_fusion.8), channel_id=1, source_target_pairs={{0,1},{1,0},{2,3},{3,2},{4,5},{5,4},{6,7},{7,6},{8,9},{9,8},{10,11... | collective-permute-start | bytes 3145736 | tf_op jit(solution)/shard_map/ppermute | solution.py:249
  153.8 7.6 %collective-permute-start.24 = (bf16[2,128,384]{2,1,0:T(8,128)(2,1)}, bf16[2,128,384]{2,1,0:T(8,128)(2,1)}, u32[]{:S(2)}, u32[]{:S(2)}) collective-permute-start(bf16[2,128,384]{2,1,0:T(8,128)(2,1)} %pad_maximum_fusion.13), channel_id=1, source_target_pairs={{0,8},{4,12},{8,0},{12,4},{16,24},{20,28},{24,16},{28,20},{1,9},{5... | collective-permute-start | bytes 589832 | tf_op jit(solution)/shard_map/ppermute | solution.py:249
  163.0 7.7 %collective-permute-start.25 = (bf16[1,128,384]{2,1,0:T(8,128)(2,1)}, bf16[1,128,384]{2,1,0:T(8,128)(2,1)}, u32[]{:S(2)}, u32[]{:S(2)}) collective-permute-start(bf16[1,128,384]{2,1,0:T(8,128)(2,1)} %add_convert_fusion.1), channel_id=1, source_target_pairs={{0,16},{4,20},{8,24},{12,28},{16,0},{20,4},{24,8},{28,12},{1,17},{... | collective-permute-start | bytes 294920 | tf_op jit(solution)/shard_map/ppermute | solution.py:249
  171.7 4.7 %collective-permute-start.26 = (bf16[1,128,384]{2,1,0:T(8,128)(2,1)S(1)}, bf16[1,128,384]{2,1,0:T(8,128)(2,1)S(1)}, u32[]{:S(2)}, u32[]{:S(2)}) collective-permute-start(bf16[1,128,384]{2,1,0:T(8,128)(2,1)S(1)} %add_convert_fusion), channel_id=1, source_target_pairs={{0,2},{1,3},{2,0},{3,1},{4,6},{5,7},{6,4},{7,5},{8,10},{9,11},{10,... | collective-permute-start | bytes 294920 | tf_op jit(solution)/shard_map/ppermute | solution.py:249
  177.8 180.9 %collective-permute-start.27 = (bf16[2,128,384]{2,1,0:T(8,128)(2,1)}, bf16[2,128,384]{2,1,0:T(8,128)(2,1)}, u32[]{:S(2)}, u32[]{:S(2)}) collective-permute-start(bf16[2,128,384]{2,1,0:T(8,128)(2,1)} %pad_maximum_fusion.14), channel_id=1, source_target_pairs={{0,1},{1,0},{2,3},{3,2},{4,5},{5,4},{6,7},{7,6},{8,9},{9,8},{10,11... | collective-permute-start | bytes 589832 | tf_op jit(solution)/shard_map/ppermute | solution.py:249
  (30 other events, 194.5 us)

commit v4 on v3

v4 whole, which is shorter than its diff:
```python
import functools

import jax
import jax.numpy as jnp
from jax import lax
from jax.experimental import pallas as pl
from jax.experimental.pallas import tpu as pltpu
from jax.sharding import PartitionSpec as P

WARM = 1000
EPS = 1e-05
FREE = 1.0
BF = jnp.bfloat16
F32 = jnp.float32


MESH = pl.DeviceIdType.MESH


def bits_of(n):
    return n.bit_length() - 1


def bit_of(at, k):
    return lax.rem(lax.div(at, 1 << k), 2)


def xor_of(at, nbits, value):
    out = 0
    for k in range(nbits):
        bit = bit_of(at, k)
        out = out + (1 - bit if (value >> k) & 1 else bit) * (1 << k)
    return out


def reversed_bits(i, n):
    out = 0
    for k in range(n):
        out = out * 2 + ((i >> k) & 1)
    return out


def fdot(left, right, dims):
    return lax.dot_general(
        left, right, (dims, ((), ())), precision=lax.Precision.HIGHEST, preferred_element_type=F32
    )


def bdot(left, right, dims):
    return lax.dot_general(left, right, (dims, ((), ())), preferred_element_type=F32)


NN, NT, TN = ((1,), (0,)), ((1,), (1,)), ((0,), (0,))
AHEAD = 3


def main_kernel(cfg, *refs):
    ncell, nch, ch, inplace = cfg
    nb = bits_of(ncell)
    take = iter(refs)

    def some(count):
        return [next(take) for _ in range(count)]

    og_ref, ct_ref, dw_ref, ew_ref, scale_ref = some(5)
    emb_hbm, mg_hbm, noise_hbm, latw_hbm, upw_hbm = some(5)
    rowd_ref, const_ref, gain_ref, bias_ref, latb_ref, pmean_ref, plogv_ref = some(7)
    decoded_ref, cgrad_ref, dsum_ref, esum_ref, small_ref, vec_ref = some(6)
    xm, xe, px, keep = some(4)
    recvs = some(nb)
    sends = {k: next(take) for k in range(nb) if k not in inplace}
    normal, mg, noise, latw, upw, hlow, lmean, lvar, sample, lgrad, resp_s, inv_s, kpart = some(13)
    klbuf, vecbuf, sm_keep, sm_s1, sm_r1, sm_s2, sm_r2 = some(7)
    sm_sc, sm_rc = some(nb), some(nb)
    fin = next(take)
    lsem, ssem, rsem, asend, arecv = some(5)

    rows, model = xm.shape
    mine = rows // 4
    lat = model // 2
    step = model // ncell
    half = model // 2
    at = lax.axis_index("cells")
    gene = lax.axis_index("genes")
    core, wye = bit_of(gene, 0), bit_of(gene, 1)
    home = core * 2 + wye
    peers = [{"cells": xor_of(at, nb, 1 << k)} for k in range(nb)]
    gpeers = [{"genes": xor_of(gene, 2, 1)}, {"genes": xor_of(gene, 2, 2)}]
    allpeers = gpeers + peers
    nall = nb + 2
    s = pl.program_id(0)
    slots = keep.shape[0]

    def remote(src, dst, ssem_at, rsem_at, peer):
        return pltpu.make_async_remote_copy(
            src_ref=src,
            dst_ref=dst,
            send_sem=ssem_at,
            recv_sem=rsem_at,
            device_id=peer,
            device_id_type=MESH,
        )

    def source(i, k):
        h = model >> (k + 1)
        if k in inplace:
            return recvs[k - 1].at[i, :, pl.ds(h, h)]
        return sends[k].at[lax.rem(i, sends[k].shape[0])]

    def copy(i, k):
        return remote(source(i, k), recvs[k].at[i], ssem.at[k, i], rsem.at[k, i], peers[k])

    def free(i, k):
        ring = sends[k].shape[0]

        @pl.when(i >= ring)
        def _():
            copy(i - ring, k).wait_send()

    side = {}

    def add_side(name, src, dst, peer):
        side[name] = (len(side), src, dst, peer)

    def rowblock(ref, b):
        return ref.at[pl.ds(pl.multiple_of(b * mine, mine), mine)]

    for name, ref in (("m", xm), ("e", xe)):
        add_side(name + "core", rowblock(ref, home), rowblock(ref, home), gpeers[0])
        add_side(name + "wye", rowblock(ref, home), rowblock(ref, home), gpeers[1])
        other = core * 2 + (1 - wye)
        add_side(name + "pass", rowblock(ref, other), rowblock(ref, other), gpeers[0])
    for r in range(nall):
        add_side(f"k{r}", klbuf.at[r], klbuf.at[nall + r], allpeers[r])
        add_side(f"v{r}", vecbuf.at[r], vecbuf.at[nall + r], allpeers[r])
    add_side("s1", sm_s1, sm_r1, gpeers[0])
    add_side("s2", sm_s2, sm_r2, gpeers[1])
    for k in range(nb):
        add_side(f"c{k}", sm_sc[k], sm_rc[k], peers[k])
    add_side("f0", fin.at[home], fin.at[home], gpeers[1])
    add_side("f1", fin.at[pl.ds(core * 2, 2)], fin.at[pl.ds(core * 2, 2)], gpeers[0])

    def side_copy(name):
        at_sem, src, dst, peer = side[name]
        return remote(src, dst, asend.at[at_sem], arecv.at[at_sem], peer)

    def start(name):
        side_copy(name).start()

    def got(name):
        side_copy(name).wait_recv()

    def permute(x, sem_at):
        if step % 128 == 0:
            cps = []
            for i in range(ncell):
                block = xor_of(at, nb, reversed_bits(i, nb))
                cps.append(
                    pltpu.make_async_copy(
                        x.at[:, pl.ds(pl.multiple_of(block * step, step), step)],
                        px.at[:, pl.ds(i * step, step)],
                        lsem.at[sem_at + i],
                    )
                )
            for cp in cps:
                cp.start()
            for cp in cps:
                cp.wait()
        else:
            row = lax.broadcasted_iota(jnp.int32, (model, 128), 0)

            def part(j, _):
                col = lax.broadcasted_iota(jnp.int32, (model, 128), 1) + j * 128
                block = col // step
                target = col % step
                for k in range(nb):
                    flag = (block // (1 << (nb - 1 - k))) % 2
                    own = bit_of(at, k)
                    target = target + (flag + own - 2 * flag * own) * ((1 << k) * step)
                pick = (row == target).astype(F32).astype(BF)
                px[:, pl.ds(pl.multiple_of(j * 128, 128), 128)] = jnp.dot(
                    x[...], pick, preferred_element_type=F32
                ).astype(BF)
                return 0

            lax.fori_loop(0, model // 128, part, 0)

    def tables():
        prec = jnp.exp(-plogv_ref[...])
        mprec = pmean_ref[...] * prec
        return prec, mprec, pmean_ref[...] * mprec + plogv_ref[...]

    def loads():
        pairs = ((emb_hbm, normal), (latw_hbm, latw), (upw_hbm, upw), (mg_hbm, mg), (noise_hbm, noise))
        return [pltpu.make_async_copy(a, b, lsem.at[i]) for i, (a, b) in enumerate(pairs)]

    @pl.when(s == 0)
    def _():
        for cp in loads():
            cp.start()
        barrier = pltpu.get_barrier_semaphore()
        for p in allpeers:
            pl.semaphore_signal(barrier, inc=1, device_id=p, device_id_type=MESH)
        for cp in loads():
            cp.wait()
        e = normal[...]
        centred = e - jnp.mean(e, -1, keepdims=True)
        inv = lax.rsqrt(jnp.mean(centred * centred, -1, keepdims=True) + EPS)
        nrm = centred * inv
        normal[...] = nrm
        inv_s[...] = inv
        hidden = nrm * gain_ref[...] + bias_ref[...]
        hlow[...] = hidden.astype(BF)
        latent = bdot(hlow[...], latw[...], NN) + latb_ref[...]
        lm, lv = latent[:, :lat], latent[:, lat:]
        lmean[...] = lm
        lvar[...] = lv
        sample[...] = (lm + jnp.exp(0.5 * lv) * noise[...].astype(F32)).astype(BF)
        mixed = normal[...] * gain_ref[...] + bias_ref[...] + bdot(sample[...], upw[...], NT)
        xm[pl.ds(pl.multiple_of(home * mine, mine), mine), :] = mixed.astype(BF)
        pl.semaphore_wait(barrier, nall)
        start("mwye")
        start("mcore")
        prec, mprec, ctab = tables()
        lm, lv = lmean[...], lvar[...]
        csum = fdot(jnp.ones((8, lat), F32), ctab, NT)[0:1]
        logits = -0.5 * (fdot(lm * lm, prec, NT) - 2.0 * fdot(lm, mprec, NT) + csum)
        logits = logits * lat ** (-0.5)
        top = jnp.exp(logits - jnp.max(logits, -1, keepdims=True))
        resp = top / jnp.sum(top, -1, keepdims=True)
        resp_s[...] = resp
        moment = jnp.exp(lv) + lm * lm
        diverge = 0.5 * (
            fdot(resp, ctab, NN)
            - lv
            + moment * fdot(resp, prec, NN)
            - 2.0 * lm * fdot(resp, mprec, NN)
            - 1.0
        )
        klbuf[0] = jnp.sum(diverge * rowd_ref[:, 0:1], 0, keepdims=True)
        start("k0")
        got("mwye")
        start("mpass")
        got("mcore")
        got("mpass")
        permute(xm, 0)

    def out_parts(i, g):
        free(i, 0)
        sends[0][lax.rem(i, sends[0].shape[0])] = jnp.dot(
            g, px[:, half:], preferred_element_type=F32
        ).astype(BF)
        copy(i, 0).start()
        keep[lax.rem(i, slots)] = jnp.dot(g, px[:, :half], preferred_element_type=F32)

    @pl.when(s < nch)
    def _():
        out_parts(s, og_ref[...])
        decoded_ref[...] = bdot(dw_ref[...], xm[...], NT).astype(BF)

    @pl.when((s >= nch) & (s < 2 * nch))
    def _():
        scale = scale_ref[...]
        z = 1.0 + ct_ref[...].astype(F32) * scale
        out_parts(s, jnp.log(z).astype(BF))
        grad = bdot(ew_ref[...], xe[...], NT)
        z = 1.0 + ct_ref[...].astype(F32) * scale
        cgrad_ref[...] = (grad * scale / z).astype(BF)

    for k in range(1, nb + 1):
        i = s - AHEAD - (k - 1)

        @pl.when((i >= 0) & (i < 2 * nch))
        def _(i=i, k=k):
            copy(i, k - 1).wait_recv()
            slot = lax.rem(i, slots)
            if k < nb:
                h = model >> (k + 1)
                lo, hi = h, 2 * h
            else:
                lo, hi = 0, step
            v = keep[slot, :, lo:hi]
            for j in range(k):
                v = v + recvs[j][i, :, lo:hi].astype(F32)
            if k < nb:
                if k in inplace:
                    recvs[k - 1][i, :, lo:hi] = v.astype(BF)
                else:
                    free(i, k)
                    sends[k][lax.rem(i, sends[k].shape[0])] = v.astype(BF)
                copy(i, k).start()
            else:

                @pl.when(i < nch)
                def _():
                    dsum_ref[...] = v

                @pl.when(i >= nch)
                def _():
                    esum_ref[...] = v

    plan = {}

    def at_step(step_no):
        def put(fn):
            plan.setdefault(step_no, []).append(fn)
            return fn

        return put

    per = -(-nall // 4)
    for r in range(nall):

        @at_step(1 + r // per)
        def _(r=r):
            got(f"k{r}")
            v = klbuf[r] + klbuf[nall + r]
            if r + 1 < nall:
                klbuf[r + 1] = v
                start(f"k{r + 1}")
            else:
                kpart[...] = v

    back = 2 + (nall - 1) // per

    @at_step(back)
    def _():
        prec, mprec, ctab = tables()
        lm, lv = lmean[...], lvar[...]
        average = kpart[...] / const_ref[0:1]
        loss = const_ref[1:2] * jnp.sum(jnp.maximum(average, FREE), -1, keepdims=True)
        active = (average > FREE).astype(F32)
        weight = rowd_ref[:, 1:2] * active
        resp = resp_s[...]
        rprec = fdot(resp, prec, NN)
        rmean = fdot(resp, mprec, NN)
        variance = jnp.exp(lv)
        moment = variance + lm * lm
        wmom, wmean = weight * moment, weight * lm
        rgrad = 0.5 * (
            fdot(weight, ctab, NT) + fdot(wmom, prec, NT) - 2.0 * fdot(wmean, mprec, NT)
        )
        logit = resp * (rgrad - jnp.sum(resp * rgrad, -1, keepdims=True)) * lat ** (-0.5)
        sgrad = bdot(mg[...], upw[...], NN)
        mgrad = (
            sgrad
            + weight * (lm * rprec - rmean)
            - lm * fdot(logit, prec, NN)
            + fdot(logit, mprec, NN)
        )
        vgrad = sgrad * 0.5 * jnp.exp(0.5 * lv) * noise[...].astype(F32) + 0.5 * weight * (
            variance * rprec - 1.0
        )
        lgrad[:, :lat] = mgrad.astype(BF)
        lgrad[:, lat:] = vgrad.astype(BF)
        lcol = fdot(logit, jnp.ones((mine, 128), F32), TN)[:, 0:1]
        cg = 0.5 * fdot(resp, weight, TN) - 0.5 * lcol
        mpg = fdot(logit, lm, TN) - fdot(resp, wmean, TN)
        pmean = pmean_ref[...]
        pg = (
            0.5 * fdot(resp, wmom, TN)
            - 0.5 * fdot(logit, lm * lm, TN)
            + pmean * pmean * cg
            + pmean * mpg
        )
        nk = pmean.shape[0]
        vecbuf[0, 0:nk] = 2.0 * pmean * prec * cg + prec * mpg
        vecbuf[0, nk : 2 * nk] = cg - prec * pg
        base = 2 * nk
        vecbuf[0, base : base + 1] = loss * jnp.ones((1, lat), F32)
        lg = lgrad[...]
        lb = jnp.sum(lg.astype(F32), 0, keepdims=True)
        hgrad = mg[...].astype(F32) + bdot(lg, latw[...], NT)
        nrm = normal[...]
        gg = jnp.sum(hgrad * nrm, 0, keepdims=True)
        sg = jnp.sum(hgrad, 0, keepdims=True)
        for j, row in enumerate((gg, sg, lb)):
            for part in range(2):
                r = base + 1 + 2 * j + part
                vecbuf[0, r : r + 1] = row[:, part * lat : (part + 1) * lat]
        vecbuf[0, base + 7 : base + 8] = jnp.zeros((1, lat), F32)
        ng = hgrad * gain_ref[...]
        eg = inv_s[...] * (
            ng - jnp.mean(ng, -1, keepdims=True) - nrm * jnp.mean(ng * nrm, -1, keepdims=True)
        )
        xe[pl.ds(pl.multiple_of(home * mine, mine), mine), :] = eg.astype(BF)
        start("ewye")
        start("ecore")
        start("v0")

    @at_step(back + 1)
    def _():
        quarter = 3 * lat // 4

        def put(q, lo, hi, left, right):
            v = bdot(left, right, TN)

            @pl.when(core == q // 2)
            def _():
                sm_keep[q % 2, :, lo:hi] = v

            @pl.when(core != q // 2)
            def _():
                sm_s1[q % 2, :, lo:hi] = v.astype(BF)

        cut = 2 * lat - 2 * quarter
        put(0, 0, quarter, hlow[...], lgrad[:, :quarter])
        put(1, 0, quarter, hlow[...], lgrad[:, quarter : 2 * quarter])
        put(2, 0, cut, hlow[...], lgrad[:, 2 * quarter :])
        put(2, cut, quarter, mg[...], sample[:, : quarter - cut])
        put(3, 0, quarter, mg[...], sample[:, quarter - cut :])
        start("s1")
        got("ewye")
        start("epass")

    @at_step(nch - 1)
    def _():
        got("ecore")
        got("epass")
        permute(xe, ncell)

    assert back + 1 < nch - 1
    for r in range(nall):

        @at_step(back + 2 + r)
        def _(r=r):
            got(f"v{r}")
            v = vecbuf[r] + vecbuf[nall + r]
            if r + 1 < nall:
                vecbuf[r + 1] = v
                start(f"v{r + 1}")
            else:
                vec_ref[...] = v

    @at_step(back + 2)
    def _():
        got("s1")
        sm_keep[wye] = sm_keep[wye] + sm_r1[wye].astype(F32)
        sm_s2[...] = (sm_keep[1 - wye] + sm_r1[1 - wye].astype(F32)).astype(BF)
        start("s2")

    def span(k):
        base = 0
        for j in reversed(range(k + 1, nb)):
            base = base + bit_of(at, j) * (step << j)
        bit = bit_of(at, k)
        size = step << k
        return (
            pl.ds(pl.multiple_of(base + bit * size, step), size),
            pl.ds(pl.multiple_of(base + (1 - bit) * size, step), size),
        )

    @at_step(back + 3)
    def _():
        got("s2")
        sm_keep[wye] = sm_keep[wye] + sm_r2[...].astype(F32)
        sm_sc[nb - 1][...] = sm_keep[wye, span(nb - 1)[1], :].astype(BF)
        start(f"c{nb - 1}")

    for k in reversed(range(nb)):

        @at_step(back + 3 + nb - k)
        def _(k=k):
            got(f"c{k}")
            kept = span(k)[0]
            sm_keep[wye, kept, :] = sm_keep[wye, kept, :] + sm_rc[k][...].astype(F32)
            if k:
                sm_sc[k - 1][...] = sm_keep[wye, span(k - 1)[1], :].astype(BF)
                start(f"c{k - 1}")
            else:
                fin[home] = sm_keep[wye, kept, :].astype(BF)
                start("f0")

    @at_step(back + 4 + nb)
    def _():
        got("f0")
        start("f1")

    @at_step(back + 5 + nb)
    def _():
        got("f1")
        small_ref[...] = fin[...].astype(F32)

    for step_no in sorted(plan):

        @pl.when(s == step_no)
        def _(fns=plan[step_no]):
            for fn in fns:
                fn()

    @pl.when(s == pl.num_programs(0) - 1)
    def _():
        def body(i, _):
            for k in range(nb):
                if k in inplace:
                    copy(i, k).wait_send()
                else:

                    @pl.when(i >= 2 * nch - sends[k].shape[0])
                    def _(k=k):
                        copy(i, k).wait_send()

            return 0

        lax.fori_loop(0, 2 * nch, body, 0)
        for name in side:
            side_copy(name).wait_send()


def main_step(
    embedded, mixed_grad, noise, lat_w, up_w, rowd, const, gain, bias, lat_b, pmean_t, plogv_t,
    og_t, counts_t, dec_t, emb_t, scale, ncell
):
    width, rows = og_t.shape
    mine, model = embedded.shape
    lat = up_w.shape[1]
    nb = bits_of(ncell)
    nall = nb + 2
    step = model // ncell
    ch = 384 if step % 128 == 0 else 192
    nch = -(-width // ch)
    inplace = tuple(k for k in range(1, nb) if (model >> (k + 1)) % 128 == 0)
    n = 2 * nch
    last = nch - 1
    first = lambda s: (jnp.minimum(s, last), 0)
    second = lambda s: (jnp.clip(s - nch, 0, last), 0)
    fixed = lambda *shape: pl.BlockSpec(shape, lambda s: (0,) * len(shape))
    lag = AHEAD + nb - 1
    ring = AHEAD + 2
    quarter = 3 * lat // 4
    nk = pmean_t.shape[0]
    vec = 2 * nk + 8
    anyv = pl.BlockSpec(memory_space=pl.ANY)
    nside = 6 + 2 * nall + 2 + nb + 2
    vm = pltpu.VMEM
    return pl.pallas_call(
        functools.partial(main_kernel, (ncell, nch, ch, inplace)),
        grid=(n + lag,),
        out_shape=[
            jax.ShapeDtypeStruct((width, rows), BF),
            jax.ShapeDtypeStruct((width, rows), BF),
            jax.ShapeDtypeStruct((width, step), F32),
            jax.ShapeDtypeStruct((width, step), F32),
            jax.ShapeDtypeStruct((4, step, quarter), F32),
            jax.ShapeDtypeStruct((vec, lat), F32),
        ],
        in_specs=[
            pl.BlockSpec((ch, rows), first),
            pl.BlockSpec((ch, rows), second),
            pl.BlockSpec((ch, model), first),
            pl.BlockSpec((ch, model), second),
            fixed(1, rows),
            anyv,
            anyv,
            anyv,
            anyv,
            anyv,
            fixed(mine, 8),
            fixed(8, lat),
            fixed(1, model),
            fixed(1, model),
            fixed(1, model),
            fixed(nk, lat),
            fixed(nk, lat),
        ],
        out_specs=[
            pl.BlockSpec((ch, rows), first),
            pl.BlockSpec((ch, rows), second),
            pl.BlockSpec((ch, step), lambda s: (jnp.clip(s - lag, 0, last), 0)),
            pl.BlockSpec((ch, step), lambda s: (jnp.clip(s - lag - nch, 0, last), 0)),
            fixed(4, step, quarter),
            fixed(vec, lat),
        ],
        scratch_shapes=[vm((rows, model), BF)] * 3
        + [vm((lag + 2, ch, model // 2), F32)]
        + [vm((n, ch, model >> (k + 1)), BF) for k in range(nb)]
        + [vm((ring, ch, model >> (k + 1)), BF) for k in range(nb) if k not in inplace]
        + [
            vm((mine, model), F32),
            vm((mine, model), BF),
            vm((mine, lat), BF),
            vm((model, 2 * lat), BF),
            vm((model, lat), BF),
            vm((mine, model), BF),
            vm((mine, lat), F32),
            vm((mine, lat), F32),
            vm((mine, lat), BF),
            vm((mine, 2 * lat), BF),
            vm((mine, nk), F32),
            vm((mine, 1), F32),
            vm((1, lat), F32),
            vm((2 * nall, 1, lat), F32),
            vm((2 * nall, vec, lat), F32),
            vm((2, model, quarter), F32),
            vm((2, model, quarter), BF),
            vm((2, model, quarter), BF),
            vm((model, quarter), BF),
            vm((model, quarter), BF),
        ]
        + [vm((step << k, quarter), BF) for k in range(nb)] * 2
        + [
            vm((4, step, quarter), BF),
            pltpu.SemaphoreType.DMA((max(5, 2 * ncell),)),
            pltpu.SemaphoreType.DMA((nb, n)),
            pltpu.SemaphoreType.DMA((nb, n)),
            pltpu.SemaphoreType.DMA((nside,)),
            pltpu.SemaphoreType.DMA((nside,)),
        ],
        compiler_params=pltpu.CompilerParams(
            collective_id=0, has_side_effects=True, vmem_limit_bytes=67043328
        ),
        name="main_step",
    )(
        og_t, counts_t, dec_t, emb_t, scale, embedded, mixed_grad, noise, lat_w, up_w,
        rowd, const, gain, bias, lat_b, pmean_t, plogv_t,
    )


def hdot(left, right, dims=((1,), (0,))):
    return lax.dot_general(left, right, (dims, ((), ())), preferred_element_type=F32)


def flip(x, axis, size, mask):
    return lax.ppermute(x, axis, [(i, i ^ mask) for i in range(size)])


def butterfly(x, axis, size):
    for k in range(bits_of(size)):
        x = x + flip(x, axis, size, 1 << k)
    return x


def scatter_rows(x, axis, size, at):
    for k in range(bits_of(size)):
        bit = (at >> k) & 1
        halves = x.reshape((2, x.shape[0] // 2) + x.shape[1:])
        keep = lax.dynamic_index_in_dim(halves, bit, 0, keepdims=False)
        send = lax.dynamic_index_in_dim(halves, 1 - bit, 0, keepdims=False)
        x = keep.astype(F32) + flip(send.astype(BF), axis, size, 1 << k).astype(F32)
    return x


def place_of(at, size):
    block = 0
    for k in range(bits_of(size)):
        block = block * 2 + ((at >> k) & 1)
    return block


def on_device(
    counts,
    library,
    cell_mask,
    slide_len,
    kl_step,
    noise,
    emb_weight,
    ln_gain,
    ln_bias,
    lat_weight,
    lat_bias,
    up_weight,
    dec_weight,
    prior_mean,
    prior_logvar,
    out_grad,
    ncell,
    ngene,
):
    rows, width = counts.shape
    model = emb_weight.shape[0]
    latent_w = up_weight.shape[1]
    cell_at = lax.axis_index("cells")
    gene_at = lax.axis_index("genes")
    nslide = slide_len.shape[0]
    place = cell_at * rows + jnp.arange(rows, dtype=jnp.int32)
    ends = jnp.cumsum(slide_len)
    slide_of = jnp.sum((ends[None, :] <= place[:, None]).astype(jnp.int32), 1)
    onehot = (slide_of[:, None] == jnp.arange(nslide, dtype=jnp.int32)[None, :]).astype(F32)
    live = cell_mask.astype(F32)
    libsize = library.astype(F32)
    stats = jnp.concatenate(
        [jnp.sum(onehot * (libsize * live)[:, None], 0), jnp.sum(onehot * live[:, None], 0)]
    )
    stats = butterfly(stats, "cells", ncell)
    lib_total, live_total = stats[:nslide], stats[nslide:]
    slide_lib = lib_total / jnp.maximum(live_total, 1.0)
    scale = jnp.sum(onehot * slide_lib[None, :], 1) / libsize
    total = jnp.maximum(jnp.sum(live_total), 1.0)
    beta = jnp.minimum(1.0, kl_step[0].astype(F32) / WARM)

    partial_mixed = hdot(out_grad, dec_weight, ((1,), (1,))).astype(BF)
    mixed_grad = scatter_rows(partial_mixed, "genes", ngene, gene_at).astype(BF)

    counts_f = counts.astype(F32)
    normed = jnp.log(1.0 + counts_f * scale[:, None]).astype(BF)
    partial_embed = hdot(normed, emb_weight, ((1,), (1,))).astype(BF)
    embedded = scatter_rows(partial_embed, "genes", ngene, gene_at)

    mine = rows // ngene
    first = place_of(gene_at, ngene) * mine
    my_noise = lax.dynamic_slice_in_dim(noise, first, mine, 0)
    my_live = lax.dynamic_slice_in_dim(live, first, mine, 0)
    rowd = jnp.concatenate(
        [my_live[:, None], (beta * my_live / total)[:, None], jnp.zeros((mine, 6), F32)], 1
    )
    const = jnp.concatenate(
        [
            jnp.full((1, latent_w), 1.0) * total,
            jnp.full((1, latent_w), 1.0) * beta,
            jnp.zeros((6, latent_w), F32),
        ],
        0,
    )
    decoded, counts_grad, dec_out, emb_out, small, vec = main_step(
        embedded, mixed_grad, my_noise, lat_weight, up_weight, rowd, const,
        ln_gain[None, :], ln_bias[None, :], lat_bias[None, :], prior_mean.T, prior_logvar.T,
        out_grad.T, counts.T, dec_weight.T, emb_weight.T, scale[None, :], ncell,
    )
    decoded, counts_grad, dec_out, emb_out = decoded.T, counts_grad.T, dec_out.T, emb_out.T
    step = model // ncell
    small = small.transpose(1, 0, 2).reshape(step, 3 * latent_w)
    latw_out = small[:, : 2 * latent_w]
    up_out = small[:, 2 * latent_w :]
    nk = prior_mean.shape[1]

    def own(x, each, axis):
        return lax.dynamic_slice_in_dim(x, cell_at * each, each, axis)

    pmean_out = own(vec[:nk], latent_w // ncell, 1).T
    plogv_out = own(vec[nk : 2 * nk], latent_w // ncell, 1).T
    base = 2 * nk
    kl_loss = vec[base, :1] / (ncell * ngene)
    gain_out, shift_out, latb_out = [
        own(vec[base + 1 + 2 * j : base + 3 + 2 * j].reshape(model), step, 0) for j in range(3)
    ]
    return (
        decoded,
        counts_grad,
        emb_out,
        gain_out,
        shift_out,
        latw_out,
        latb_out,
        up_out,
        dec_out,
        pmean_out,
        plogv_out,
        kl_loss,
    )


def solution(mesh):
    ncell, ngene = mesh.shape["cells"], mesh.shape["genes"]

    def body(*args):
        return on_device(*args, ncell=ncell, ngene=ngene)

    return jax.shard_map(
        body,
        mesh=mesh,
        in_specs=(
            P("cells", "genes"),
            P("cells"),
            P("cells"),
            P(),
            P(),
            P("cells", None),
            P(None, "genes"),
            P(),
            P(),
            P(),
            P(),
            P(),
            P(None, "genes"),
            P(),
            P(),
            P("cells", "genes"),
        ),
        out_specs=(
            P("cells", "genes"),
            P("cells", "genes"),
            P("cells", "genes"),
            P("cells"),
            P("cells"),
            P("cells", None),
            P("cells"),
            P("cells", None),
            P("cells", "genes"),
            P("cells", None),
            P("cells", None),
            P(),
        ),
        check_vma=False,
    )
```

time: 377 us -> 306 us (0.81)
  Pallas kernels: 178 us -> 210 us
  starting transfers between devices: 38.3 us -> 9.3 us
  waiting for transfers between devices: 49.4 us -> 21.5 us
  other arithmetic: 28.7 us -> 10.6 us
  matrix products: 37 us -> 20.4 us
  local copies, waits for them, and re-layouts: 40.5 us -> 30.4 us
    pallas_call x1, Pallas kernels: 178 us -> 210 us  [main_step(): pl.pallas_call(functools.partial(main_kernel, (ncell, nch, ch, inplace)),...]
    ppermute x28 -> x7, starting transfers between devices: 38.3 us -> 9.3 us  [flip(): return lax.ppermute(x, axis, [(i, i ^ mask) for i in range(size)])]
    ppermute x28 -> x7, waiting for transfers between devices: 49.4 us -> 21.5 us  [flip(): return lax.ppermute(x, axis, [(i, i ^ mask) for i in range(size)])]
    dot_general x8 -> x2, matrix products: 30 us -> 20.4 us  [hdot(): lax.dot_general(left, right, (dims, ((), ())), preferred_element_type=F32)]
    concatenate x6 -> x2, other arithmetic: 7.73 us -> 0.15 us  [the longest x1 0.08 us: on_device(): jnp.concatenate([jnp.full((1, latent_w), 1.0) * total, jnp.full((1, laten...]
    dot_general x6 -> x0, matrix products: 7.01 us -> none  [edot(): lax.dot_general(left, right, (dims, ((), ())), precision=lax.Precision.HI...]
    select_n x5 -> x0, other arithmetic: 5.47 us -> none  [gather_rows(): first = jnp.where(bit == 0, x, other)]
    squeeze x3 -> x2, local copies, waits for them, and re-layouts: 4.91 us -> 1.11 us  [scatter_rows(): send = lax.dynamic_index_in_dim(halves, 1 - bit, 0, keepdims=False)]
  transfers between devices with their start and end apart: 28 -> 7, of which waited for: 16 -> 4; matrix products, arithmetic and copies ran while one was open for 13% -> 10% of each run, Pallas kernels for 47% -> 0%
where the time goes in v4:
time: 306 us
  Pallas kernels  210 us (69%)
  local copies, waits for them, and re-layouts  30.4 us (10%)
  waiting for transfers between devices  21.5 us (7%)
  matrix products  20.4 us (7%)
  other arithmetic  10.6 us (3%)
  starting transfers between devices  9.3 us (3%)
  between operations  4.02 us (1%)
    pallas_call x1, Pallas kernels, main_step(): pl.pallas_call(functools.partial(main_kernel, (ncell, nch, ch, inplace)),...  210 us
    ppermute x7, waiting for transfers between devices, flip(): return lax.ppermute(x, axis, [(i, i ^ mask) for i in range(size)])  21.5 us
    dot_general x2, matrix products, hdot(): lax.dot_general(left, right, (dims, ((), ())), preferred_element_type=F32)  20.4 us
    unnamed x32, local copies, waits for them, and re-layouts  19.4 us
    ppermute x7, starting transfers between devices, flip(): return lax.ppermute(x, axis, [(i, i ^ mask) for i in range(size)])  9.3 us
  transfers between devices with their start and end apart: 7, of which 4 were waited for; matrix products, arithmetic and copies ran while one was open for 10% of the time, Pallas kernels for 0%

profile of v4, /device:TPU:0, one launch (start us, length us, event | category | flops | bytes accessed | tf_op | source)
XLA Modules:
  0.0 305.8 jit_solution(4092663515110506973)
XLA Ops:
  2.0 0.8 reduce-window.8
  3.2 3.0 collective-permute-start
  6.2 12.2 %convolution_convert_fusion = bf16[1024,1024]{1,0:T(8,128)(2,1)S(1)} fusion(bf16[1024,3375]{0,1:T(8,128)(2,1)} %param.31, bf16[1024,3375]{0,1:T(8,128)(2,1)} %param.28), kind=kOutput, calls=%fused_computation.7 | convolution fusion | flops 7078936576 | bytes 15921152 | tf_op jit(solution)/shard_map/dot_general | solution.py:620
  18.4 1.3 copy-done.3
  19.9 1.6 collective-permute-start.1
  21.5 2.0 collective-permute-done.1
  23.5 2.6 collective-permute-start.2
  26.1 1.9 collective-permute-done.2
  28.8 8.2 %fusion.3 = bf16[1024,1024]{1,0:T(8,128)(2,1)S(1)} fusion(bf16[1024,3375]{0,1:T(8,128)(2,1)S(1)} %copy-done.1, bf16[1024,3375]{0,1:T(8,128)(2,1)S(1)} %copy-done, f32[1024]{0:T(1024)S(1)} %convert_divide_fusion), kind=kOutput, calls=%fused_computation.6 | convolution fusion | flops 7092760576 | bytes 15925248 | tf_op jit(solution)/shard_map/dot_general | solution.py:620
  37.0 1.3 copy-done.4
  38.3 1.0 dynamic-slice_bitcast_fusion.1
  40.0 1.7 constant_dynamic-slice_fusion.refs_7_
  42.4 1.6 convert_add_fusion
  44.1 1.6 collective-permute-start.6
  45.7 1.9 convert_add_fusion.1
  47.7 1.3 copy-done.2
  49.0 0.9 fusion.5
  50.5 0.8 copy.37.refs_10_
  51.3 7.7 %collective-permute-done.6 = bf16[256,1024]{1,0:T(8,128)(2,1)S(1)} collective-permute-done((bf16[256,1024]{1,0:T(8,128)(2,1)S(1)}, bf16[256,1024]{1,0:T(8,128)(2,1)S(1)}, u32[]{:S(2)}, u32[]{:S(2)}) %collective-permute-start.6) | collective-permute-done | bytes 524320 | tf_op jit(solution)/shard_map/ppermute | solution.py:624
  59.0 0.9 fusion.4.refs_6_
  59.9 9.9 %collective-permute-done.4 = bf16[256,1024]{1,0:T(8,128)(2,1)} collective-permute-done((bf16[256,1024]{1,0:T(8,128)(2,1)}, bf16[256,1024]{1,0:T(8,128)(2,1)}, u32[]{:S(2)}, u32[]{:S(2)}) %collective-permute-start.4) | collective-permute-done | bytes 524320 | tf_op jit(solution)/shard_map/ppermute | solution.py:624
  69.9 2.5 bitcast_add_fusion.1.refs_5_
  73.1 209.5 %main_step.1 = (bf16[3375,1024]{1,0:T(8,128)(2,1)}, bf16[3375,1024]{1,0:T(8,128)(2,1)}, f32[3375,128]{1,0:T(8,128)}, f32[3375,128]{1,0:T(8,128)}, f32[4,128,384]{2,1,0:T(8,128)}, /*index=5*/f32[40,512]{1,0:T(8,128)}) custom-call(bf16[3375,1024]{1,0:T(8,128)(2,1)} %bitcast.63, bf16[3375,1024]{1,0:T(8,128)(2,1)} %bitcast.64, bf16[3375,1024]{1,0:T(8,128)(2,1)} %bitcast.65, ...), custom_call_target="tpu_custom_call" | custom-call | tf_op jit(solution)/shard_map/main_step/pallas_call | solution.py:536
  282.6 1.4 copy.38
  284.1 0.8 slice_bitcast_fusion
  285.7 1.2 slice.39
  288.0 1.0 copy.39
  289.6 0.8 copy.40
  291.9 6.8 %copy.49 = bf16[1024,3375]{0,1:T(8,128)(2,1)} copy(bf16[1024,3375]{0,1:T(8,128)(2,1)} %bitcast.70) | data formatting | bytes 13824000
  298.7 3.5 %copy.50 = bf16[1024,3375]{0,1:T(8,128)(2,1)} copy(bf16[1024,3375]{0,1:T(8,128)(2,1)S(1)} %bitcast.69) | data formatting | bytes 13824000
  302.3 1.2 copy.51
  303.5 1.2 copy.52
  (55 shorter events, 7.5 us)
Async XLA Ops:
  3.2 16.6 %collective-permute-start = (f32[6]{0:T(128)S(1)}, f32[6]{0:T(128)S(1)}, u32[]{:S(2)}, u32[]{:S(2)}) collective-permute-start(f32[6]{0:T(128)S(1)} %pad_maximum_fusion), channel_id=1, source_target_pairs={{0,4},{4,0},{8,12},{12,8},{16,20},{20,16},{24,28},{28,24},{1,5},{5... | collective-permute-start | bytes 80 | tf_op jit(solution)/shard_map/ppermute | solution.py:624
  6.2 22.5 %copy-start.8 = (s32[1024]{0:T(1024)S(1)}, s32[1024]{0:T(1024)}, u32[]{:S(2)}) copy-start(s32[1024]{0:T(1024)} %param.17) | copy-start | bytes 12292
  6.2 22.6 %copy-start = (bf16[1024,3375]{0,1:T(8,128)(2,1)S(1)}, bf16[1024,3375]{0,1:T(8,128)(2,1)}, u32[]{:S(2)}) copy-start(bf16[1024,3375]{0,1:T(8,128)(2,1)} %param.16) | copy-start | bytes 20736004
  6.2 22.6 %copy-start.1 = (bf16[1024,3375]{0,1:T(8,128)(2,1)S(1)}, bf16[1024,3375]{0,1:T(8,128)(2,1)}, u32[]{:S(2)}) copy-start(bf16[1024,3375]{0,1:T(8,128)(2,1)} %param.22) | copy-start | bytes 20736004
  18.3 1.3 copy-start.3
  19.7 22.7 %collective-permute-start.5 = (bf16[512,1024]{1,0:T(8,128)(2,1)S(1)}, bf16[512,1024]{1,0:T(8,128)(2,1)S(1)}, u32[]{:S(2)}, u32[]{:S(2)}) collective-permute-start(bf16[512,1024]{1,0:T(8,128)(2,1)S(1)} %dynamic-slice_bitcast_fusion), channel_id=1, source_target_pairs={{0,1},{1,0},{2,3},{3,2},{4,5},{5,4},{6,7},{7,6},{8,9},{9,8},{10,11... | collective-permute-start | bytes 3145736 | tf_op jit(solution)/shard_map/ppermute | solution.py:624
  19.9 3.6 %collective-permute-start.1 = (f32[6]{0:T(128)S(1)}, f32[6]{0:T(128)S(1)}, u32[]{:S(2)}, u32[]{:S(2)}) collective-permute-start(f32[6]{0:T(128)S(1)} %fusion.12), channel_id=1, source_target_pairs={{0,8},{4,12},{8,0},{12,4},{16,24},{20,28},{24,16},{28,20},{1,9},{5... | collective-permute-start | bytes 80 | tf_op jit(solution)/shard_map/ppermute | solution.py:624
  23.5 4.5 %collective-permute-start.2 = (f32[6]{0:T(128)S(1)}, f32[6]{0:T(128)S(1)}, u32[]{:S(2)}, u32[]{:S(2)}) collective-permute-start(f32[6]{0:T(128)S(1)} %add.76), channel_id=1, source_target_pairs={{0,16},{4,20},{8,24},{12,28},{16,0},{20,4},{24,8},{28,12},{1,17},{... | collective-permute-start | bytes 80 | tf_op jit(solution)/shard_map/ppermute | solution.py:624
  28.7 8.2 %copy-start.7 = (f32[1024]{0:T(1024)}, f32[1024]{0:T(1024)S(1)}, u32[]{:S(2)}) copy-start(f32[1024]{0:T(1024)S(1)} %convert_divide_fusion) | copy-start | bytes 12292
  37.0 1.3 copy-start.4
  39.3 6.4 %collective-permute-start.3 = (bf16[512,1024]{1,0:T(8,128)(2,1)}, bf16[512,1024]{1,0:T(8,128)(2,1)}, u32[]{:S(2)}, u32[]{:S(2)}) collective-permute-start(bf16[512,1024]{1,0:T(8,128)(2,1)} %dynamic-slice_bitcast_fusion.1), channel_id=1, source_target_pairs={{0,1},{1,0},{2,3},{3,2},{4,5},{5,4},{6,7},{7,6},{8,9},{9,8},{10,11... | collective-permute-start | bytes 3145736 | tf_op jit(solution)/shard_map/ppermute | solution.py:624
  44.1 14.9 %collective-permute-start.6 = (bf16[256,1024]{1,0:T(8,128)(2,1)S(1)}, bf16[256,1024]{1,0:T(8,128)(2,1)S(1)}, u32[]{:S(2)}, u32[]{:S(2)}) collective-permute-start(bf16[256,1024]{1,0:T(8,128)(2,1)S(1)} %fusion.6), channel_id=1, source_target_pairs={{0,2},{1,3},{2,0},{3,1},{4,6},{5,7},{6,4},{7,5},{8,10},{9,11},{10,... | collective-permute-start | bytes 1572872 | tf_op jit(solution)/shard_map/ppermute | solution.py:624
  47.6 1.3 copy-start.2
  49.8 20.0 %collective-permute-start.4 = (bf16[256,1024]{1,0:T(8,128)(2,1)}, bf16[256,1024]{1,0:T(8,128)(2,1)}, u32[]{:S(2)}, u32[]{:S(2)}) collective-permute-start(bf16[256,1024]{1,0:T(8,128)(2,1)} %fusion.5), channel_id=1, source_target_pairs={{0,2},{1,3},{2,0},{3,1},{4,6},{5,7},{6,4},{7,5},{8,10},{9,11},{10,... | collective-permute-start | bytes 1572872 | tf_op jit(solution)/shard_map/ppermute | solution.py:624
  289.6 9.1 %slice-start = ((s8[6914048]{0:T(1024)(128)(4,1)}), s8[2719744]{0:T(1024)(128)(4,1)S(1)}, s32[]{:S(2)}) async-start(s8[6914048]{0:T(1024)(128)(4,1)} %bitcast.67), calls=%async_computation | async-start | bytes 5439488
  291.9 6.8 %slice-start.1 = ((s8[6914048]{0:T(1024)(128)(4,1)}), s8[4194304]{0:T(1024)(128)(4,1)S(1)}, s32[]{:S(2)}) async-start(s8[6914048]{0:T(1024)(128)(4,1)} %bitcast.67), calls=%async_computation.1 | async-start | bytes 8388608
  298.7 3.5 %copy-start.6 = (f32[3375,128]{1,0:T(8,128)S(1)}, f32[3375,128]{1,0:T(8,128)}, u32[]{:S(2)}) copy-start(f32[3375,128]{1,0:T(8,128)} %get-tuple-element.20) | copy-start | bytes 5184004
  298.7 4.7 %copy-start.5 = (f32[3375,128]{1,0:T(8,128)S(1)}, f32[3375,128]{1,0:T(8,128)}, u32[]{:S(2)}) copy-start(f32[3375,128]{1,0:T(8,128)} %get-tuple-element.23) | copy-start | bytes 5184004

commit v5 on v4

--- a/solution.py
+++ b/solution.py
@@ -54,6 +54,246 @@
 AHEAD = 3
 
 
+def front_kernel(cfg, *refs):
+    ncell, nslide, lat = cfg
+    nb = bits_of(ncell)
+    slen_ref, kls_ref, lib_ref, mask_ref, ct_hbm, og_hbm, et_hbm, dt_hbm = refs[:8]
+    emb_ref, mgk_ref, mgs_ref, scale_ref, const_ref, rowd_ref = refs[8:14]
+    ct, og, et, dt, low, msend, mrecv, esend, erecv, ysend, yrecv, stb, stv = refs[14:27]
+    lsem, asend, arecv = refs[27:]
+    rows = lib_ref.shape[1]
+    mine = rows // 4
+    top = stv.shape[0] // 2
+    at = lax.axis_index("cells")
+    gene = lax.axis_index("genes")
+    core, wye = bit_of(gene, 0), bit_of(gene, 1)
+    home = core * 2 + wye
+    peers = [{"cells": xor_of(at, nb, 1 << k)} for k in range(nb)]
+    gpeers = [{"genes": xor_of(gene, 2, 1)}, {"genes": xor_of(gene, 2, 2)}]
+    s = pl.program_id(0)
+
+    def block_of(j):
+        far, away = 1 - lax.rem(j, 2), 1 - lax.div(j, 2)
+        side = far * (1 - core) + (1 - far) * core
+        return side * 2 + away * (1 - wye) + (1 - away) * wye
+
+    def cols(j):
+        return pl.ds(pl.multiple_of(block_of(j) * mine, mine), mine)
+
+    def load(which, j):
+        src, dst = ((og_hbm, og), (ct_hbm, ct))[which]
+        return pltpu.make_async_copy(src.at[:, cols(j)], dst.at[j], lsem.at[2 + 4 * which + j])
+
+    def whole(which):
+        src, dst = ((dt_hbm, dt), (et_hbm, et))[which]
+        return pltpu.make_async_copy(src, dst, lsem.at[which])
+
+    def remote(src, dst, sem, peer):
+        return pltpu.make_async_remote_copy(
+            src_ref=src,
+            dst_ref=dst,
+            send_sem=asend.at[sem],
+            recv_sem=arecv.at[sem],
+            device_id=peer,
+            device_id_type=MESH,
+        )
+
+    def mcopy(h):
+        return remote(msend.at[h], mrecv.at[h], h, gpeers[0])
+
+    def ecopy(h):
+        return remote(esend.at[h], erecv.at[h], 2 + h, gpeers[0])
+
+    def ycopy():
+        return remote(ysend, yrecv, 4, gpeers[1])
+
+    def scopy(r):
+        return remote(stb.at[r], stb.at[nb + r], 5 + r, peers[r])
+
+    def slides():
+        place = at * rows + lax.broadcasted_iota(jnp.int32, (1, rows), 1)
+        begin = 0
+        for q in range(nslide):
+            end = begin + slen_ref[q]
+            yield q, ((place >= begin) & (place < end)).astype(F32)
+            begin = end
+
+    def round_done(r):
+        scopy(r).wait_recv()
+        v = stb[r] + stb[nb + r]
+        if r + 1 < nb:
+            stb[r + 1] = v
+            scopy(r + 1).start()
+        else:
+            stv[...] = v
+
+    @pl.when(s == 0)
+    def _():
+        barrier = pltpu.get_barrier_semaphore()
+        for p in peers + gpeers:
+            pl.semaphore_signal(barrier, inc=1, device_id=p, device_id_type=MESH)
+        whole(0).start()
+        load(0, 0).start()
+        load(0, 1).start()
+        whole(1).start()
+        for j in range(4):
+            load(1, j).start()
+        load(0, 2).start()
+        load(0, 3).start()
+        stb[0] = jnp.zeros_like(stv)
+        live = mask_ref[...].astype(F32)
+        libsize = lib_ref[...].astype(F32)
+        for q, row in slides():
+            stb[0, q : q + 1] = jnp.sum(row * (libsize * live), 1, keepdims=True) * jnp.ones(
+                (1, 128), F32
+            )
+            stb[0, top + q : top + q + 1] = jnp.sum(
+                row * live, 1, keepdims=True
+            ) * jnp.ones((1, 128), F32)
+        pl.semaphore_wait(barrier, nb + 2)
+        scopy(0).start()
+        whole(0).wait()
+
+    @pl.when(s == 1)
+    def _():
+        round_done(0)
+
+    @pl.when(s == 2)
+    def _():
+        for r in range(1, nb):
+            round_done(r)
+        whole(1).wait()
+        live = mask_ref[...].astype(F32)
+        total = jnp.zeros((1, 1), F32)
+        scale = jnp.zeros((1, rows), F32)
+        for q, row in slides():
+            count = stv[top + q : top + q + 1, 0:1]
+            scale = scale + row * (stv[q : q + 1, 0:1] / jnp.maximum(count, 1.0))
+            total = total + count
+        scale_ref[...] = scale / lib_ref[...].astype(F32)
+        total = jnp.maximum(total, 1.0)
+        beta = jnp.minimum(1.0, kls_ref[0].astype(F32) / WARM)
+        line = lax.broadcasted_iota(jnp.int32, (8, lat), 0)
+        const_ref[...] = jnp.where(line == 0, total, beta)
+        own = mask_ref[:, pl.ds(pl.multiple_of(home * mine, mine), mine)].astype(F32)
+        line = lax.broadcasted_iota(jnp.int32, (8, mine), 0)
+        both = jnp.where(line == 0, own, jnp.where(line == 1, beta * own / total, 0.0))
+        eye = (
+            lax.broadcasted_iota(jnp.int32, (8, 128), 0)
+            == lax.broadcasted_iota(jnp.int32, (8, 128), 1)
+        ).astype(F32)
+        rowd_ref[...] = fdot(both, eye, TN)
+
+    def out_block(j, part):
+        h = lax.div(j, 2)
+
+        @pl.when(lax.rem(j, 2) == 0)
+        def _():
+            msend[h] = part.astype(BF)
+            mcopy(h).start()
+
+        @pl.when(j == 1)
+        def _():
+            mcopy(0).wait_recv()
+            mgs_ref[...] = (part + mrecv[0].astype(F32)).astype(BF)
+
+        @pl.when(j == 3)
+        def _():
+            mcopy(1).wait_recv()
+            mgk_ref[...] = part + mrecv[1].astype(F32)
+
+    @pl.when((s < 2) | (s >= 6))
+    def _():
+        j = s - 4 * lax.div(s, 6)
+        load(0, j).wait()
+        out_block(j, bdot(og[j], dt[...], TN))
+
+    @pl.when((s >= 2) & (s < 6))
+    def _():
+        j = s - 2
+        h = lax.div(j, 2)
+        load(1, j).wait()
+        low[...] = jnp.log(1.0 + ct[j].astype(F32) * scale_ref[:, cols(j)]).astype(BF)
+        part = bdot(low[...], et[...], TN)
+
+        @pl.when(lax.rem(j, 2) == 0)
+        def _():
+            esend[h] = part.astype(BF)
+            ecopy(h).start()
+
+        @pl.when(j == 1)
+        def _():
+            ecopy(0).wait_recv()
+            ysend[...] = (part + erecv[0].astype(F32)).astype(BF)
+            ycopy().start()
+
+        @pl.when(j == 3)
+        def _():
+            ecopy(1).wait_recv()
+            emb_ref[...] = part + erecv[1].astype(F32)
+
+    @pl.when(s == 7)
+    def _():
+        ycopy().wait_recv()
+        emb_ref[...] = emb_ref[...] + yrecv[...].astype(F32)
+        for h in range(2):
+            mcopy(h).wait_send()
+            ecopy(h).wait_send()
+        ycopy().wait_send()
+        for r in range(nb):
+            scopy(r).wait_send()
+
+
+def front_step(slide_len, kl_step, library, mask, counts_t, og_t, emb_t, dec_t, ncell, lat):
+    width, rows = counts_t.shape
+    model = emb_t.shape[1]
+    mine = rows // 4
+    nb = bits_of(ncell)
+    nslide = slide_len.shape[0]
+    top = -(-nslide // 8) * 8
+    anyv = pl.BlockSpec(memory_space=pl.ANY)
+    smem = pl.BlockSpec(memory_space=pltpu.SMEM)
+    fixed = lambda *shape: pl.BlockSpec(shape, lambda s: (0,) * len(shape))
+    vm = pltpu.VMEM
+    return pl.pallas_call(
+        functools.partial(front_kernel, (ncell, nslide, lat)),
+        grid=(8,),
+        out_shape=[
+            jax.ShapeDtypeStruct((mine, model), F32),
+            jax.ShapeDtypeStruct((mine, model), F32),
+            jax.ShapeDtypeStruct((mine, model), BF),
+            jax.ShapeDtypeStruct((1, rows), F32),
+            jax.ShapeDtypeStruct((8, lat), F32),
+            jax.ShapeDtypeStruct((mine, 128), F32),
+        ],
+        in_specs=[smem, smem, fixed(1, rows), fixed(1, rows), anyv, anyv, anyv, anyv],
+        out_specs=[
+            fixed(mine, model),
+            fixed(mine, model),
+            fixed(mine, model),
+            fixed(1, rows),
+            fixed(8, lat),
+            fixed(mine, 128),
+        ],
+        scratch_shapes=[vm((4, width, mine), BF)] * 2
+        + [vm((width, model), BF)] * 2
+        + [vm((width, mine), BF)]
+        + [vm((2, mine, model), BF)] * 4
+        + [vm((mine, model), BF)] * 2
+        + [
+            vm((2 * nb, 2 * top, 128), F32),
+            vm((2 * top, 128), F32),
+            pltpu.SemaphoreType.DMA((10,)),
+            pltpu.SemaphoreType.DMA((5 + nb,)),
+            pltpu.SemaphoreType.DMA((5 + nb,)),
+        ],
+        compiler_params=pltpu.CompilerParams(
+            collective_id=1, has_side_effects=True, vmem_limit_bytes=67043328
+        ),
+        name="front_step",
+    )(slide_len, kl_step, library, mask, counts_t, og_t, emb_t, dec_t)
+
+
 def main_kernel(cfg, *refs):
     ncell, nch, ch, inplace = cfg
     nb = bits_of(ncell)
@@ -63,13 +303,13 @@
         return [next(take) for _ in range(count)]
 
     og_ref, ct_ref, dw_ref, ew_ref, scale_ref = some(5)
-    emb_hbm, mg_hbm, noise_hbm, latw_hbm, upw_hbm = some(5)
+    emb_hbm, mgk_hbm, mgs_hbm, noise_hbm, latw_hbm, upw_hbm = some(6)
     rowd_ref, const_ref, gain_ref, bias_ref, latb_ref, pmean_ref, plogv_ref = some(7)
     decoded_ref, cgrad_ref, dsum_ref, esum_ref, small_ref, vec_ref = some(6)
     xm, xe, px, keep = some(4)
     recvs = some(nb)
     sends = {k: next(take) for k in range(nb) if k not in inplace}
-    normal, mg, noise, latw, upw, hlow, lmean, lvar, sample, lgrad, resp_s, inv_s, kpart = some(13)
+    normal, mgk, mg, noise, latw, upw, hlow, lmean, lvar, sample, lgrad, resp_s, inv_s, kpart = some(14)
     klbuf, vecbuf, sm_keep, sm_s1, sm_r1, sm_s2, sm_r2 = some(7)
     sm_sc, sm_rc = some(nb), some(nb)
     fin = next(take)
@@ -86,7 +326,7 @@
     home = core * 2 + wye
     peers = [{"cells": xor_of(at, nb, 1 << k)} for k in range(nb)]
     gpeers = [{"genes": xor_of(gene, 2, 1)}, {"genes": xor_of(gene, 2, 2)}]
-    allpeers = gpeers + peers
+    allpeers = peers + gpeers
     nall = nb + 2
     s = pl.program_id(0)
     slots = keep.shape[0]
@@ -130,6 +370,7 @@
         add_side(name + "wye", rowblock(ref, home), rowblock(ref, home), gpeers[1])
         other = core * 2 + (1 - wye)
         add_side(name + "pass", rowblock(ref, other), rowblock(ref, other), gpeers[0])
+    add_side("g", mgs_hbm, rowblock(xe, core * 2 + (1 - wye)), gpeers[1])
     for r in range(nall):
         add_side(f"k{r}", klbuf.at[r], klbuf.at[nall + r], allpeers[r])
         add_side(f"v{r}", vecbuf.at[r], vecbuf.at[nall + r], allpeers[r])
@@ -191,7 +432,13 @@
         return prec, mprec, pmean_ref[...] * mprec + plogv_ref[...]
 
     def loads():
-        pairs = ((emb_hbm, normal), (latw_hbm, latw), (upw_hbm, upw), (mg_hbm, mg), (noise_hbm, noise))
+        pairs = (
+            (emb_hbm, normal),
+            (latw_hbm, latw),
+            (upw_hbm, upw),
+            (rowblock(noise_hbm, home), noise),
+            (mgk_hbm, mgk),
+        )
         return [pltpu.make_async_copy(a, b, lsem.at[i]) for i, (a, b) in enumerate(pairs)]
 
     @pl.when(s == 0)
@@ -221,6 +468,7 @@
         pl.semaphore_wait(barrier, nall)
         start("mwye")
         start("mcore")
+        start("g")
         prec, mprec, ctab = tables()
         lm, lv = lmean[...], lvar[...]
         csum = fdot(jnp.ones((8, lat), F32), ctab, NT)[0:1]
@@ -341,6 +589,9 @@
             fdot(weight, ctab, NT) + fdot(wmom, prec, NT) - 2.0 * fdot(wmean, mprec, NT)
         )
         logit = resp * (rgrad - jnp.sum(resp * rgrad, -1, keepdims=True)) * lat ** (-0.5)
+        got("g")
+        own = xe[pl.ds(pl.multiple_of(home * mine, mine), mine), :].astype(F32)
+        mg[...] = (mgk[...] + own).astype(BF)
         sgrad = bdot(mg[...], upw[...], NN)
         mgrad = (
             sgrad
@@ -410,6 +661,9 @@
         put(2, cut, quarter, mg[...], sample[:, : quarter - cut])
         put(3, 0, quarter, mg[...], sample[:, quarter - cut :])
         start("s1")
+
+    @at_step(back + 2)
+    def _():
         got("ewye")
         start("epass")
 
@@ -419,10 +673,10 @@
         got("epass")
         permute(xe, ncell)
 
-    assert back + 1 < nch - 1
+    assert back + 2 < nch - 1
     for r in range(nall):
 
-        @at_step(back + 2 + r)
+        @at_step(back + 4 + r)
         def _(r=r):
             got(f"v{r}")
             v = vecbuf[r] + vecbuf[nall + r]
@@ -450,7 +704,7 @@
             pl.ds(pl.multiple_of(base + (1 - bit) * size, step), size),
         )
 
-    @at_step(back + 3)
+    @at_step(back + 5)
     def _():
         got("s2")
         sm_keep[wye] = sm_keep[wye] + sm_r2[...].astype(F32)
@@ -459,7 +713,7 @@
 
     for k in reversed(range(nb)):
 
-        @at_step(back + 3 + nb - k)
+        @at_step(back + 5 + 2 * (nb - k) + (0 if k else 2))
         def _(k=k):
             got(f"c{k}")
             kept = span(k)[0]
@@ -471,15 +725,16 @@
                 fin[home] = sm_keep[wye, kept, :].astype(BF)
                 start("f0")
 
-    @at_step(back + 4 + nb)
+    @at_step(back + 8 + 2 * nb)
     def _():
         got("f0")
         start("f1")
 
-    @at_step(back + 5 + nb)
+    @at_step(back + 9 + 2 * nb)
     def _():
         got("f1")
         small_ref[...] = fin[...].astype(F32)
+
 
     for step_no in sorted(plan):
 
@@ -508,7 +763,7 @@
 
 
 def main_step(
-    embedded, mixed_grad, noise, lat_w, up_w, rowd, const, gain, bias, lat_b, pmean_t, plogv_t,
+    embedded, mg_kept, mg_sent, noise, lat_w, up_w, rowd, const, gain, bias, lat_b, pmean_t, plogv_t,
     og_t, counts_t, dec_t, emb_t, scale, ncell
 ):
     width, rows = og_t.shape
@@ -531,7 +786,7 @@
     nk = pmean_t.shape[0]
     vec = 2 * nk + 8
     anyv = pl.BlockSpec(memory_space=pl.ANY)
-    nside = 6 + 2 * nall + 2 + nb + 2
+    nside = 7 + 2 * nall + 2 + nb + 2
     vm = pltpu.VMEM
     return pl.pallas_call(
         functools.partial(main_kernel, (ncell, nch, ch, inplace)),
@@ -555,7 +810,8 @@
             anyv,
             anyv,
             anyv,
-            fixed(mine, 8),
+            anyv,
+            fixed(mine, 128),
             fixed(8, lat),
             fixed(1, model),
             fixed(1, model),
@@ -572,10 +828,11 @@
             fixed(vec, lat),
         ],
         scratch_shapes=[vm((rows, model), BF)] * 3
-        + [vm((lag + 2, ch, model // 2), F32)]
+        + [vm((lag + 1, ch, model // 2), F32)]
         + [vm((n, ch, model >> (k + 1)), BF) for k in range(nb)]
         + [vm((ring, ch, model >> (k + 1)), BF) for k in range(nb) if k not in inplace]
         + [
+            vm((mine, model), F32),
             vm((mine, model), F32),
             vm((mine, model), BF),
             vm((mine, lat), BF),
@@ -611,40 +868,9 @@
         ),
         name="main_step",
     )(
-        og_t, counts_t, dec_t, emb_t, scale, embedded, mixed_grad, noise, lat_w, up_w,
+        og_t, counts_t, dec_t, emb_t, scale, embedded, mg_kept, mg_sent, noise, lat_w, up_w,
         rowd, const, gain, bias, lat_b, pmean_t, plogv_t,
     )
-
-
-def hdot(left, right, dims=((1,), (0,))):
-    return lax.dot_general(left, right, (dims, ((), ())), preferred_element_type=F32)
-
-
-def flip(x, axis, size, mask):
-    return lax.ppermute(x, axis, [(i, i ^ mask) for i in range(size)])
-
-
-def butterfly(x, axis, size):
-    for k in range(bits_of(size)):
-        x = x + flip(x, axis, size, 1 << k)
-    return x
-
-
-def scatter_rows(x, axis, size, at):
-    for k in range(bits_of(size)):
-        bit = (at >> k) & 1
-        halves = x.reshape((2, x.shape[0] // 2) + x.shape[1:])
-        keep = lax.dynamic_index_in_dim(halves, bit, 0, keepdims=False)
-        send = lax.dynamic_index_in_dim(halves, 1 - bit, 0, keepdims=False)
-        x = keep.astype(F32) + flip(send.astype(BF), axis, size, 1 << k).astype(F32)
-    return x
-
-
-def place_of(at, size):
-    block = 0
-    for k in range(bits_of(size)):
-        block = block * 2 + ((at >> k) & 1)
-    return block
 
 
 def on_device(
@@ -671,51 +897,15 @@
     model = emb_weight.shape[0]
     latent_w = up_weight.shape[1]
     cell_at = lax.axis_index("cells")
-    gene_at = lax.axis_index("genes")
-    nslide = slide_len.shape[0]
-    place = cell_at * rows + jnp.arange(rows, dtype=jnp.int32)
-    ends = jnp.cumsum(slide_len)
-    slide_of = jnp.sum((ends[None, :] <= place[:, None]).astype(jnp.int32), 1)
-    onehot = (slide_of[:, None] == jnp.arange(nslide, dtype=jnp.int32)[None, :]).astype(F32)
-    live = cell_mask.astype(F32)
-    libsize = library.astype(F32)
-    stats = jnp.concatenate(
-        [jnp.sum(onehot * (libsize * live)[:, None], 0), jnp.sum(onehot * live[:, None], 0)]
-    )
-    stats = butterfly(stats, "cells", ncell)
-    lib_total, live_total = stats[:nslide], stats[nslide:]
-    slide_lib = lib_total / jnp.maximum(live_total, 1.0)
-    scale = jnp.sum(onehot * slide_lib[None, :], 1) / libsize
-    total = jnp.maximum(jnp.sum(live_total), 1.0)
-    beta = jnp.minimum(1.0, kl_step[0].astype(F32) / WARM)
-
-    partial_mixed = hdot(out_grad, dec_weight, ((1,), (1,))).astype(BF)
-    mixed_grad = scatter_rows(partial_mixed, "genes", ngene, gene_at).astype(BF)
-
-    counts_f = counts.astype(F32)
-    normed = jnp.log(1.0 + counts_f * scale[:, None]).astype(BF)
-    partial_embed = hdot(normed, emb_weight, ((1,), (1,))).astype(BF)
-    embedded = scatter_rows(partial_embed, "genes", ngene, gene_at)
-
-    mine = rows // ngene
-    first = place_of(gene_at, ngene) * mine
-    my_noise = lax.dynamic_slice_in_dim(noise, first, mine, 0)
-    my_live = lax.dynamic_slice_in_dim(live, first, mine, 0)
-    rowd = jnp.concatenate(
-        [my_live[:, None], (beta * my_live / total)[:, None], jnp.zeros((mine, 6), F32)], 1
-    )
-    const = jnp.concatenate(
-        [
-            jnp.full((1, latent_w), 1.0) * total,
-            jnp.full((1, latent_w), 1.0) * beta,
-            jnp.zeros((6, latent_w), F32),
-        ],
-        0,
+    og_t, counts_t, dec_t, emb_t = out_grad.T, counts.T, dec_weight.T, emb_weight.T
+    embedded, mg_kept, mg_sent, scale, const, rowd = front_step(
+        slide_len, kl_step, library[None, :], cell_mask[None, :], counts_t, og_t, emb_t, dec_t,
+        ncell, latent_w,
     )
     decoded, counts_grad, dec_out, emb_out, small, vec = main_step(
-        embedded, mixed_grad, my_noise, lat_weight, up_weight, rowd, const,
+        embedded, mg_kept, mg_sent, noise, lat_weight, up_weight, rowd, const,
         ln_gain[None, :], ln_bias[None, :], lat_bias[None, :], prior_mean.T, prior_logvar.T,
-        out_grad.T, counts.T, dec_weight.T, emb_weight.T, scale[None, :], ncell,
+        og_t, counts_t, dec_t, emb_t, scale, ncell,
     )
     decoded, counts_grad, dec_out, emb_out = decoded.T, counts_grad.T, dec_out.T, emb_out.T
     step = model // ncell

time: 306 us -> 253 us (0.83)
  waiting for transfers between devices: 21.5 us -> 0 us
  matrix products: 20.4 us -> 0 us
  Pallas kernels: 210 us -> 228 us
  other arithmetic: 10.6 us -> 0.01 us
  starting transfers between devices: 9.3 us -> 0 us
  local copies, waits for them, and re-layouts: 30.4 us -> 21.3 us
    pallas_call x0 -> x1, Pallas kernels: none -> 35.5 us  [front_step(): pl.pallas_call(functools.partial(front_kernel, (ncell, nslide, lat)), gri...]
    ppermute x7 -> x0, waiting for transfers between devices: 21.5 us -> none  [flip(): return lax.ppermute(x, axis, [(i, i ^ mask) for i in range(size)])]
    dot_general x2 -> x0, matrix products: 20.4 us -> none  [hdot(): lax.dot_general(left, right, (dims, ((), ())), preferred_element_type=F32)]
    pallas_call x1, Pallas kernels: 210 us -> 192 us  [main_step(): pl.pallas_call(functools.partial(main_kernel, (ncell, nch, ch, inplace)),...]
    ppermute x7 -> x0, starting transfers between devices: 9.3 us -> none  [flip(): return lax.ppermute(x, axis, [(i, i ^ mask) for i in range(size)])]
    add x7 -> x0, other arithmetic: 6.17 us -> none  [the longest x3 6.08 us: scatter_rows(): x = keep.astype(F32) + flip(send.astype(BF), axis, size, 1 << k).astype(F32)]
    unnamed x32 -> x18, local copies, waits for them, and re-layouts: 19.4 us -> 15.4 us
  transfers between devices with their start and end apart: 7 -> 0, of which waited for: 4 -> 0; matrix products, arithmetic and copies ran while one was open for 10% -> 0% of each run, Pallas kernels for 0% -> 0%
where the time goes in v5:
time: 253 us; the launch traced here: 252 us
  Pallas kernels  228 us (90%)
  local copies, waits for them, and re-layouts  21.3 us (8%)
  between operations  3.14 us (1%)
    pallas_call x1, Pallas kernels, main_step(): pl.pallas_call(functools.partial(main_kernel, (ncell, nch, ch, inplace)),...  192 us
    pallas_call x1, Pallas kernels, front_step(): pl.pallas_call(functools.partial(front_kernel, (ncell, nslide, lat)), gri...  35.5 us
    unnamed x18, local copies, waits for them, and re-layouts  15.4 us

profile of v5, /device:TPU:0, one launch (start us, length us, event | category | flops | bytes accessed | tf_op | source)
XLA Modules:
  0.0 252.1 jit_solution(17316821525279867842)
XLA Ops:
  1.3 35.5 %front_step.1 = (f32[256,1024]{1,0:T(8,128)}, f32[256,1024]{1,0:T(8,128)}, bf16[256,1024]{1,0:T(8,128)(2,1)}, f32[1,1024]{1,0:T(1,128)}, f32[8,512]{1,0:T(8,128)}, /*index=5*/f32[256,128]{1,0:T(8,128)}) custom-call(s32[3]{0:T(128)} %refs_0_.1, s32[1]{0:T(128)S(6)} %copy.38.refs_1_, s32[1,1024]{1,0:T(1,128)} %bitcast.50, s32[1,1024]{1,0:T(1,128)} %bitcast.51, ...), custom_call_target="tpu_custom_call" | custom-call | tf_op jit(solution)/shard_map/front_step/pallas_call | solution.py:258
  36.8 192.2 %main_step.1 = (bf16[3375,1024]{1,0:T(8,128)(2,1)}, bf16[3375,1024]{1,0:T(8,128)(2,1)}, f32[3375,128]{1,0:T(8,128)}, f32[3375,128]{1,0:T(8,128)}, f32[4,128,384]{2,1,0:T(8,128)}, /*index=5*/f32[40,512]{1,0:T(8,128)}) custom-call(bf16[3375,1024]{1,0:T(8,128)(2,1)} %bitcast.32, bf16[3375,1024]{1,0:T(8,128)(2,1)} %bitcast.34, bf16[3375,1024]{1,0:T(8,128)(2,1)} %bitcast.36, ...), custom_call_target="tpu_custom_call" | custom-call | tf_op jit(solution)/shard_map/main_step/pallas_call | solution.py:791
  229.0 0.8 fusion
  229.8 0.7 dynamic-slice_bitcast_fusion
  230.5 0.8 slice_bitcast_fusion
  231.3 0.6 dynamic_slice.15
  231.9 0.6 dynamic_slice.16
  232.5 0.6 dynamic_slice.17
  233.1 1.2 slice.31
  234.9 1.4 copy.28
  236.4 1.0 copy.29
  237.4 0.0 slice-start
  237.4 0.8 copy.30
  238.2 0.0 slice-start.1
  238.2 6.8 %copy.39 = bf16[1024,3375]{0,1:T(8,128)(2,1)} copy(bf16[1024,3375]{0,1:T(8,128)(2,1)} %bitcast.42) | data formatting | bytes 13824000
  245.1 0.0 slice-done
  245.1 0.0 slice-done.1
  245.1 0.0 copy-start.1
  245.1 0.0 copy-start
  245.1 3.5 %copy.40 = bf16[1024,3375]{0,1:T(8,128)(2,1)} copy(bf16[1024,3375]{0,1:T(8,128)(2,1)S(1)} %bitcast.41) | data formatting | bytes 13824000
  248.6 0.0 copy-done.1
  248.6 1.2 copy.41
  249.8 0.0 copy-done
  249.8 1.2 copy.42
  (6 shorter events, 0.1 us)
Async XLA Ops:
  237.4 7.7 %slice-start = ((s8[6914048]{0:T(1024)(128)(4,1)}), s8[2719744]{0:T(1024)(128)(4,1)S(1)}, s32[]{:S(2)}) async-start(s8[6914048]{0:T(1024)(128)(4,1)} %bitcast.39), calls=%async_computation | async-start | bytes 5439488
  238.2 6.8 %slice-start.1 = ((s8[6914048]{0:T(1024)(128)(4,1)}), s8[4194304]{0:T(1024)(128)(4,1)S(1)}, s32[]{:S(2)}) async-start(s8[6914048]{0:T(1024)(128)(4,1)} %bitcast.39), calls=%async_computation.1 | async-start | bytes 8388608
  245.1 3.5 %copy-start.1 = (f32[3375,128]{1,0:T(8,128)S(1)}, f32[3375,128]{1,0:T(8,128)}, u32[]{:S(2)}) copy-start(f32[3375,128]{1,0:T(8,128)} %get-tuple-element.32) | copy-start | bytes 5184004
  245.1 4.7 %copy-start = (f32[3375,128]{1,0:T(8,128)S(1)}, f32[3375,128]{1,0:T(8,128)}, u32[]{:S(2)}) copy-start(f32[3375,128]{1,0:T(8,128)} %get-tuple-element.35) | copy-start | bytes 5184004

commit v6 on v5

--- a/solution.py
+++ b/solution.py
@@ -80,9 +80,14 @@
     def cols(j):
         return pl.ds(pl.multiple_of(block_of(j) * mine, mine), mine)
 
-    def load(which, j):
+    def load(which, h, f):
         src, dst = ((og_hbm, og), (ct_hbm, ct))[which]
-        return pltpu.make_async_copy(src.at[:, cols(j)], dst.at[j], lsem.at[2 + 4 * which + j])
+        j = 2 * h + f
+        return pltpu.make_async_copy(
+            src.at[:, cols(j)],
+            dst.at[h, :, pl.ds(f * mine, mine)],
+            lsem.at[2 + 4 * which + j],
+        )
 
     def whole(which):
         src, dst = ((dt_hbm, dt), (et_hbm, et))[which]
@@ -133,13 +138,11 @@
         for p in peers + gpeers:
             pl.semaphore_signal(barrier, inc=1, device_id=p, device_id_type=MESH)
         whole(0).start()
-        load(0, 0).start()
-        load(0, 1).start()
-        whole(1).start()
-        for j in range(4):
-            load(1, j).start()
-        load(0, 2).start()
-        load(0, 3).start()
+        for which, h in ((0, 0), (1, 0), (1, 1), (0, 1)):
+            for f in range(2):
+                load(which, h, f).start()
+            if (which, h) == (0, 0):
+                whole(1).start()
         stb[0] = jnp.zeros_like(stv)
         live = mask_ref[...].astype(F32)
         libsize = lib_ref[...].astype(F32)
@@ -153,12 +156,9 @@
         pl.semaphore_wait(barrier, nb + 2)
         scopy(0).start()
         whole(0).wait()
+        round_done(0)
 
     @pl.when(s == 1)
-    def _():
-        round_done(0)
-
-    @pl.when(s == 2)
     def _():
         for r in range(1, nb):
             round_done(r)
@@ -184,55 +184,46 @@
         ).astype(F32)
         rowd_ref[...] = fdot(both, eye, TN)
 
-    def out_block(j, part):
-        h = lax.div(j, 2)
-
-        @pl.when(lax.rem(j, 2) == 0)
-        def _():
-            msend[h] = part.astype(BF)
-            mcopy(h).start()
-
-        @pl.when(j == 1)
-        def _():
-            mcopy(0).wait_recv()
-            mgs_ref[...] = (part + mrecv[0].astype(F32)).astype(BF)
-
-        @pl.when(j == 3)
-        def _():
-            mcopy(1).wait_recv()
-            mgk_ref[...] = part + mrecv[1].astype(F32)
-
-    @pl.when((s < 2) | (s >= 6))
-    def _():
-        j = s - 4 * lax.div(s, 6)
-        load(0, j).wait()
-        out_block(j, bdot(og[j], dt[...], TN))
-
-    @pl.when((s >= 2) & (s < 6))
-    def _():
-        j = s - 2
-        h = lax.div(j, 2)
-        load(1, j).wait()
-        low[...] = jnp.log(1.0 + ct[j].astype(F32) * scale_ref[:, cols(j)]).astype(BF)
-        part = bdot(low[...], et[...], TN)
-
-        @pl.when(lax.rem(j, 2) == 0)
-        def _():
-            esend[h] = part.astype(BF)
-            ecopy(h).start()
-
-        @pl.when(j == 1)
-        def _():
-            ecopy(0).wait_recv()
-            ysend[...] = (part + erecv[0].astype(F32)).astype(BF)
-            ycopy().start()
-
-        @pl.when(j == 3)
-        def _():
-            ecopy(1).wait_recv()
-            emb_ref[...] = part + erecv[1].astype(F32)
-
-    @pl.when(s == 7)
+    def pair(h, left, right, kept, send, copy):
+        part = bdot(left, right, TN)
+        send[h] = part[:mine].astype(BF)
+        copy(h).start()
+        kept[...] = part[mine:]
+
+    @pl.when((s == 0) | (s == 3))
+    def _():
+        h = lax.div(s, 3)
+        for f in range(2):
+            load(0, h, f).wait()
+        pair(h, og[h], dt[...], mgk_ref, msend, mcopy)
+
+    @pl.when((s == 1) | (s == 2))
+    def _():
+        h = s - 1
+        for f in range(2):
+            load(1, h, f).wait()
+            z = 1.0 + ct[h, :, f * mine : (f + 1) * mine].astype(F32) * scale_ref[
+                :, cols(2 * h + f)
+            ]
+            low[:, f * mine : (f + 1) * mine] = jnp.log(z).astype(BF)
+        pair(h, low[...], et[...], emb_ref, esend, ecopy)
+
+    @pl.when(s == 1)
+    def _():
+        ecopy(0).wait_recv()
+        ysend[...] = (emb_ref[...] + erecv[0].astype(F32)).astype(BF)
+        ycopy().start()
+        mcopy(0).wait_recv()
+        mgs_ref[...] = (mgk_ref[...] + mrecv[0].astype(F32)).astype(BF)
+
+    @pl.when(s == 3)
+    def _():
+        ecopy(1).wait_recv()
+        emb_ref[...] = emb_ref[...] + erecv[1].astype(F32)
+        mcopy(1).wait_recv()
+        mgk_ref[...] = mgk_ref[...] + mrecv[1].astype(F32)
+
+    @pl.when(s == 3)
     def _():
         ycopy().wait_recv()
         emb_ref[...] = emb_ref[...] + yrecv[...].astype(F32)
@@ -257,7 +248,7 @@
     vm = pltpu.VMEM
     return pl.pallas_call(
         functools.partial(front_kernel, (ncell, nslide, lat)),
-        grid=(8,),
+        grid=(4,),
         out_shape=[
             jax.ShapeDtypeStruct((mine, model), F32),
             jax.ShapeDtypeStruct((mine, model), F32),
@@ -275,9 +266,9 @@
             fixed(8, lat),
             fixed(mine, 128),
         ],
-        scratch_shapes=[vm((4, width, mine), BF)] * 2
+        scratch_shapes=[vm((2, width, 2 * mine), BF)] * 2
         + [vm((width, model), BF)] * 2
-        + [vm((width, mine), BF)]
+        + [vm((width, 2 * mine), BF)]
         + [vm((2, mine, model), BF)] * 4
         + [vm((mine, model), BF)] * 2
         + [
@@ -772,7 +763,7 @@
     nb = bits_of(ncell)
     nall = nb + 2
     step = model // ncell
-    ch = 384 if step % 128 == 0 else 192
+    ch = 376 if step % 128 == 0 else 192
     nch = -(-width // ch)
     inplace = tuple(k for k in range(1, nb) if (model >> (k + 1)) % 128 == 0)
     n = 2 * nch
@@ -873,6 +864,85 @@
     )
 
 
+def last_kernel(cfg, *refs):
+    ncell, ngene, nk = cfg
+    big_in, (small, vec) = refs[:4], refs[4:6]
+    big_out = refs[6:10]
+    gain, shift, latw, latb, up, pmean, plogv, loss = refs[10:18]
+    held, sem = refs[18:22], refs[22]
+    part = 256
+    pieces = []
+    for src, dst, mid in zip(big_in, big_out, held):
+        for c in range(0, src.shape[1], part):
+            cut = pl.ds(c, min(part, src.shape[1] - c))
+            i = len(pieces)
+            pieces.append(
+                (
+                    pltpu.make_async_copy(src.at[:, cut], mid.at[:, cut], sem.at[0, i]),
+                    pltpu.make_async_copy(mid.at[:, cut], dst.at[:, cut], sem.at[1, i]),
+                )
+            )
+    for come, _ in pieces:
+        come.start()
+
+    def small_outputs():
+        at = lax.axis_index("cells")
+        lat = vec.shape[1]
+        step, each = gain.shape[1], pmean.shape[1]
+        quarter = small.shape[2]
+        cut = 2 * lat - 2 * quarter
+        latw[:, :quarter] = small[0]
+        latw[:, quarter : 2 * quarter] = small[1]
+        latw[:, 2 * quarter :] = small[2, :, :cut]
+        up[:, : quarter - cut] = small[2, :, cut:]
+        up[:, quarter - cut :] = small[3]
+
+        def own(rows, size, base):
+            col = lax.broadcasted_iota(jnp.int32, (lat, size), 0) + base
+            mine = lax.broadcasted_iota(jnp.int32, (lat, size), 1) + at * size
+            return fdot(rows, (col == mine).astype(F32), NN)
+
+        pmean[...] = own(vec[:nk], each, 0)
+        plogv[...] = own(vec[nk : 2 * nk], each, 0)
+        tail = vec[2 * nk : 2 * nk + 8]
+        first, second = own(tail, step, 0), own(tail, step, lat)
+        for j, ref in enumerate((gain, shift, latb)):
+            ref[...] = first[1 + 2 * j : 2 + 2 * j] + second[2 + 2 * j : 3 + 2 * j]
+        loss[...] = tail[0:1, 0:1] * (1.0 / (ncell * ngene))
+
+    for i, (come, go) in enumerate(pieces):
+        come.wait()
+        go.start()
+        if i == 0:
+            small_outputs()
+    for _, go in pieces:
+        go.wait()
+
+
+def last_step(decoded, cgrad, dsum, esum, small, vec, nk, ncell, ngene):
+    width, rows = decoded.shape
+    step = dsum.shape[1]
+    lat = vec.shape[1]
+    model = step * ncell
+    each = lat // ncell
+    fixed = lambda shape: pl.BlockSpec(shape, lambda: (0,) * len(shape))
+    big = [pl.BlockSpec(memory_space=pl.ANY)] * 4
+    wide = sum(-(-n // 256) for n in (rows, rows, step, step))
+    shapes = [(1, step), (1, step), (step, 2 * lat), (1, step), (step, lat)]
+    shapes += [(nk, each), (nk, each), (1, 1)]
+    return pl.pallas_call(
+        functools.partial(last_kernel, (ncell, ngene, nk)),
+        out_shape=[jax.ShapeDtypeStruct(x.shape, x.dtype) for x in (decoded, cgrad, dsum, esum)]
+        + [jax.ShapeDtypeStruct(shape, F32) for shape in shapes],
+        in_specs=big + [fixed(small.shape), fixed(vec.shape)],
+        out_specs=big + [fixed(shape) for shape in shapes],
+        scratch_shapes=[pltpu.VMEM(x.shape, x.dtype) for x in (decoded, cgrad, dsum, esum)]
+        + [pltpu.SemaphoreType.DMA((2, wide))],
+        compiler_params=pltpu.CompilerParams(vmem_limit_bytes=67043328),
+        name="last_step",
+    )(decoded, cgrad, dsum, esum, small, vec)
+
+
 def on_device(
     counts,
     library,
@@ -896,7 +966,6 @@
     rows, width = counts.shape
     model = emb_weight.shape[0]
     latent_w = up_weight.shape[1]
-    cell_at = lax.axis_index("cells")
     og_t, counts_t, dec_t, emb_t = out_grad.T, counts.T, dec_weight.T, emb_weight.T
     embedded, mg_kept, mg_sent, scale, const, rowd = front_step(
         slide_len, kl_step, library[None, :], cell_mask[None, :], counts_t, og_t, emb_t, dec_t,
@@ -907,36 +976,22 @@
         ln_gain[None, :], ln_bias[None, :], lat_bias[None, :], prior_mean.T, prior_logvar.T,
         og_t, counts_t, dec_t, emb_t, scale, ncell,
     )
-    decoded, counts_grad, dec_out, emb_out = decoded.T, counts_grad.T, dec_out.T, emb_out.T
-    step = model // ncell
-    small = small.transpose(1, 0, 2).reshape(step, 3 * latent_w)
-    latw_out = small[:, : 2 * latent_w]
-    up_out = small[:, 2 * latent_w :]
-    nk = prior_mean.shape[1]
-
-    def own(x, each, axis):
-        return lax.dynamic_slice_in_dim(x, cell_at * each, each, axis)
-
-    pmean_out = own(vec[:nk], latent_w // ncell, 1).T
-    plogv_out = own(vec[nk : 2 * nk], latent_w // ncell, 1).T
-    base = 2 * nk
-    kl_loss = vec[base, :1] / (ncell * ngene)
-    gain_out, shift_out, latb_out = [
-        own(vec[base + 1 + 2 * j : base + 3 + 2 * j].reshape(model), step, 0) for j in range(3)
-    ]
+    decoded, counts_grad, dec_out, emb_out, gain, shift, latw, latb, up, pmean, plogv, loss = last_step(
+        decoded, counts_grad, dec_out, emb_out, small, vec, prior_mean.shape[1], ncell, ngene
+    )
     return (
-        decoded,
-        counts_grad,
-        emb_out,
-        gain_out,
-        shift_out,
-        latw_out,
-        latb_out,
-        up_out,
-        dec_out,
-        pmean_out,
-        plogv_out,
-        kl_loss,
+        decoded.T,
+        counts_grad.T,
+        emb_out.T,
+        gain[0],
+        shift[0],
+        latw,
+        latb[0],
+        up,
+        dec_out.T,
+        pmean.T,
+        plogv.T,
+        loss[0],
     )
 
 

time: 253 us -> 243 us (0.960)
  local copies, waits for them, and re-layouts: 21.3 us -> 0 us
  Pallas kernels: 228 us -> 242 us
    unnamed x18 -> x0, local copies, waits for them, and re-layouts: 15.4 us -> none
    pallas_call x0 -> x1, Pallas kernels: none -> 14.5 us  [last_step(): pl.pallas_call(functools.partial(last_kernel, (ncell, ngene, nk)), out_sh...]
where the time goes in v6:
time: 243 us
  Pallas kernels  242 us (100%)
    pallas_call x1, Pallas kernels, main_step(): pl.pallas_call(functools.partial(main_kernel, (ncell, nch, ch, inplace)),...  192 us
    pallas_call x1, Pallas kernels, front_step(): pl.pallas_call(functools.partial(front_kernel, (ncell, nslide, lat)), gri...  35.4 us
    pallas_call x1, Pallas kernels, last_step(): pl.pallas_call(functools.partial(last_kernel, (ncell, ngene, nk)), out_sh...  14.5 us

profile of v6, /device:TPU:0, one launch (start us, length us, event | category | flops | bytes accessed | tf_op | source)
XLA Modules:
  0.0 243.2 jit_solution(4334767411435080286)
XLA Ops:
  1.3 35.4 %front_step.1 = (f32[256,1024]{1,0:T(8,128)}, f32[256,1024]{1,0:T(8,128)}, bf16[256,1024]{1,0:T(8,128)(2,1)}, f32[1,1024]{1,0:T(1,128)}, f32[8,512]{1,0:T(8,128)}, /*index=5*/f32[256,128]{1,0:T(8,128)}) custom-call(s32[3]{0:T(128)} %refs_0_.1, s32[1]{0:T(128)S(6)} %copy.28.refs_1_, s32[1,1024]{1,0:T(1,128)} %bitcast.31, s32[1,1024]{1,0:T(1,128)} %bitcast.32, ...), custom_call_target="tpu_custom_call" | custom-call | tf_op jit(solution)/shard_map/front_step/pallas_call | solution.py:249
  36.7 191.9 %main_step.1 = (bf16[3375,1024]{1,0:T(8,128)(2,1)}, bf16[3375,1024]{1,0:T(8,128)(2,1)}, f32[3375,128]{1,0:T(8,128)}, f32[3375,128]{1,0:T(8,128)}, f32[4,128,384]{2,1,0:T(8,128)}, /*index=5*/f32[40,512]{1,0:T(8,128)}) custom-call(bf16[3375,1024]{1,0:T(8,128)(2,1)} %bitcast.22, bf16[3375,1024]{1,0:T(8,128)(2,1)} %bitcast.24, bf16[3375,1024]{1,0:T(8,128)(2,1)} %bitcast.26, ...), custom_call_target="tpu_custom_call" | custom-call | tf_op jit(solution)/shard_map/main_step/pallas_call | solution.py:782
  228.6 14.5 %last_step.1 = (bf16[3375,1024]{1,0:T(8,128)(2,1)}, bf16[3375,1024]{1,0:T(8,128)(2,1)}, f32[3375,128]{1,0:T(8,128)}, f32[3375,128]{1,0:T(8,128)}, f32[1,128]{1,0...) custom-call(bf16[3375,1024]{1,0:T(8,128)(2,1)} %get-tuple-element.42, ...), custom_call_target="tpu_custom_call" | custom-call | tf_op jit(solution)/shard_map/last_step/pallas_call | solution.py:933

commit v7 on v6

--- a/solution.py
+++ b/solution.py
@@ -103,17 +103,21 @@
             device_id_type=MESH,
         )
 
+    half = dt.shape[1] // 2
+
     def mcopy(h):
         return remote(msend.at[h], mrecv.at[h], h, gpeers[0])
 
-    def ecopy(h):
-        return remote(esend.at[h], erecv.at[h], 2 + h, gpeers[0])
-
-    def ycopy():
-        return remote(ysend, yrecv, 4, gpeers[1])
+    def ecopy(h, c):
+        cut = pl.ds(c * half, half)
+        return remote(esend.at[h, :, cut], erecv.at[h, :, cut], 2 + 2 * h + c, gpeers[0])
+
+    def ycopy(c):
+        cut = pl.ds(c * half, half)
+        return remote(ysend.at[:, cut], yrecv.at[:, cut], 6 + c, gpeers[1])
 
     def scopy(r):
-        return remote(stb.at[r], stb.at[nb + r], 5 + r, peers[r])
+        return remote(stb.at[r], stb.at[nb + r], 8 + r, peers[r])
 
     def slides():
         place = at * rows + lax.broadcasted_iota(jnp.int32, (1, rows), 1)
@@ -160,7 +164,7 @@
 
     @pl.when(s == 1)
     def _():
-        for r in range(1, nb):
+        for r in range(3, nb):
             round_done(r)
         whole(1).wait()
         live = mask_ref[...].astype(F32)
@@ -184,18 +188,30 @@
         ).astype(F32)
         rowd_ref[...] = fdot(both, eye, TN)
 
-    def pair(h, left, right, kept, send, copy):
-        part = bdot(left, right, TN)
-        send[h] = part[:mine].astype(BF)
-        copy(h).start()
-        kept[...] = part[mine:]
-
     @pl.when((s == 0) | (s == 3))
     def _():
         h = lax.div(s, 3)
         for f in range(2):
             load(0, h, f).wait()
-        pair(h, og[h], dt[...], mgk_ref, msend, mcopy)
+        for f in range(2):
+            part = bdot(og[h, :, f * mine : (f + 1) * mine], dt[...], TN)
+            if f == 0:
+                msend[h] = part.astype(BF)
+                mcopy(h).start()
+            else:
+                mgk_ref[...] = part
+            if f + 1 < nb:
+
+                @pl.when(s == 0)
+                def _(f=f):
+                    round_done(f + 1)
+
+
+    def forward(c):
+        cut = slice(c * half, (c + 1) * half)
+        ecopy(0, c).wait_recv()
+        ysend[:, cut] = (emb_ref[:, cut] + erecv[0, :, cut].astype(F32)).astype(BF)
+        ycopy(c).start()
 
     @pl.when((s == 1) | (s == 2))
     def _():
@@ -206,31 +222,41 @@
                 :, cols(2 * h + f)
             ]
             low[:, f * mine : (f + 1) * mine] = jnp.log(z).astype(BF)
-        pair(h, low[...], et[...], emb_ref, esend, ecopy)
+        for c in range(2):
+            cut = slice(c * half, (c + 1) * half)
+            part = bdot(low[...], et[:, cut], TN)
+            esend[h, :, cut] = part[:mine].astype(BF)
+            ecopy(h, c).start()
+            emb_ref[:, cut] = part[mine:]
+
+            @pl.when((s == 1) & (c == 1))
+            def _():
+                forward(0)
 
     @pl.when(s == 1)
     def _():
-        ecopy(0).wait_recv()
-        ysend[...] = (emb_ref[...] + erecv[0].astype(F32)).astype(BF)
-        ycopy().start()
+        forward(1)
         mcopy(0).wait_recv()
         mgs_ref[...] = (mgk_ref[...] + mrecv[0].astype(F32)).astype(BF)
 
     @pl.when(s == 3)
     def _():
-        ecopy(1).wait_recv()
+        for c in range(2):
+            ecopy(1, c).wait_recv()
         emb_ref[...] = emb_ref[...] + erecv[1].astype(F32)
         mcopy(1).wait_recv()
         mgk_ref[...] = mgk_ref[...] + mrecv[1].astype(F32)
 
     @pl.when(s == 3)
     def _():
-        ycopy().wait_recv()
+        for c in range(2):
+            ycopy(c).wait_recv()
         emb_ref[...] = emb_ref[...] + yrecv[...].astype(F32)
         for h in range(2):
             mcopy(h).wait_send()
-            ecopy(h).wait_send()
-        ycopy().wait_send()
+            ycopy(h).wait_send()
+            for c in range(2):
+                ecopy(h, c).wait_send()
         for r in range(nb):
             scopy(r).wait_send()
 
@@ -275,8 +301,8 @@
             vm((2 * nb, 2 * top, 128), F32),
             vm((2 * top, 128), F32),
             pltpu.SemaphoreType.DMA((10,)),
-            pltpu.SemaphoreType.DMA((5 + nb,)),
-            pltpu.SemaphoreType.DMA((5 + nb,)),
+            pltpu.SemaphoreType.DMA((8 + nb,)),
+            pltpu.SemaphoreType.DMA((8 + nb,)),
         ],
         compiler_params=pltpu.CompilerParams(
             collective_id=1, has_side_effects=True, vmem_limit_bytes=67043328
@@ -439,8 +465,8 @@
         barrier = pltpu.get_barrier_semaphore()
         for p in allpeers:
             pl.semaphore_signal(barrier, inc=1, device_id=p, device_id_type=MESH)
-        for cp in loads():
-            cp.wait()
+        first, latw_in, upw_in, noise_in, mgk_in = loads()
+        first.wait()
         e = normal[...]
         centred = e - jnp.mean(e, -1, keepdims=True)
         inv = lax.rsqrt(jnp.mean(centred * centred, -1, keepdims=True) + EPS)
@@ -449,10 +475,13 @@
         inv_s[...] = inv
         hidden = nrm * gain_ref[...] + bias_ref[...]
         hlow[...] = hidden.astype(BF)
+        latw_in.wait()
         latent = bdot(hlow[...], latw[...], NN) + latb_ref[...]
         lm, lv = latent[:, :lat], latent[:, lat:]
         lmean[...] = lm
         lvar[...] = lv
+        noise_in.wait()
+        upw_in.wait()
         sample[...] = (lm + jnp.exp(0.5 * lv) * noise[...].astype(F32)).astype(BF)
         mixed = normal[...] * gain_ref[...] + bias_ref[...] + bdot(sample[...], upw[...], NT)
         xm[pl.ds(pl.multiple_of(home * mine, mine), mine), :] = mixed.astype(BF)
@@ -460,6 +489,7 @@
         start("mwye")
         start("mcore")
         start("g")
+        mgk_in.wait()
         prec, mprec, ctab = tables()
         lm, lv = lmean[...], lvar[...]
         csum = fdot(jnp.ones((8, lat), F32), ctab, NT)[0:1]

time: 243 us -> 239 us (0.984)
  Pallas kernels: 242 us -> 237 us
    pallas_call x1, Pallas kernels: 192 us -> 189 us  [main_step(): pl.pallas_call(functools.partial(main_kernel, (ncell, nch, ch, inplace)),...]
where the time goes in v7:
time: 239 us; the launch traced here: 238 us
  Pallas kernels  237 us (99%)
    pallas_call x1, Pallas kernels, main_step(): pl.pallas_call(functools.partial(main_kernel, (ncell, nch, ch, inplace)),...  189 us
    pallas_call x1, Pallas kernels, front_step(): pl.pallas_call(functools.partial(front_kernel, (ncell, nslide, lat)), gri...  33.5 us
    pallas_call x1, Pallas kernels, last_step(): pl.pallas_call(functools.partial(last_kernel, (ncell, ngene, nk)), out_sh...  14.5 us

profile of v7, /device:TPU:0, one launch (start us, length us, event | category | flops | bytes accessed | tf_op | source)
XLA Modules:
  0.0 238.3 jit_solution(15853783785851513916)
XLA Ops:
  1.3 33.5 %front_step.1 = (f32[256,1024]{1,0:T(8,128)}, f32[256,1024]{1,0:T(8,128)}, bf16[256,1024]{1,0:T(8,128)(2,1)}, f32[1,1024]{1,0:T(1,128)}, f32[8,512]{1,0:T(8,128)}, /*index=5*/f32[256,128]{1,0:T(8,128)}) custom-call(s32[3]{0:T(128)} %refs_0_.1, s32[1]{0:T(128)S(6)} %copy.28.refs_1_, s32[1,1024]{1,0:T(1,128)} %bitcast.31, s32[1,1024]{1,0:T(1,128)} %bitcast.32, ...), custom_call_target="tpu_custom_call" | custom-call | tf_op jit(solution)/shard_map/front_step/pallas_call | solution.py:275
  34.8 188.8 %main_step.1 = (bf16[3375,1024]{1,0:T(8,128)(2,1)}, bf16[3375,1024]{1,0:T(8,128)(2,1)}, f32[3375,128]{1,0:T(8,128)}, f32[3375,128]{1,0:T(8,128)}, f32[4,128,384]{2,1,0:T(8,128)}, /*index=5*/f32[40,512]{1,0:T(8,128)}) custom-call(bf16[3375,1024]{1,0:T(8,128)(2,1)} %bitcast.22, bf16[3375,1024]{1,0:T(8,128)(2,1)} %bitcast.24, bf16[3375,1024]{1,0:T(8,128)(2,1)} %bitcast.26, ...), custom_call_target="tpu_custom_call" | custom-call | tf_op jit(solution)/shard_map/main_step/pallas_call | solution.py:812
  223.6 14.5 %last_step.1 = (bf16[3375,1024]{1,0:T(8,128)(2,1)}, bf16[3375,1024]{1,0:T(8,128)(2,1)}, f32[3375,128]{1,0:T(8,128)}, f32[3375,128]{1,0:T(8,128)}, f32[1,128]{1,0...) custom-call(bf16[3375,1024]{1,0:T(8,128)(2,1)} %get-tuple-element.42, ...), custom_call_target="tpu_custom_call" | custom-call | tf_op jit(solution)/shard_map/last_step/pallas_call | solution.py:963
